TPU v7x, 256 devices: a whole 4x4x8 slice. The times are simulated.
256 devices in a mesh: dom: 64 (over x, z, core), slab: 4 (over y).
Axes of the slice: x: 4, y: 4, z: 8, core: 2. Of those that a mesh axis runs over, the one named last changes fastest.
Arguments:
- logperm: float32 [256, 16, 64, 128], P('dom', 'slab'), may hold values from -4.2 to 4.2
- source: float32 [16, 64, 128], P('slab'), may hold values from -6 to 6
- observed: float32 [16, 64, 128], P('slab'), may hold values from -1.2 to 1.2
- brownian: float32 [256, 256], replicated, may hold values from -6 to 6
Outputs:
- particles_next: float32 [256, 16, 64, 128], P('dom', 'slab')
All inputs are finite; a program needn't handle non-finite values.
Results may differ from a plain program's by a relative error of at most 0.0003.
Values sent between devices are 32-bit elements; how exact they have to be, the bound alone decides.
No kernel may reach another device: no remote copies, remote signals or barrier semaphores. Data moves between devices by JAX's collectives and lax.ppermute only.
A program may use at most 64 MiB of HBM per device.

v0:
```python
import math

import jax
import jax.numpy as jnp
from jax import lax
from jax.sharding import PartitionSpec as P

SWEEPS = 8


misfit_weight = 1000.0


def with_halo(block, sides, width):
    for axis, dim in sides:
        count = lax.axis_size(axis)
        forward = [(i, i + 1) for i in range(count - 1)]
        backward = [(target, source) for source, target in forward]
        low = lax.ppermute(
            lax.slice_in_dim(block, block.shape[dim] - width, None, axis=dim), axis, forward
        )
        high = lax.ppermute(lax.slice_in_dim(block, 0, width, axis=dim), axis, backward)
        block = jnp.concatenate([low, block, high], axis=dim)
    return block


def neighbor_sum(core, below, above, fill):
    pad_y = jnp.pad(core, ((0, 0), (0, 0), (1, 1), (0, 0)), constant_values=fill)
    pad_z = jnp.pad(core, ((0, 0), (0, 0), (0, 0), (1, 1)), constant_values=fill)
    return below + above + pad_y[:, :, :-2] + pad_y[:, :, 2:] + pad_z[..., :-2] + pad_z[..., 2:]


def grad_field(e_core, e_below, e_above, p_core, p_below, p_above, q_core, q_below, q_above):
    summed = e_below * (p_core - p_below) * (q_core - q_below) + e_above * (p_core - p_above) * (
        q_core - q_above
    )
    for dimension in (2, 3):
        padding = [(0, 0), (0, 0), (0, 0), (0, 0)]
        padding[dimension] = (1, 1)
        e_pad = jnp.pad(e_core, padding, constant_values=1.0)
        p_pad = jnp.pad(p_core, padding)
        q_pad = jnp.pad(q_core, padding)
        extent = e_core.shape[dimension]
        for offset in (0, 2):
            e_near = lax.slice_in_dim(e_pad, offset, offset + extent, axis=dimension)
            p_near = lax.slice_in_dim(p_pad, offset, offset + extent, axis=dimension)
            q_near = lax.slice_in_dim(q_pad, offset, offset + extent, axis=dimension)
            summed = summed + e_near * (p_core - p_near) * (q_core - q_near)
    return -0.5 * e_core * summed


def on_device(logperm, source, observed, brownian):
    particles, width, rows_y, depth_z = logperm.shape
    slabs = lax.axis_size("slab")
    cells = width * slabs * rows_y * depth_z
    extended = with_halo(logperm, (("slab", 1),), 1)
    e_ext = jnp.exp(0.5 * extended)
    e_core = e_ext[:, 1:-1]
    inverse = 1.0 / neighbor_sum(e_core, e_ext[:, :-2], e_ext[:, 2:], 1.0)

    def relax_rim(rhs):
        value = inverse * rhs
        for sweep_index in range(SWEEPS - 1):
            bordered = with_halo(value, (("slab", 1),), 1)
            value = inverse * (
                rhs + e_core * neighbor_sum(value, bordered[:, :-2], bordered[:, 2:], 0.0)
            )
        return value / e_core

    pressure = relax_rim(source[None])
    misfit = misfit_weight * (pressure - observed[None])
    adjoint = relax_rim(misfit)
    states = with_halo(jnp.stack([pressure, adjoint]), (("slab", 2),), 1)
    gradient = grad_field(
        e_core,
        e_ext[:, :-2],
        e_ext[:, 2:],
        pressure,
        states[0][:, :-2],
        states[0][:, 2:],
        adjoint,
        states[1][:, :-2],
        states[1][:, 2:],
    )
    g_flat = gradient.reshape(particles, -1)
    u_cells, g_cells = (
        lax.all_to_all(
            logperm.reshape(particles, -1), "dom", split_axis=1, concat_axis=0, tiled=True
        ),
        lax.all_to_all(g_flat, "dom", split_axis=1, concat_axis=0, tiled=True),
    )
    ensemble = u_cells.shape[0]
    centre = jnp.mean(u_cells, axis=0, keepdims=True)
    spread = u_cells - centre
    partial_gram = lax.dot_general(
        spread,
        g_cells,
        (((1,), (1,)), ((), ())),
        precision=lax.Precision.HIGHEST,
        preferred_element_type=jnp.float32,
    )
    gram = lax.psum(partial_gram, ("dom", "slab"))
    step_size = ensemble / (4.0 * (cells + 1))
    mixing = -(step_size / ensemble) * gram + math.sqrt(2.0 * step_size / ensemble) * brownian
    moved = (
        centre
        + 1.25 * spread
        + lax.dot_general(
            mixing,
            spread,
            (((0,), (0,)), ((), ())),
            precision=lax.Precision.HIGHEST,
            preferred_element_type=jnp.float32,
        )
    )
    returned = lax.all_to_all(moved, "dom", split_axis=0, concat_axis=1, tiled=True)
    return returned.reshape(logperm.shape)


def solution(mesh):
    return jax.shard_map(
        on_device,
        mesh=mesh,
        in_specs=(P("dom", "slab", None, None), P("slab", None, None), P("slab", None, None), P()),
        out_specs=P("dom", "slab", None, None),
        check_vma=False,
    )
```

profile of v0, /device:TPU:8, one launch (start us, length us, event | category | flops | bytes accessed | tf_op | source)
XLA Modules:
  0.0 496.1 jit_solution(12891519340523834035)
XLA Ops:
  7.6 3.5 collective-permute-start
  11.1 2.4 collective-permute-start.1
  14.7 3.2 collective-permute-done.1
  19.5 3.2 collective-permute-start.2
  22.7 2.7 collective-permute-start.3
  26.4 3.2 collective-permute-done.3
  30.0 1.9 collective-permute-start.4
  31.9 3.9 collective-permute-start.5
  36.9 1.9 collective-permute-done.5
  39.2 1.9 collective-permute-start.6
  41.1 3.9 collective-permute-start.7
  46.1 1.9 collective-permute-done.7
  48.4 1.9 collective-permute-start.8
  50.4 3.9 collective-permute-start.9
  55.3 1.9 collective-permute-done.9
  57.6 1.9 collective-permute-start.10
  59.6 3.9 collective-permute-start.11
  64.8 1.9 collective-permute-done.11
  67.2 2.1 collective-permute-start.12
  69.3 3.9 collective-permute-start.13
  73.2 2.2 collective-permute-done.12
  75.4 1.9 collective-permute-done.13
  79.6 3.9 collective-permute-start.15
  85.0 1.9 collective-permute-done.15
  87.4 2.0 collective-permute-start.16
  89.4 3.9 collective-permute-start.17
  94.2 2.0 collective-permute-done.17
  98.6 3.9 collective-permute-start.19
  103.6 1.9 collective-permute-done.19
  107.9 3.9 collective-permute-start.21
  112.9 1.9 collective-permute-done.21
  115.3 1.9 collective-permute-start.22
  117.2 3.9 collective-permute-start.23
  122.1 1.9 collective-permute-done.23
  126.5 3.9 collective-permute-start.25
  131.4 1.9 collective-permute-done.25
  135.8 3.9 collective-permute-start.27
  140.7 1.9 collective-permute-done.27
  143.1 1.9 collective-permute-start.28
  145.1 4.1 collective-permute-start.29
  150.0 2.1 collective-permute-done.29
  155.3 4.6 collective-permute-start.31
  161.2 12.1 %all-to-all-start = ((f32[4,64,512]{2,0,1:T(4,128)}), f32[4,64,512]{2,0,1:T(4,128)S(1)}, u32[]{:S(2)}, u32[]{:S(2)}) async-start(f32[4,64,512]{2,0,1:T(4,128)} %copy.7), calls=%async_computation | async-start | bytes 1048576 | tf_op jit(solution)/shard_map/all_to_all | solution.py:87
  177.0 13.4 %all-to-all-done = f32[4,64,512]{2,0,1:T(4,128)S(1)} async-done(((f32[4,64,512]{2,0,1:T(4,128)}), f32[4,64,512]{2,0,1:T(4,128)S(1)}, u32[]{:S(2)}, u32[]{:S(2)}) %all-to-all-start) | async-done | bytes 524320 | tf_op jit(solution)/shard_map/all_to_all | solution.py:87
  190.3 6.4 %all-to-all-start.1 = ((f32[4,64,512]{2,0,1:T(4,128)}), f32[4,64,512]{2,0,1:T(4,128)S(1)}, u32[]{:S(2)}, u32[]{:S(2)}) async-start(f32[4,64,512]{2,0,1:T(4,128)} %copy.8), calls=%async_computation.1 | async-start | bytes 1048576 | tf_op jit(solution)/shard_map/all_to_all | solution.py:90
  197.2 16.7 %all-to-all-done.1 = f32[4,64,512]{2,0,1:T(4,128)S(1)} async-done(((f32[4,64,512]{2,0,1:T(4,128)}), f32[4,64,512]{2,0,1:T(4,128)S(1)}, u32[]{:S(2)}, u32[]{:S(2)}) %all-to-all-start.1) | async-done | bytes 524320 | tf_op jit(solution)/shard_map/all_to_all | solution.py:90
  215.7 245.9 %all-reduce.36.cloned.1.call-done = f32[256,256]{1,0:T(8,128)} async-done(((f32[256,256]{1,0:T(8,128)}), f32[256,256]{1,0:T(8,128)}) %all-reduce.36.cloned.1.call-update) | async-done | bytes 262160 | tf_op jit(solution)/shard_map/psum | solution.py:102
  463.3 24.9 %all_to_all.54 = f32[64,4,512]{2,1,0:T(4,128)S(1)} all-to-all(f32[64,4,512]{2,1,0:T(4,128)S(1)} %all_to_all.48), channel_id=1, replica_groups=mesh['dom'=64,'slab'=4] {'dom'}, dimensions={0} | all-to-all | bytes 1048576 | tf_op jit(solution)/shard_map/all_to_all | solution.py:116
  (83 shorter events, 45.8 us)
Async XLA Ops:
  6.5 12.6 %copy-start.1 = (f32[4,64,128]{2,1,0:T(8,128)S(1)}, f32[4,64,128]{2,1,0:T(8,128)}, u32[]{:S(2)}) copy-start(f32[4,64,128]{2,1,0:T(8,128)} %param.5) | copy-start | bytes 393220
  7.6 7.1 %collective-permute-start = (f32[4,1,64,128]{3,2,1,0:T(8,128)S(1)}, f32[4,1,64,128]{3,2,1,0:T(8,128)S(1)}, u32[]{:S(2)}, u32[]{:S(2)}) collective-permute-start(f32[4,1,64,128]{3,2,1,0:T(8,128)S(1)} %get-tuple-element.41), channel_id=1, source_target_pairs={{0,1},{1,2},{2,3},{4,5},{5,6},{6,7},{8,9},{9,10},{10,11},{12,13},{... | collective-permute-start | bytes 393224 | tf_op jit(solution)/shard_map/ppermute | solution.py:19
  11.1 6.9 %collective-permute-start.1 = (f32[4,1,64,128]{3,2,1,0:T(8,128)S(1)}, f32[4,1,64,128]{3,2,1,0:T(8,128)S(1)}, u32[]{:S(2)}, u32[]{:S(2)}) collective-permute-start(f32[4,1,64,128]{3,2,1,0:T(8,128)S(1)} %get-tuple-element.42), channel_id=1, source_target_pairs={{1,0},{2,1},{3,2},{5,4},{6,5},{7,6},{9,8},{10,9},{11,10},{13,12},{... | collective-permute-start | bytes 393224 | tf_op jit(solution)/shard_map/ppermute | solution.py:22
  19.5 6.9 %collective-permute-start.2 = (f32[4,1,64,128]{3,2,1,0:T(8,128)S(1)}, f32[4,1,64,128]{3,2,1,0:T(8,128)S(1)}, u32[]{:S(2)}, u32[]{:S(2)}) collective-permute-start(f32[4,1,64,128]{3,2,1,0:T(8,128)S(1)} %get-tuple-element.39), channel_id=1, source_target_pairs={{0,1},{1,2},{2,3},{4,5},{5,6},{6,7},{8,9},{9,10},{10,11},{12,13},{... | collective-permute-start | bytes 393224 | tf_op jit(solution)/shard_map/ppermute | solution.py:19
  22.7 6.9 %collective-permute-start.3 = (f32[4,1,64,128]{3,2,1,0:T(8,128)S(1)}, f32[4,1,64,128]{3,2,1,0:T(8,128)S(1)}, u32[]{:S(2)}, u32[]{:S(2)}) collective-permute-start(f32[4,1,64,128]{3,2,1,0:T(8,128)S(1)} %get-tuple-element.40), channel_id=1, source_target_pairs={{1,0},{2,1},{3,2},{5,4},{6,5},{7,6},{9,8},{10,9},{11,10},{13,12},{... | collective-permute-start | bytes 393224 | tf_op jit(solution)/shard_map/ppermute | solution.py:22
  30.0 6.9 %collective-permute-start.4 = (f32[4,1,64,128]{3,2,1,0:T(8,128)S(1)}, f32[4,1,64,128]{3,2,1,0:T(8,128)S(1)}, u32[]{:S(2)}, u32[]{:S(2)}) collective-permute-start(f32[4,1,64,128]{3,2,1,0:T(8,128)S(1)} %get-tuple-element.37), channel_id=1, source_target_pairs={{0,1},{1,2},{2,3},{4,5},{5,6},{6,7},{8,9},{9,10},{10,11},{12,13},{... | collective-permute-start | bytes 393224 | tf_op jit(solution)/shard_map/ppermute | solution.py:19
  31.9 6.9 %collective-permute-start.5 = (f32[4,1,64,128]{3,2,1,0:T(8,128)S(1)}, f32[4,1,64,128]{3,2,1,0:T(8,128)S(1)}, u32[]{:S(2)}, u32[]{:S(2)}) collective-permute-start(f32[4,1,64,128]{3,2,1,0:T(8,128)S(1)} %get-tuple-element.38), channel_id=1, source_target_pairs={{1,0},{2,1},{3,2},{5,4},{6,5},{7,6},{9,8},{10,9},{11,10},{13,12},{... | collective-permute-start | bytes 393224 | tf_op jit(solution)/shard_map/ppermute | solution.py:22
  39.2 6.9 %collective-permute-start.6 = (f32[4,1,64,128]{3,2,1,0:T(8,128)S(1)}, f32[4,1,64,128]{3,2,1,0:T(8,128)S(1)}, u32[]{:S(2)}, u32[]{:S(2)}) collective-permute-start(f32[4,1,64,128]{3,2,1,0:T(8,128)S(1)} %get-tuple-element.35), channel_id=1, source_target_pairs={{0,1},{1,2},{2,3},{4,5},{5,6},{6,7},{8,9},{9,10},{10,11},{12,13},{... | collective-permute-start | bytes 393224 | tf_op jit(solution)/shard_map/ppermute | solution.py:19
  41.1 6.9 %collective-permute-start.7 = (f32[4,1,64,128]{3,2,1,0:T(8,128)S(1)}, f32[4,1,64,128]{3,2,1,0:T(8,128)S(1)}, u32[]{:S(2)}, u32[]{:S(2)}) collective-permute-start(f32[4,1,64,128]{3,2,1,0:T(8,128)S(1)} %get-tuple-element.36), channel_id=1, source_target_pairs={{1,0},{2,1},{3,2},{5,4},{6,5},{7,6},{9,8},{10,9},{11,10},{13,12},{... | collective-permute-start | bytes 393224 | tf_op jit(solution)/shard_map/ppermute | solution.py:22
  48.4 6.9 %collective-permute-start.8 = (f32[4,1,64,128]{3,2,1,0:T(8,128)S(1)}, f32[4,1,64,128]{3,2,1,0:T(8,128)S(1)}, u32[]{:S(2)}, u32[]{:S(2)}) collective-permute-start(f32[4,1,64,128]{3,2,1,0:T(8,128)S(1)} %get-tuple-element.33), channel_id=1, source_target_pairs={{0,1},{1,2},{2,3},{4,5},{5,6},{6,7},{8,9},{9,10},{10,11},{12,13},{... | collective-permute-start | bytes 393224 | tf_op jit(solution)/shard_map/ppermute | solution.py:19
  50.4 6.9 %collective-permute-start.9 = (f32[4,1,64,128]{3,2,1,0:T(8,128)S(1)}, f32[4,1,64,128]{3,2,1,0:T(8,128)S(1)}, u32[]{:S(2)}, u32[]{:S(2)}) collective-permute-start(f32[4,1,64,128]{3,2,1,0:T(8,128)S(1)} %get-tuple-element.34), channel_id=1, source_target_pairs={{1,0},{2,1},{3,2},{5,4},{6,5},{7,6},{9,8},{10,9},{11,10},{13,12},{... | collective-permute-start | bytes 393224 | tf_op jit(solution)/shard_map/ppermute | solution.py:22
  57.6 7.2 %collective-permute-start.10 = (f32[4,1,64,128]{3,2,1,0:T(8,128)S(1)}, f32[4,1,64,128]{3,2,1,0:T(8,128)S(1)}, u32[]{:S(2)}, u32[]{:S(2)}) collective-permute-start(f32[4,1,64,128]{3,2,1,0:T(8,128)S(1)} %get-tuple-element.31), channel_id=1, source_target_pairs={{0,1},{1,2},{2,3},{4,5},{5,6},{6,7},{8,9},{9,10},{10,11},{12,13},{... | collective-permute-start | bytes 393224 | tf_op jit(solution)/shard_map/ppermute | solution.py:19
  59.6 7.2 %collective-permute-start.11 = (f32[4,1,64,128]{3,2,1,0:T(8,128)S(1)}, f32[4,1,64,128]{3,2,1,0:T(8,128)S(1)}, u32[]{:S(2)}, u32[]{:S(2)}) collective-permute-start(f32[4,1,64,128]{3,2,1,0:T(8,128)S(1)} %get-tuple-element.32), channel_id=1, source_target_pairs={{1,0},{2,1},{3,2},{5,4},{6,5},{7,6},{9,8},{10,9},{11,10},{13,12},{... | collective-permute-start | bytes 393224 | tf_op jit(solution)/shard_map/ppermute | solution.py:22
  67.2 19.7 %copy-start = (f32[4,64,128]{2,1,0:T(8,128)S(1)}, f32[4,64,128]{2,1,0:T(8,128)}, u32[]{:S(2)}) copy-start(f32[4,64,128]{2,1,0:T(8,128)} %param.6) | copy-start | bytes 393220
  67.2 8.2 %collective-permute-start.12 = (f32[4,1,64,128]{3,2,1,0:T(8,128)S(1)}, f32[4,1,64,128]{3,2,1,0:T(8,128)S(1)}, u32[]{:S(2)}, u32[]{:S(2)}) collective-permute-start(f32[4,1,64,128]{3,2,1,0:T(8,128)S(1)} %get-tuple-element.29), channel_id=1, source_target_pairs={{0,1},{1,2},{2,3},{4,5},{5,6},{6,7},{8,9},{9,10},{10,11},{12,13},{... | collective-permute-start | bytes 393224 | tf_op jit(solution)/shard_map/ppermute | solution.py:19
  69.3 8.0 %collective-permute-start.13 = (f32[4,1,64,128]{3,2,1,0:T(8,128)S(1)}, f32[4,1,64,128]{3,2,1,0:T(8,128)S(1)}, u32[]{:S(2)}, u32[]{:S(2)}) collective-permute-start(f32[4,1,64,128]{3,2,1,0:T(8,128)S(1)} %get-tuple-element.30), channel_id=1, source_target_pairs={{1,0},{2,1},{3,2},{5,4},{6,5},{7,6},{9,8},{10,9},{11,10},{13,12},{... | collective-permute-start | bytes 393224 | tf_op jit(solution)/shard_map/ppermute | solution.py:22
  77.7 7.3 %collective-permute-start.14 = (f32[4,1,64,128]{3,2,1,0:T(8,128)S(1)}, f32[4,1,64,128]{3,2,1,0:T(8,128)S(1)}, u32[]{:S(2)}, u32[]{:S(2)}) collective-permute-start(f32[4,1,64,128]{3,2,1,0:T(8,128)S(1)} %get-tuple-element.27), channel_id=1, source_target_pairs={{0,1},{1,2},{2,3},{4,5},{5,6},{6,7},{8,9},{9,10},{10,11},{12,13},{... | collective-permute-start | bytes 393224 | tf_op jit(solution)/shard_map/ppermute | solution.py:19
  79.6 7.3 %collective-permute-start.15 = (f32[4,1,64,128]{3,2,1,0:T(8,128)S(1)}, f32[4,1,64,128]{3,2,1,0:T(8,128)S(1)}, u32[]{:S(2)}, u32[]{:S(2)}) collective-permute-start(f32[4,1,64,128]{3,2,1,0:T(8,128)S(1)} %get-tuple-element.28), channel_id=1, source_target_pairs={{1,0},{2,1},{3,2},{5,4},{6,5},{7,6},{9,8},{10,9},{11,10},{13,12},{... | collective-permute-start | bytes 393224 | tf_op jit(solution)/shard_map/ppermute | solution.py:22
  87.4 6.9 %collective-permute-start.16 = (f32[4,1,64,128]{3,2,1,0:T(8,128)S(1)}, f32[4,1,64,128]{3,2,1,0:T(8,128)S(1)}, u32[]{:S(2)}, u32[]{:S(2)}) collective-permute-start(f32[4,1,64,128]{3,2,1,0:T(8,128)S(1)} %get-tuple-element.25), channel_id=1, source_target_pairs={{0,1},{1,2},{2,3},{4,5},{5,6},{6,7},{8,9},{9,10},{10,11},{12,13},{... | collective-permute-start | bytes 393224 | tf_op jit(solution)/shard_map/ppermute | solution.py:19
  89.4 6.9 %collective-permute-start.17 = (f32[4,1,64,128]{3,2,1,0:T(8,128)S(1)}, f32[4,1,64,128]{3,2,1,0:T(8,128)S(1)}, u32[]{:S(2)}, u32[]{:S(2)}) collective-permute-start(f32[4,1,64,128]{3,2,1,0:T(8,128)S(1)} %get-tuple-element.26), channel_id=1, source_target_pairs={{1,0},{2,1},{3,2},{5,4},{6,5},{7,6},{9,8},{10,9},{11,10},{13,12},{... | collective-permute-start | bytes 393224 | tf_op jit(solution)/shard_map/ppermute | solution.py:22
  96.7 6.9 %collective-permute-start.18 = (f32[4,1,64,128]{3,2,1,0:T(8,128)S(1)}, f32[4,1,64,128]{3,2,1,0:T(8,128)S(1)}, u32[]{:S(2)}, u32[]{:S(2)}) collective-permute-start(f32[4,1,64,128]{3,2,1,0:T(8,128)S(1)} %get-tuple-element.23), channel_id=1, source_target_pairs={{0,1},{1,2},{2,3},{4,5},{5,6},{6,7},{8,9},{9,10},{10,11},{12,13},{... | collective-permute-start | bytes 393224 | tf_op jit(solution)/shard_map/ppermute | solution.py:19
  98.6 6.9 %collective-permute-start.19 = (f32[4,1,64,128]{3,2,1,0:T(8,128)S(1)}, f32[4,1,64,128]{3,2,1,0:T(8,128)S(1)}, u32[]{:S(2)}, u32[]{:S(2)}) collective-permute-start(f32[4,1,64,128]{3,2,1,0:T(8,128)S(1)} %get-tuple-element.24), channel_id=1, source_target_pairs={{1,0},{2,1},{3,2},{5,4},{6,5},{7,6},{9,8},{10,9},{11,10},{13,12},{... | collective-permute-start | bytes 393224 | tf_op jit(solution)/shard_map/ppermute | solution.py:22
  106.0 6.9 %collective-permute-start.20 = (f32[4,1,64,128]{3,2,1,0:T(8,128)S(1)}, f32[4,1,64,128]{3,2,1,0:T(8,128)S(1)}, u32[]{:S(2)}, u32[]{:S(2)}) collective-permute-start(f32[4,1,64,128]{3,2,1,0:T(8,128)S(1)} %get-tuple-element.21), channel_id=1, source_target_pairs={{0,1},{1,2},{2,3},{4,5},{5,6},{6,7},{8,9},{9,10},{10,11},{12,13},{... | collective-permute-start | bytes 393224 | tf_op jit(solution)/shard_map/ppermute | solution.py:19
  107.9 6.9 %collective-permute-start.21 = (f32[4,1,64,128]{3,2,1,0:T(8,128)S(1)}, f32[4,1,64,128]{3,2,1,0:T(8,128)S(1)}, u32[]{:S(2)}, u32[]{:S(2)}) collective-permute-start(f32[4,1,64,128]{3,2,1,0:T(8,128)S(1)} %get-tuple-element.22), channel_id=1, source_target_pairs={{1,0},{2,1},{3,2},{5,4},{6,5},{7,6},{9,8},{10,9},{11,10},{13,12},{... | collective-permute-start | bytes 393224 | tf_op jit(solution)/shard_map/ppermute | solution.py:22
  115.3 6.9 %collective-permute-start.22 = (f32[4,1,64,128]{3,2,1,0:T(8,128)S(1)}, f32[4,1,64,128]{3,2,1,0:T(8,128)S(1)}, u32[]{:S(2)}, u32[]{:S(2)}) collective-permute-start(f32[4,1,64,128]{3,2,1,0:T(8,128)S(1)} %get-tuple-element.19), channel_id=1, source_target_pairs={{0,1},{1,2},{2,3},{4,5},{5,6},{6,7},{8,9},{9,10},{10,11},{12,13},{... | collective-permute-start | bytes 393224 | tf_op jit(solution)/shard_map/ppermute | solution.py:19
  117.2 6.9 %collective-permute-start.23 = (f32[4,1,64,128]{3,2,1,0:T(8,128)S(1)}, f32[4,1,64,128]{3,2,1,0:T(8,128)S(1)}, u32[]{:S(2)}, u32[]{:S(2)}) collective-permute-start(f32[4,1,64,128]{3,2,1,0:T(8,128)S(1)} %get-tuple-element.20), channel_id=1, source_target_pairs={{1,0},{2,1},{3,2},{5,4},{6,5},{7,6},{9,8},{10,9},{11,10},{13,12},{... | collective-permute-start | bytes 393224 | tf_op jit(solution)/shard_map/ppermute | solution.py:22
  124.6 6.9 %collective-permute-start.24 = (f32[4,1,64,128]{3,2,1,0:T(8,128)S(1)}, f32[4,1,64,128]{3,2,1,0:T(8,128)S(1)}, u32[]{:S(2)}, u32[]{:S(2)}) collective-permute-start(f32[4,1,64,128]{3,2,1,0:T(8,128)S(1)} %get-tuple-element.17), channel_id=1, source_target_pairs={{0,1},{1,2},{2,3},{4,5},{5,6},{6,7},{8,9},{9,10},{10,11},{12,13},{... | collective-permute-start | bytes 393224 | tf_op jit(solution)/shard_map/ppermute | solution.py:19
  126.5 6.9 %collective-permute-start.25 = (f32[4,1,64,128]{3,2,1,0:T(8,128)S(1)}, f32[4,1,64,128]{3,2,1,0:T(8,128)S(1)}, u32[]{:S(2)}, u32[]{:S(2)}) collective-permute-start(f32[4,1,64,128]{3,2,1,0:T(8,128)S(1)} %get-tuple-element.18), channel_id=1, source_target_pairs={{1,0},{2,1},{3,2},{5,4},{6,5},{7,6},{9,8},{10,9},{11,10},{13,12},{... | collective-permute-start | bytes 393224 | tf_op jit(solution)/shard_map/ppermute | solution.py:22
  133.8 6.9 %collective-permute-start.26 = (f32[4,1,64,128]{3,2,1,0:T(8,128)S(1)}, f32[4,1,64,128]{3,2,1,0:T(8,128)S(1)}, u32[]{:S(2)}, u32[]{:S(2)}) collective-permute-start(f32[4,1,64,128]{3,2,1,0:T(8,128)S(1)} %get-tuple-element.15), channel_id=1, source_target_pairs={{0,1},{1,2},{2,3},{4,5},{5,6},{6,7},{8,9},{9,10},{10,11},{12,13},{... | collective-permute-start | bytes 393224 | tf_op jit(solution)/shard_map/ppermute | solution.py:19
  135.8 6.9 %collective-permute-start.27 = (f32[4,1,64,128]{3,2,1,0:T(8,128)S(1)}, f32[4,1,64,128]{3,2,1,0:T(8,128)S(1)}, u32[]{:S(2)}, u32[]{:S(2)}) collective-permute-start(f32[4,1,64,128]{3,2,1,0:T(8,128)S(1)} %get-tuple-element.16), channel_id=1, source_target_pairs={{1,0},{2,1},{3,2},{5,4},{6,5},{7,6},{9,8},{10,9},{11,10},{13,12},{... | collective-permute-start | bytes 393224 | tf_op jit(solution)/shard_map/ppermute | solution.py:22
  143.1 6.9 %collective-permute-start.28 = (f32[4,1,64,128]{3,2,1,0:T(8,128)S(1)}, f32[4,1,64,128]{3,2,1,0:T(8,128)S(1)}, u32[]{:S(2)}, u32[]{:S(2)}) collective-permute-start(f32[4,1,64,128]{3,2,1,0:T(8,128)S(1)} %get-tuple-element.13), channel_id=1, source_target_pairs={{0,1},{1,2},{2,3},{4,5},{5,6},{6,7},{8,9},{9,10},{10,11},{12,13},{... | collective-permute-start | bytes 393224 | tf_op jit(solution)/shard_map/ppermute | solution.py:19
  145.1 14.9 %copy-start.2 = (f32[4,4,64,128]{3,2,1,0:T(8,128)S(1)}, f32[4,4,64,128]{3,2,1,0:T(8,128)}, u32[]{:S(2)}) copy-start(f32[4,4,64,128]{3,2,1,0:T(8,128)} %param.4) | copy-start | bytes 1572868
  145.1 7.0 %collective-permute-start.29 = (f32[4,1,64,128]{3,2,1,0:T(8,128)S(1)}, f32[4,1,64,128]{3,2,1,0:T(8,128)S(1)}, u32[]{:S(2)}, u32[]{:S(2)}) collective-permute-start(f32[4,1,64,128]{3,2,1,0:T(8,128)S(1)} %get-tuple-element.14), channel_id=1, source_target_pairs={{1,0},{2,1},{3,2},{5,4},{6,5},{7,6},{9,8},{10,9},{11,10},{13,12},{... | collective-permute-start | bytes 393224 | tf_op jit(solution)/shard_map/ppermute | solution.py:22
  153.4 19.9 %collective-permute-start.30 = (f32[2,4,1,64,128]{4,3,2,1,0:T(8,128)}, f32[2,4,1,64,128]{4,3,2,1,0:T(8,128)}, u32[]{:S(2)}, u32[]{:S(2)}) collective-permute-start(f32[2,4,1,64,128]{4,3,2,1,0:T(8,128)} %get-tuple-element.11), channel_id=1, source_target_pairs={{0,1},{1,2},{2,3},{4,5},{5,6},{6,7},{8,9},{9,10},{10,11},{12,13},{... | collective-permute-start | bytes 786440 | tf_op jit(solution)/shard_map/ppermute | solution.py:19
  155.3 18.0 %collective-permute-start.31 = (f32[2,4,1,64,128]{4,3,2,1,0:T(8,128)}, f32[2,4,1,64,128]{4,3,2,1,0:T(8,128)}, u32[]{:S(2)}, u32[]{:S(2)}) collective-permute-start(f32[2,4,1,64,128]{4,3,2,1,0:T(8,128)} %get-tuple-element.12), channel_id=1, source_target_pairs={{1,0},{2,1},{3,2},{5,4},{6,5},{7,6},{9,8},{10,9},{11,10},{13,12},{... | collective-permute-start | bytes 786440 | tf_op jit(solution)/shard_map/ppermute | solution.py:22
  161.2 29.1 %all-to-all-start = ((f32[4,64,512]{2,0,1:T(4,128)}), f32[4,64,512]{2,0,1:T(4,128)S(1)}, u32[]{:S(2)}, u32[]{:S(2)}) async-start(f32[4,64,512]{2,0,1:T(4,128)} %copy.7), calls=%async_computation | async-start | bytes 1048576 | tf_op jit(solution)/shard_map/all_to_all | solution.py:87
  190.3 23.6 %all-to-all-start.1 = ((f32[4,64,512]{2,0,1:T(4,128)}), f32[4,64,512]{2,0,1:T(4,128)S(1)}, u32[]{:S(2)}, u32[]{:S(2)}) async-start(f32[4,64,512]{2,0,1:T(4,128)} %copy.8), calls=%async_computation.1 | async-start | bytes 1048576 | tf_op jit(solution)/shard_map/all_to_all | solution.py:90
  196.7 264.8 %all-reduce.36.cloned.1.call-start = ((), (), s32[]{:S(2)}) async-start(), calls=%async_computation.3 | async-start | bytes 524288 | tf_op jit(solution)/shard_map/psum | solution.py:102
  214.1 247.4 %copy-start.3 = (f32[256,256]{1,0:T(8,128)S(1)}, f32[256,256]{1,0:T(8,128)}, u32[]{:S(2)}) copy-start(f32[256,256]{1,0:T(8,128)} %param.7) | copy-start | bytes 786436
Sparse Core Ops, SparseCore 0:
  215.6 245.9 all-reduce.35
where the time goes:
time: 499 us; the launch traced here: 496 us
  waiting for transfers between devices  325 us (65%)
  starting transfers between devices  113 us (23%)
  blocking collectives  24.9 us (5%)
  between operations  14.1 us (3%)
  other arithmetic  10.8 us (2%)
  local copies, waits for them, and re-layouts  5.66 us (1%)
    psum x1, waiting for transfers between devices, on_device(): gram = lax.psum(partial_gram, ('dom', 'slab'))  246 us
    ppermute x16, starting transfers between devices, with_halo(): lax.ppermute(lax.slice_in_dim(block, 0, width, axis=dim), axis, backward)  60.7 us
    ppermute x16, starting transfers between devices, with_halo(): lax.ppermute(lax.slice_in_dim(block, block.shape[dim] - width, None, axis...  33.7 us
    ppermute x16, waiting for transfers between devices, with_halo(): lax.ppermute(lax.slice_in_dim(block, 0, width, axis=dim), axis, backward)  31.7 us
    all_to_all x1, blocking collectives, on_device(): lax.all_to_all(moved, 'dom', split_axis=0, concat_axis=1, tiled=True)  24.9 us
    ppermute x16, waiting for transfers between devices, with_halo(): lax.ppermute(lax.slice_in_dim(block, block.shape[dim] - width, None, axis...  17 us
    all_to_all x1, waiting for transfers between devices, on_device(): lax.all_to_all(g_flat, 'dom', split_axis=1, concat_axis=0, tiled=True)  16.7 us
    all_to_all x1, waiting for transfers between devices, on_device(): lax.all_to_all(logperm.reshape(particles, -1), 'dom', split_axis=1, conca...  13.4 us
  transfers between devices with their start and end apart: 35, of which 33 were waited for; matrix products, arithmetic and copies ran while one was open for 1% of the time, Pallas kernels for 0%

commit v1 on v0

v1 whole, which is shorter than its diff:
```python
import math

import jax
import jax.numpy as jnp
from jax import lax
from jax.experimental import pallas as pl
from jax.experimental.pallas import tpu as pltpu
from jax.sharding import Mesh
from jax.sharding import PartitionSpec as P

SWEEPS = 8
MISFIT_WEIGHT = 1000.0
PAD = 8


def darcy_kernel(u_ref, src_ref, obs_ref, g_ref, e_s, w0, w1, inv_s, b_s, a_s, p_s):
    layers, rows, lanes = u_ref.shape
    lane = lax.broadcasted_iota(jnp.int32, (rows, lanes), 1)
    first = lane == 0
    last = lane == lanes - 1
    mid = pl.ds(PAD, rows)
    up = pl.ds(PAD - 1, rows)
    down = pl.ds(PAD + 1, rows)

    def before(v, fill):
        return jnp.where(first, fill, pltpu.roll(v, 1, 1))

    def after(v, fill):
        return jnp.where(last, fill, pltpu.roll(v, lanes - 1, 1))

    def each_layer(body):
        def step(i, carry):
            body(i)
            return carry

        lax.fori_loop(0, layers, step, 0, unroll=2)

    def neighbors(ref, i, fill):
        core = ref[i + 1, mid, :]
        return (
            (ref[i, mid, :] + ref[i + 2, mid, :])
            + (ref[i + 1, up, :] + ref[i + 1, down, :])
            + (before(core, fill) + after(core, fill))
        )

    e_s[...] = jnp.ones_like(e_s)
    w0[...] = jnp.zeros_like(w0)
    w1[...] = jnp.zeros_like(w1)
    p_s[...] = jnp.zeros_like(p_s)

    def fill_e(i):
        e_s[i + 1, mid, :] = jnp.exp(0.5 * u_ref[i])

    each_layer(fill_e)

    def fill_inv(i):
        inverse = 1.0 / neighbors(e_s, i, 1.0)
        inv_s[i] = inverse
        b_s[i] = inverse * e_s[i + 1, mid, :]
        start = inverse * src_ref[i]
        a_s[i] = start
        w0[i + 1, mid, :] = start

    each_layer(fill_inv)

    def relax():
        now, new = w0, w1
        for _ in range(SWEEPS - 1):

            def sweep(i, now=now, new=new):
                new[i + 1, mid, :] = a_s[i] + b_s[i] * neighbors(now, i, 0.0)

            each_layer(sweep)
            now, new = new, now
        return now

    end = relax()

    def to_adjoint(i):
        pressure = end[i + 1, mid, :] / e_s[i + 1, mid, :]
        p_s[i + 1, mid, :] = pressure
        start = inv_s[i] * (MISFIT_WEIGHT * (pressure - obs_ref[i]))
        a_s[i] = start
        w0[i + 1, mid, :] = start

    each_layer(to_adjoint)
    end = relax()

    def to_pressure(i):
        end[i + 1, mid, :] = end[i + 1, mid, :] / e_s[i + 1, mid, :]

    each_layer(to_pressure)

    def gradient(i):
        e = e_s[i + 1, mid, :]
        p = p_s[i + 1, mid, :]
        q = end[i + 1, mid, :]
        total = None
        for at, where in ((i, mid), (i + 2, mid), (i + 1, up), (i + 1, down)):
            term = e_s[at, where, :] * (p - p_s[at, where, :]) * (q - end[at, where, :])
            total = term if total is None else total + term
        for shift in (before, after):
            total = total + shift(e, 1.0) * (p - shift(p, 0.0)) * (q - shift(q, 0.0))
        return -0.5 * e * total

    slabs = layers // 4

    def write(s, carry):
        for b in range(4):
            g_ref[b * slabs + s] = gradient(s * 4 + b)
        return carry

    lax.fori_loop(0, slabs, write, 0)


def darcy(u, source, observed):
    layers, rows, lanes = u.shape
    padded = pltpu.VMEM((layers + 2, rows + 2 * PAD, lanes), jnp.float32)
    plain = pltpu.VMEM((layers, rows, lanes), jnp.float32)
    return pl.pallas_call(
        darcy_kernel,
        out_shape=jax.ShapeDtypeStruct(u.shape, jnp.float32),
        scratch_shapes=[padded, padded, padded, plain, plain, plain, padded],
        compiler_params=pltpu.CompilerParams(vmem_limit_bytes=24 << 20),
        name="darcy",
    )(u, source, observed)


def split(v):
    high = v.astype(jnp.bfloat16)
    low = (v - high.astype(jnp.float32)).astype(jnp.bfloat16)
    return high, low


def gram_kernel(u_ref, g_ref, o_ref):
    @pl.when(pl.program_id(0) == 0)
    def _():
        o_ref[...] = jnp.zeros_like(o_ref)

    members = u_ref.shape[0]
    block = g_ref.shape[0]
    u = u_ref[...]
    s = u - jnp.sum(u, axis=0, keepdims=True) * (1.0 / members)
    s_high, s_low = split(s)
    pair = jnp.concatenate(split(g_ref[...]), axis=0)
    dims = (((1,), (1,)), ((), ()))
    out = lax.dot_general(pair, s_high, dims, preferred_element_type=jnp.float32)
    out = out + lax.dot_general(pair, s_low, dims, preferred_element_type=jnp.float32)
    o_ref[...] += out[:block] + out[block:]


def gram_product(u_all, g, tile):
    members, cells = u_all.shape
    block = g.shape[0]
    return pl.pallas_call(
        gram_kernel,
        grid=(cells // tile,),
        in_specs=[
            pl.BlockSpec((members, tile), lambda i: (0, i)),
            pl.BlockSpec((block, tile), lambda i: (0, i)),
        ],
        out_specs=pl.BlockSpec((block, members), lambda i: (0, 0)),
        out_shape=jax.ShapeDtypeStruct((block, members), jnp.float32),
        compiler_params=pltpu.CompilerParams(vmem_limit_bytes=24 << 20),
        name="gram",
    )(u_all, g)


def move_kernel(u_ref, own_ref, m_ref, o_ref):
    members = u_ref.shape[0]
    block, groups, lanes = o_ref.shape
    u = u_ref[...]
    centre = jnp.sum(u, axis=0, keepdims=True) * (1.0 / members)
    s_high, s_low = split(u - centre)
    pair = jnp.concatenate(split(m_ref[...]), axis=0)
    dims = (((1,), (0,)), ((), ()))
    out = lax.dot_general(pair, s_high, dims, preferred_element_type=jnp.float32)
    out = out + lax.dot_general(pair, s_low, dims, preferred_element_type=jnp.float32)
    moved = centre + 1.25 * (own_ref[...] - centre) + (out[:block] + out[block:])
    for r in range(groups):
        o_ref[:, r, :] = moved[:, r * lanes : (r + 1) * lanes]


def move(u_all, own, mixing, tile):
    members, cells = u_all.shape
    block = own.shape[0]
    lanes = 128
    return pl.pallas_call(
        move_kernel,
        grid=(cells // tile,),
        in_specs=[
            pl.BlockSpec((members, tile), lambda i: (0, i)),
            pl.BlockSpec((block, tile), lambda i: (0, i)),
            pl.BlockSpec((block, members), lambda i: (0, 0)),
        ],
        out_specs=pl.BlockSpec((block, tile // lanes, lanes), lambda i: (0, i, 0)),
        out_shape=jax.ShapeDtypeStruct((block, cells // lanes, lanes), jnp.float32),
        compiler_params=pltpu.CompilerParams(vmem_limit_bytes=24 << 20),
        name="move",
    )(u_all, own, mixing)


def on_device(logperm, source, observed, brownian):
    particles, width, rows, lanes = logperm.shape
    slabs = lax.axis_size("y")
    xs = lax.axis_size("x")
    groups = lax.axis_size("z") * lax.axis_size("c")
    ensemble = particles * xs * groups
    layer = rows * lanes
    cells = width * slabs * layer

    chunks = jnp.swapaxes(logperm.reshape(particles, width, layer), 0, 1)
    own = lax.all_to_all(chunks, "x", split_axis=0, concat_axis=0, tiled=True)
    own = own.reshape(xs * particles, layer)
    u_all = lax.all_gather(own, ("z", "c"), axis=0, tiled=True)

    own_now, logperm_now = lax.optimization_barrier((own, logperm))
    shared = jnp.stack([source, observed])
    sent = jnp.concatenate(
        [logperm_now[:, None], jnp.broadcast_to(shared[None], (particles,) + shared.shape)], axis=1
    )
    whole = lax.all_to_all(sent, "y", split_axis=0, concat_axis=0, tiled=True)
    whole = jnp.swapaxes(whole, 0, 1).reshape(3, slabs * width, rows, lanes)
    gradient = darcy(whole[0], whole[1], whole[2])
    g = lax.all_to_all(gradient, ("x", "y"), split_axis=0, concat_axis=0, tiled=True)
    g = g.reshape(xs * particles, layer)

    step_size = ensemble / (4.0 * (cells + 1))
    noise = brownian.reshape(xs, groups, particles, xs, groups, particles)
    noise = lax.dynamic_index_in_dim(noise, lax.axis_index(("z", "c")), axis=4, keepdims=False)
    noise = jnp.transpose(noise, (3, 4, 1, 0, 2)).reshape(xs * particles, ensemble)
    noise = math.sqrt(2.0 * step_size / ensemble) * noise

    part = gram_product(u_all, g, 1024)
    copies = jnp.broadcast_to(part[None], (xs * slabs,) + part.shape)
    gram = jnp.sum(lax.all_to_all(copies, ("x", "y"), split_axis=0, concat_axis=0, tiled=True), axis=0)
    mixing = -(step_size / ensemble) * gram + noise
    moved = move(u_all, own_now, mixing, 1024)
    moved = moved.reshape(xs, particles, rows, lanes)
    returned = lax.all_to_all(moved, "x", split_axis=0, concat_axis=0, tiled=True)
    return jnp.swapaxes(returned, 0, 1)


def solution(mesh):
    fine = Mesh(mesh.devices.reshape(4, 8, 2, 4), ("x", "z", "c", "y"))
    dom = ("x", "z", "c")
    return jax.shard_map(
        on_device,
        mesh=fine,
        in_specs=(P(dom, "y", None, None), P("y", None, None), P("y", None, None), P()),
        out_specs=P(dom, "y", None, None),
        check_vma=False,
    )
```

time: 499 us -> 140 us (0.28)
  waiting for transfers between devices: 325 us -> 6.16 us
  starting transfers between devices: 113 us -> 7.26 us
  blocking collectives: 24.9 us -> 62.9 us
  Pallas kernels: 0 us -> 23.1 us
  local copies, waits for them, and re-layouts: 5.66 us -> 23.9 us
  other arithmetic: 10.8 us -> 3.03 us
    psum x1 -> x0, waiting for transfers between devices: 246 us -> none  [on_device(): gram = lax.psum(partial_gram, ('dom', 'slab'))]
    ppermute x32 -> x0, starting transfers between devices: 94.5 us -> none  [the longest x16 60.7 us: with_halo(): lax.ppermute(lax.slice_in_dim(block, 0, width, axis=dim), axis, backward)]
    ppermute x32 -> x0, waiting for transfers between devices: 48.7 us -> none  [the longest x16 31.7 us: with_halo(): lax.ppermute(lax.slice_in_dim(block, 0, width, axis=dim), axis, backward)]
    all_to_all x1 -> x4, blocking collectives: 24.9 us -> 62.9 us  [the longest x1 22.8 us: on_device(): whole = lax.all_to_all(sent, 'y', split_axis=0, concat_axis=0, tiled=True)]
    all_to_all x2 -> x1, waiting for transfers between devices: 30.1 us -> 0.01 us  [on_device(): lax.all_to_all(copies, ('x', 'y'), split_axis=0, concat_axis=0, tiled=True)]
    pallas_call x0 -> x3, Pallas kernels: none -> 23.1 us  [the longest x1 14.4 us: darcy(): pl.pallas_call(darcy_kernel, out_shape=jax.ShapeDtypeStruct(u.shape, jnp....]
    reshape x1 -> x4, local copies, waits for them, and re-layouts: 0.83 us -> 12.5 us  [the longest x1 9.98 us: on_device(): noise = brownian.reshape(xs, groups, particles, xs, groups, particles)]
    all_to_all x2 -> x1, starting transfers between devices: 18.5 us -> 7.26 us  [on_device(): lax.all_to_all(copies, ('x', 'y'), split_axis=0, concat_axis=0, tiled=True)]
  transfers between devices with their start and end apart: 35 -> 2, of which waited for: 33 -> 1; matrix products, arithmetic and copies ran while one was open for 1% -> 11% of each run, Pallas kernels for 0% -> 10%
where the time goes in v1:
time: 140 us
  blocking collectives  62.9 us (45%)
  local copies, waits for them, and re-layouts  23.9 us (17%)
  Pallas kernels  23.1 us (16%)
  between operations  13.6 us (10%)
  starting transfers between devices  7.26 us (5%)
  waiting for transfers between devices  6.16 us (4%)
  other arithmetic  3.03 us (2%)
    all_to_all x1, blocking collectives, on_device(): whole = lax.all_to_all(sent, 'y', split_axis=0, concat_axis=0, tiled=True)  22.8 us
    pallas_call x1, Pallas kernels, darcy(): pl.pallas_call(darcy_kernel, out_shape=jax.ShapeDtypeStruct(u.shape, jnp....  14.4 us
    all_to_all x1, blocking collectives, on_device(): own = lax.all_to_all(chunks, 'x', split_axis=0, concat_axis=0, tiled=True)  13.7 us
    all_to_all x1, blocking collectives, on_device(): lax.all_to_all(moved, 'x', split_axis=0, concat_axis=0, tiled=True)  13.4 us
    all_to_all x1, blocking collectives, on_device(): lax.all_to_all(gradient, ('x', 'y'), split_axis=0, concat_axis=0, tiled=T...  13 us
    reshape x1, local copies, waits for them, and re-layouts, on_device(): noise = brownian.reshape(xs, groups, particles, xs, groups, particles)  9.98 us
    all_to_all x1, starting transfers between devices, on_device(): lax.all_to_all(copies, ('x', 'y'), split_axis=0, concat_axis=0, tiled=True)  7.26 us
    unnamed x15, local copies, waits for them, and re-layouts  7.09 us
  transfers between devices with their start and end apart: 2, of which 1 were waited for; matrix products, arithmetic and copies ran while one was open for 11% of the time, Pallas kernels for 10%

profile of v1, /device:TPU:8, one launch (start us, length us, event | category | flops | bytes accessed | tf_op | source)
XLA Modules:
  0.0 139.9 jit_solution(13622978951175435378)
XLA Ops:
  6.5 0.0 all-gather.2.cloned.1.call-start
  6.5 1.2 reshape.29
  7.8 0.3 copy.21
  8.1 0.0 copy-start.5
  8.2 0.0 copy-start.6
  8.2 13.7 %all_to_all.25 = f32[4,4,8192]{2,1,0:T(4,128)S(1)} all-to-all(f32[4,4,8192]{2,1,0:T(4,128)S(1)} %bitcast.28), channel_id=1, replica_groups=mesh['x'=4,'z'=8,'c'=2,'y'=4] {'x'}, dimensions={0} | all-to-all | bytes 1048576 | tf_op jit(solution)/shard_map/all_to_all | solution.py:213
  21.9 0.0 copy-start.3
  21.9 1.0 reshape.30.own_ref
  22.8 0.0 all-gather.2.cloned.1.call-update
  22.9 0.0 copy-done.5
  22.9 0.0 copy-done.6
  22.9 0.1 broadcast_in_dim.7
  23.0 0.0 copy-done.3
  23.0 0.2 pad_maximum_fusion
  23.2 22.8 %all_to_all.26 = f32[4,3,4,64,128]{4,3,2,1,0:T(8,128)S(1)} all-to-all(f32[4,3,4,64,128]{4,3,2,1,0:T(8,128)S(1)} %pad_maximum_fusion), channel_id=1, replica_groups=mesh['x'=4,'z'=8,'c'=2,'y'=4] {'y'}, dimensions={0} | all-to-all | bytes 3145728 | tf_op jit(solution)/shard_map/all_to_all | solution.py:222
  46.0 0.1 fusion
  46.1 14.4 %darcy.1 = f32[16,64,128]{2,1,0:T(8,128)S(1)} custom-call(f32[16,64,128]{2,1,0:T(8,128)S(1)} %bitcast.25, f32[16,64,128]{2,1,0:T(8,128)S(1)} %bitcast.24, f32[16,64,128]{2,1,0:T(8,128)S(1)} %bitcast.23), custom_call_target="tpu_custom_call" | custom-call | tf_op jit(solution)/shard_map/darcy/pallas_call | solution.py:120
  60.5 13.0 %all_to_all.27 = f32[16,64,128]{2,1,0:T(8,128)S(1)} all-to-all(f32[16,64,128]{2,1,0:T(8,128)S(1)} %darcy.1), channel_id=1, replica_groups=mesh['x'=4,'z'=8,'c'=2,'y'=4] {'x','y'}, dimensions={0} | all-to-all | bytes 1048576 | tf_op jit(solution)/shard_map/all_to_all | solution.py:225
  73.5 0.3 copy.20
  73.8 6.1 %all-gather.2.cloned.1.call-done.u_ref = f32[256,8192]{1,0:T(8,128)} async-done(((f32[16,8192]{1,0:T(8,128)}), f32[256,8192]{1,0:T(8,128)}) %all-gather.2.cloned.1.call-update) | async-done | bytes 8388624 | tf_op jit(solution)/shard_map/all_gather | solution.py:215
  80.0 0.0 copy-start
  80.0 3.4 %copy-done = f32[256,8192]{1,0:T(8,128)S(1)} copy-done((f32[256,8192]{1,0:T(8,128)S(1)}, f32[256,8192]{1,0:T(8,128)}, u32[]{:S(2)}) %copy-start) | copy-done | bytes 8388632
  83.3 0.0 copy-start.4
  83.3 4.3 %gram.1 = f32[16,256]{1,0:T(8,128)S(1)} custom-call(f32[256,8192]{1,0:T(8,128)S(1)} %copy-done, f32[16,8192]{1,0:T(8,128)S(1)} %bitcast.21), custom_call_target="tpu_custom_call" | custom-call | tf_op jit(solution)/shard_map/gram/pallas_call | solution.py:155
  87.7 0.8 broadcast_in_dim.8
  88.4 7.3 %all-to-all-start.3 = ((f32[16,16,256]{2,1,0:T(8,128)}), f32[16,16,256]{2,1,0:T(8,128)S(1)}, u32[]{:S(2)}, u32[]{:S(2)}) async-start(f32[16,16,256]{2,1,0:T(8,128)} %broadcast_in_dim.8), calls=%async_computation.3 | async-start | bytes 524288 | tf_op jit(solution)/shard_map/all_to_all | solution.py:236
  95.7 0.0 copy-done.4
  95.7 10.0 %reshape.32 = f32[4,16,4,4,16,4]{5,4,3,2,1,0:T(8,128)} reshape(f32[256,256]{1,0:T(8,128)S(1)} %copy-done.4) | data formatting | bytes 524288 | tf_op jit(solution)/shard_map/reshape | solution.py:229
  105.7 0.0 copy-start.2
  105.7 2.8 %dynamic-slice_multiply_fusion = f32[4,16,4,4,1,4]{5,4,3,2,1,0:T(1,128)S(1)} fusion(f32[4,16,4,4,16,4]{5,4,3,2,1,0:T(8,128)} %reshape.32, s32[]{:T(128)S(6)} %select_n.4), kind=kLoop, calls=%fused_computation.3 | loop fusion | flops 4096 | bytes 32772 | tf_op jit(solution)/shard_map/mul | solution.py:232
  108.5 2.0 %copy.15 = f32[4,4,16,4,4]{4,3,2,1,0:T(4,128)S(1)} copy(f32[4,4,16,4,4]{1,0,4,2,3:T(4,128)S(1)} %bitcast.27) | data formatting | bytes 32768 | tf_op jit(solution)/shard_map/mul | solution.py:232
  110.5 0.5 mul.31
  111.0 0.0 all-to-all-done.3
  111.0 0.0 copy-done.2
  111.0 0.0 copy-start.1
  111.1 3.4 %copy-done.1 = f32[256,8192]{1,0:T(8,128)S(1)} copy-done((f32[256,8192]{1,0:T(8,128)S(1)}, f32[256,8192]{1,0:T(8,128)}, u32[]{:S(2)}) %copy-start.1) | copy-done | bytes 8388632
  114.4 4.4 %move.1 = f32[16,64,128]{2,1,0:T(8,128)S(1)} custom-call(f32[256,8192]{1,0:T(8,128)S(1)} %copy-done.1, f32[16,8192]{1,0:T(8,128)S(1)} %copy-done.2, f32[16,256]{1,0:T(8,128)S(1)} %multiply_add_fusion.m_ref), custom_call_target="tpu_custom_call" | custom-call | tf_op jit(solution)/shard_map/move/pallas_call | solution.py:188
  118.8 13.4 %all_to_all.28 = f32[4,4,64,128]{3,2,1,0:T(8,128)S(1)} all-to-all(f32[4,4,64,128]{3,2,1,0:T(8,128)S(1)} %bitcast.22), channel_id=1, replica_groups=mesh['x'=4,'z'=8,'c'=2,'y'=4] {'x'}, dimensions={0} | all-to-all | bytes 1048576 | tf_op jit(solution)/shard_map/all_to_all | solution.py:240
  132.2 0.8 copy.16
  (3 shorter events, 0.0 us)
Async XLA Ops:
  6.5 73.4 %all-gather.2.cloned.1.call-start = ((), (), s32[]{:S(2)}) async-start(), calls=%async_computation.5 | async-start | bytes 8912896 | tf_op jit(solution)/shard_map/all_gather | solution.py:215
  8.1 14.7 %copy-start.5 = (f32[4,64,128]{2,1,0:T(8,128)S(1)}, f32[4,64,128]{2,1,0:T(8,128)}, u32[]{:S(2)}) copy-start(f32[4,64,128]{2,1,0:T(8,128)} %param.6) | copy-start | bytes 393220
  8.2 14.7 %copy-start.6 = (f32[4,64,128]{2,1,0:T(8,128)S(1)}, f32[4,64,128]{2,1,0:T(8,128)}, u32[]{:S(2)}) copy-start(f32[4,64,128]{2,1,0:T(8,128)} %param.5) | copy-start | bytes 393220
  21.9 1.2 copy-start.3
  80.0 3.4 %copy-start = (f32[256,8192]{1,0:T(8,128)S(1)}, f32[256,8192]{1,0:T(8,128)}, u32[]{:S(2)}) copy-start(f32[256,8192]{1,0:T(8,128)} %all-gather.2.cloned.1.call-done.u_ref) | copy-start | bytes 25165828
  83.3 12.3 %copy-start.4 = (f32[256,256]{1,0:T(8,128)S(1)}, f32[256,256]{1,0:T(8,128)}, u32[]{:S(2)}) copy-start(f32[256,256]{1,0:T(8,128)} %param.7) | copy-start | bytes 786436
  88.4 22.6 %all-to-all-start.3 = ((f32[16,16,256]{2,1,0:T(8,128)}), f32[16,16,256]{2,1,0:T(8,128)S(1)}, u32[]{:S(2)}, u32[]{:S(2)}) async-start(f32[16,16,256]{2,1,0:T(8,128)} %broadcast_in_dim.8), calls=%async_computation.3 | async-start | bytes 524288 | tf_op jit(solution)/shard_map/all_to_all | solution.py:236
  105.7 5.4 %copy-start.2 = (f32[16,8192]{1,0:T(8,128)S(1)}, f32[16,8192]{1,0:T(8,128)}, u32[]{:S(2)}) copy-start(f32[16,8192]{1,0:T(8,128)} %reshape.30.own_ref) | copy-start | bytes 1572868
  111.0 3.4 %copy-start.1 = (f32[256,8192]{1,0:T(8,128)S(1)}, f32[256,8192]{1,0:T(8,128)}, u32[]{:S(2)}) copy-start(f32[256,8192]{1,0:T(8,128)} %all-gather.2.cloned.1.call-done.u_ref) | copy-start | bytes 25165828
Sparse Core Ops, SparseCore 0:
  23.0 56.9 all-gather.1

commit v2 on v1

--- a/solution.py
+++ b/solution.py
@@ -132,72 +132,131 @@
     return high, low
 
 
-def gram_kernel(u_ref, g_ref, o_ref):
-    @pl.when(pl.program_id(0) == 0)
+def rows_of(ref, r):
+    members, groups, lanes = ref.shape
+    return ref.reshape(members * groups, lanes)[pl.ds(r, members, stride=groups), :]
+
+
+def flat(ref):
+    return jnp.concatenate([rows_of(ref, r) for r in range(ref.shape[1])], axis=1)
+
+
+def gram_kernel(u_ref, g_ref, o_ref, acc):
+    step = pl.program_id(0)
+
+    @pl.when(step == 0)
     def _():
-        o_ref[...] = jnp.zeros_like(o_ref)
+        acc[...] = jnp.zeros_like(acc)
 
     members = u_ref.shape[0]
     block = g_ref.shape[0]
-    u = u_ref[...]
+    u = flat(u_ref)
     s = u - jnp.sum(u, axis=0, keepdims=True) * (1.0 / members)
     s_high, s_low = split(s)
-    pair = jnp.concatenate(split(g_ref[...]), axis=0)
+    pair = jnp.concatenate(split(flat(g_ref)), axis=0)
     dims = (((1,), (1,)), ((), ()))
     out = lax.dot_general(pair, s_high, dims, preferred_element_type=jnp.float32)
     out = out + lax.dot_general(pair, s_low, dims, preferred_element_type=jnp.float32)
-    o_ref[...] += out[:block] + out[block:]
-
-
-def gram_product(u_all, g, tile):
-    members, cells = u_all.shape
+    acc[...] += out[:block] + out[block:]
+
+    @pl.when(step == pl.num_programs(0) - 1)
+    def _():
+        for d in range(o_ref.shape[0]):
+            o_ref[d] = acc[...]
+
+
+def gram_product(u_all, g, copies, groups):
+    members, rows, lanes = u_all.shape
     block = g.shape[0]
     return pl.pallas_call(
         gram_kernel,
-        grid=(cells // tile,),
+        grid=(rows // groups,),
         in_specs=[
-            pl.BlockSpec((members, tile), lambda i: (0, i)),
-            pl.BlockSpec((block, tile), lambda i: (0, i)),
+            pl.BlockSpec((members, groups, lanes), lambda i: (0, i, 0)),
+            pl.BlockSpec((block, groups, lanes), lambda i: (0, i, 0)),
         ],
-        out_specs=pl.BlockSpec((block, members), lambda i: (0, 0)),
-        out_shape=jax.ShapeDtypeStruct((block, members), jnp.float32),
+        out_specs=pl.BlockSpec((copies, block, members), lambda i: (0, 0, 0)),
+        out_shape=jax.ShapeDtypeStruct((copies, block, members), jnp.float32),
+        scratch_shapes=[pltpu.VMEM((block, members), jnp.float32)],
         compiler_params=pltpu.CompilerParams(vmem_limit_bytes=24 << 20),
         name="gram",
     )(u_all, g)
 
 
-def move_kernel(u_ref, own_ref, m_ref, o_ref):
+def move_kernel(u_ref, own_ref, parts_ref, noise_ref, o_ref, pair_s, *, scale):
+    @pl.when(pl.program_id(0) == 0)
+    def _():
+        total = parts_ref[0]
+        for d in range(1, parts_ref.shape[0]):
+            total = total + parts_ref[d]
+        pair_s[...] = jnp.concatenate(split(noise_ref[...] - scale * total), axis=0)
+
     members = u_ref.shape[0]
     block, groups, lanes = o_ref.shape
-    u = u_ref[...]
+    u = flat(u_ref)
     centre = jnp.sum(u, axis=0, keepdims=True) * (1.0 / members)
     s_high, s_low = split(u - centre)
-    pair = jnp.concatenate(split(m_ref[...]), axis=0)
     dims = (((1,), (0,)), ((), ()))
-    out = lax.dot_general(pair, s_high, dims, preferred_element_type=jnp.float32)
-    out = out + lax.dot_general(pair, s_low, dims, preferred_element_type=jnp.float32)
-    moved = centre + 1.25 * (own_ref[...] - centre) + (out[:block] + out[block:])
+    out = lax.dot_general(pair_s[...], s_high, dims, preferred_element_type=jnp.float32)
+    out = out + lax.dot_general(pair_s[...], s_low, dims, preferred_element_type=jnp.float32)
+    moved = centre + 1.25 * (flat(own_ref) - centre) + (out[:block] + out[block:])
+    rows = o_ref.reshape(block * groups, lanes)
     for r in range(groups):
-        o_ref[:, r, :] = moved[:, r * lanes : (r + 1) * lanes]
-
-
-def move(u_all, own, mixing, tile):
-    members, cells = u_all.shape
+        rows[pl.ds(r, block, stride=groups), :] = moved[:, r * lanes : (r + 1) * lanes]
+
+
+def move(u_all, own, parts, noise, scale, groups):
+    members, rows, lanes = u_all.shape
     block = own.shape[0]
-    lanes = 128
     return pl.pallas_call(
-        move_kernel,
-        grid=(cells // tile,),
+        lambda *refs: move_kernel(*refs, scale=scale),
+        grid=(rows // groups,),
         in_specs=[
-            pl.BlockSpec((members, tile), lambda i: (0, i)),
-            pl.BlockSpec((block, tile), lambda i: (0, i)),
-            pl.BlockSpec((block, members), lambda i: (0, 0)),
+            pl.BlockSpec((members, groups, lanes), lambda i: (0, i, 0)),
+            pl.BlockSpec((block, groups, lanes), lambda i: (0, i, 0)),
+            pl.BlockSpec(parts.shape, lambda i: (0, 0, 0)),
+            pl.BlockSpec(noise.shape, lambda i: (0, 0)),
         ],
-        out_specs=pl.BlockSpec((block, tile // lanes, lanes), lambda i: (0, i, 0)),
-        out_shape=jax.ShapeDtypeStruct((block, cells // lanes, lanes), jnp.float32),
+        out_specs=pl.BlockSpec((block, groups, lanes), lambda i: (0, i, 0)),
+        out_shape=jax.ShapeDtypeStruct((block, rows, lanes), jnp.float32),
+        scratch_shapes=[pltpu.VMEM((2 * block, members), jnp.bfloat16)],
         compiler_params=pltpu.CompilerParams(vmem_limit_bytes=24 << 20),
         name="move",
-    )(u_all, own, mixing)
+    )(u_all, own, parts, noise)
+
+
+def noise_kernel(at_ref, b_ref, o_ref, *, xs, groups, particles, scale):
+    block, members = o_ref.shape
+    per_x = groups * particles
+    t = lax.broadcasted_iota(jnp.int32, (block, members), 0)
+    j = lax.broadcasted_iota(jnp.int32, (block, members), 1)
+    column = (t // particles) * per_x + at_ref[0] * particles + t % particles
+    chosen = jnp.where(j == column, scale, 0.0)
+    k = lax.broadcasted_iota(jnp.int32, (members, members), 0)
+    m = lax.broadcasted_iota(jnp.int32, (members, members), 1)
+    row = ((m // particles) % xs) * per_x + (m // (xs * particles)) * particles + m % particles
+    order = jnp.where(k == row, 1.0, 0.0)
+    picked = lax.dot_general(
+        chosen, b_ref[...], (((1,), (1,)), ((), ())),
+        precision=lax.Precision.HIGHEST, preferred_element_type=jnp.float32,
+    )
+    o_ref[...] = lax.dot_general(
+        picked, order, (((1,), (0,)), ((), ())),
+        precision=lax.Precision.HIGHEST, preferred_element_type=jnp.float32,
+    )
+
+
+def ordered_noise(brownian, at, xs, groups, particles, scale):
+    return pl.pallas_call(
+        lambda *refs: noise_kernel(*refs, xs=xs, groups=groups, particles=particles, scale=scale),
+        in_specs=[
+            pl.BlockSpec(memory_space=pltpu.SMEM),
+            pl.BlockSpec(memory_space=pltpu.VMEM),
+        ],
+        out_shape=jax.ShapeDtypeStruct((xs * particles, brownian.shape[0]), jnp.float32),
+        compiler_params=pltpu.CompilerParams(vmem_limit_bytes=24 << 20),
+        name="noise",
+    )(at.reshape(1), brownian)
 
 
 def on_device(logperm, source, observed, brownian):
@@ -209,33 +268,31 @@
     layer = rows * lanes
     cells = width * slabs * layer
 
-    chunks = jnp.swapaxes(logperm.reshape(particles, width, layer), 0, 1)
+    chunks = jnp.swapaxes(logperm, 0, 1)
     own = lax.all_to_all(chunks, "x", split_axis=0, concat_axis=0, tiled=True)
-    own = own.reshape(xs * particles, layer)
+    own = own.reshape(xs * particles, rows, lanes)
     u_all = lax.all_gather(own, ("z", "c"), axis=0, tiled=True)
-
-    own_now, logperm_now = lax.optimization_barrier((own, logperm))
+    u_all = pltpu.with_memory_space_constraint(u_all, pltpu.HBM)
+
+    own, logperm = lax.optimization_barrier((own, logperm))
     shared = jnp.stack([source, observed])
     sent = jnp.concatenate(
-        [logperm_now[:, None], jnp.broadcast_to(shared[None], (particles,) + shared.shape)], axis=1
+        [logperm[:, None], jnp.broadcast_to(shared[None], (particles,) + shared.shape)], axis=1
     )
     whole = lax.all_to_all(sent, "y", split_axis=0, concat_axis=0, tiled=True)
     whole = jnp.swapaxes(whole, 0, 1).reshape(3, slabs * width, rows, lanes)
     gradient = darcy(whole[0], whole[1], whole[2])
     g = lax.all_to_all(gradient, ("x", "y"), split_axis=0, concat_axis=0, tiled=True)
-    g = g.reshape(xs * particles, layer)
 
     step_size = ensemble / (4.0 * (cells + 1))
-    noise = brownian.reshape(xs, groups, particles, xs, groups, particles)
-    noise = lax.dynamic_index_in_dim(noise, lax.axis_index(("z", "c")), axis=4, keepdims=False)
-    noise = jnp.transpose(noise, (3, 4, 1, 0, 2)).reshape(xs * particles, ensemble)
-    noise = math.sqrt(2.0 * step_size / ensemble) * noise
-
-    part = gram_product(u_all, g, 1024)
-    copies = jnp.broadcast_to(part[None], (xs * slabs,) + part.shape)
-    gram = jnp.sum(lax.all_to_all(copies, ("x", "y"), split_axis=0, concat_axis=0, tiled=True), axis=0)
-    mixing = -(step_size / ensemble) * gram + noise
-    moved = move(u_all, own_now, mixing, 1024)
+    at = lax.axis_index(("z", "c"))
+    noise_scale = math.sqrt(2.0 * step_size / ensemble)
+    noise = ordered_noise(brownian, at, xs, groups, particles, noise_scale)
+    g, noise = lax.optimization_barrier((g, noise))
+
+    parts = gram_product(u_all, g, xs * slabs, 8)
+    parts = lax.all_to_all(parts, ("x", "y"), split_axis=0, concat_axis=0, tiled=True)
+    moved = move(u_all, own, parts, noise, step_size / ensemble, 8)
     moved = moved.reshape(xs, particles, rows, lanes)
     returned = lax.all_to_all(moved, "x", split_axis=0, concat_axis=0, tiled=True)
     return jnp.swapaxes(returned, 0, 1)

time: 140 us -> 128 us (0.914)
  local copies, waits for them, and re-layouts: 23.9 us -> 2.19 us
  Pallas kernels: 23.1 us -> 31.7 us
  waiting for transfers between devices: 6.16 us -> 13.1 us
  other arithmetic: 3.03 us -> 0.17 us
  starting transfers between devices: 7.26 us -> 4.83 us
    reshape x4 -> x0, local copies, waits for them, and re-layouts: 12.5 us -> none  [the longest x1 9.98 us: on_device(): noise = brownian.reshape(xs, groups, particles, xs, groups, particles)]
    all_to_all x1, waiting for transfers between devices: 0.01 us -> 8.08 us  [on_device(): lax.all_to_all(gradient, ('x', 'y'), split_axis=0, concat_axis=0, tiled=T...]
    pallas_call x2 -> x3, Pallas kernels: 8.72 us -> 16.5 us  [the longest x1 7.99 us: move(): pl.pallas_call(lambda *refs: move_kernel(*refs, scale=scale), grid=(rows...]
    unnamed x15 -> x11, local copies, waits for them, and re-layouts: 7.09 us -> 1.14 us
    mul x1 -> x0, other arithmetic: 2.83 us -> none  [on_device(): noise = math.sqrt(2.0 * step_size / ensemble) * noise]
    mul x2 -> x0, local copies, waits for them, and re-layouts: 2.47 us -> none  [on_device(): noise = math.sqrt(2.0 * step_size / ensemble) * noise]
    all_to_all x1, starting transfers between devices: 7.26 us -> 4.82 us  [on_device(): lax.all_to_all(gradient, ('x', 'y'), split_axis=0, concat_axis=0, tiled=T...]
    all_to_all x1, blocking collectives: 13.4 us -> 11.2 us  [on_device(): lax.all_to_all(moved, 'x', split_axis=0, concat_axis=0, tiled=True)]
  transfers between devices with their start and end apart: 2 -> 2, of which waited for: 1 -> 2; matrix products, arithmetic and copies ran while one was open for 11% -> 0% of each run, Pallas kernels for 10% -> 12%
where the time goes in v2:
time: 128 us
  blocking collectives  62.3 us (49%)
  Pallas kernels  31.7 us (25%)
  between operations  13.5 us (11%)
  waiting for transfers between devices  13.1 us (10%)
  starting transfers between devices  4.83 us (4%)
  local copies, waits for them, and re-layouts  2.19 us (2%)
    all_to_all x1, blocking collectives, on_device(): whole = lax.all_to_all(sent, 'y', split_axis=0, concat_axis=0, tiled=True)  22.8 us
    pallas_call x1, Pallas kernels, darcy(): pl.pallas_call(darcy_kernel, out_shape=jax.ShapeDtypeStruct(u.shape, jnp....  15.2 us
    all_to_all x1, blocking collectives, on_device(): lax.all_to_all(parts, ('x', 'y'), split_axis=0, concat_axis=0, tiled=True)  14.4 us
    all_to_all x1, blocking collectives, on_device(): own = lax.all_to_all(chunks, 'x', split_axis=0, concat_axis=0, tiled=True)  13.8 us
    all_to_all x1, blocking collectives, on_device(): lax.all_to_all(moved, 'x', split_axis=0, concat_axis=0, tiled=True)  11.2 us
    all_to_all x1, waiting for transfers between devices, on_device(): lax.all_to_all(gradient, ('x', 'y'), split_axis=0, concat_axis=0, tiled=T...  8.08 us
    pallas_call x1, Pallas kernels, move(): pl.pallas_call(lambda *refs: move_kernel(*refs, scale=scale), grid=(rows...  7.99 us
    pallas_call x1, Pallas kernels, gram_product(): pl.pallas_call(gram_kernel, grid=(rows // groups,), in_specs=[pl.BlockSpe...  7.76 us
  transfers between devices with their start and end apart: 2, of which 2 were waited for; matrix products, arithmetic and copies ran while one was open for 0% of the time, Pallas kernels for 12%

profile of v2, /device:TPU:8, one launch (start us, length us, event | category | flops | bytes accessed | tf_op | source)
XLA Modules:
  0.0 127.7 jit_solution(18072350989662071084)
XLA Ops:
  6.5 0.0 copy-start.4
  6.5 0.0 copy-start.3
  6.5 0.0 all-gather.2.cloned.1.call-start
  6.5 1.1 copy.10
  7.7 0.0 copy-start.2
  7.7 13.8 %all_to_all.25 = f32[4,4,64,128]{3,2,1,0:T(8,128)} all-to-all(f32[4,4,64,128]{3,2,1,0:T(8,128)S(1)} %bitcast.22), channel_id=1, replica_groups=mesh['x'=4,'z'=8,'c'=2,'y'=4] {'x'}, dimensions={0} | all-to-all | bytes 1048576 | tf_op jit(solution)/shard_map/all_to_all | solution.py:272
  21.5 0.0 all-gather.2.cloned.1.call-update
  21.5 0.0 copy-done.4
  21.5 0.0 copy-done.3
  21.6 0.1 broadcast_in_dim.10
  21.7 0.0 copy-done.2
  21.7 0.2 pad_maximum_fusion
  21.8 22.8 %all_to_all.26 = f32[4,3,4,64,128]{4,3,2,1,0:T(8,128)S(1)} all-to-all(f32[4,3,4,64,128]{4,3,2,1,0:T(8,128)S(1)} %pad_maximum_fusion), channel_id=1, replica_groups=mesh['x'=4,'z'=8,'c'=2,'y'=4] {'y'}, dimensions={0} | all-to-all | bytes 3145728 | tf_op jit(solution)/shard_map/all_to_all | solution.py:282
  44.6 0.1 fusion
  44.7 0.0 copy-start.1
  44.7 15.2 %darcy.1 = f32[16,64,128]{2,1,0:T(8,128)} custom-call(f32[16,64,128]{2,1,0:T(8,128)S(1)} %bitcast.19, f32[16,64,128]{2,1,0:T(8,128)S(1)} %bitcast.18, f32[16,64,128]{2,1,0:T(8,128)S(1)} %bitcast.17), custom_call_target="tpu_custom_call" | custom-call | tf_op jit(solution)/shard_map/darcy/pallas_call | solution.py:120
  59.9 4.8 %all-to-all-start.2 = ((f32[16,64,128]{2,1,0:T(8,128)}), f32[16,64,128]{2,1,0:T(8,128)S(1)}, u32[]{:S(2)}, u32[]{:S(2)}) async-start(f32[16,64,128]{2,1,0:T(8,128)} %darcy.1), calls=%async_computation.2 | async-start | bytes 1048576 | tf_op jit(solution)/shard_map/all_to_all | solution.py:285
  64.7 0.0 copy-done.1
  64.7 0.7 noise.1.refs_3_
  65.5 0.0 copy-start
  65.5 8.1 %all-to-all-done.2.g_ref = f32[16,64,128]{2,1,0:T(8,128)S(1)} async-done(((f32[16,64,128]{2,1,0:T(8,128)}), f32[16,64,128]{2,1,0:T(8,128)S(1)}, u32[]{:S(2)}, u32[]{:S(2)}) %all-to-all-start.2) | async-done | bytes 524320 | tf_op jit(solution)/shard_map/all_to_all | solution.py:285
  73.5 5.1 %all-gather.2.cloned.1.call-done.u_ref.refs_0_ = f32[256,64,128]{2,1,0:T(8,128)} async-done(((f32[16,64,128]{2,1,0:T(8,128)}), f32[256,64,128]{2,1,0:T(8,128)}) %all-gather.2.cloned.1.call-update) | async-done | bytes 8388624 | tf_op jit(solution)/shard_map/all_gather | solution.py:274
  78.6 7.8 %gram.1 = f32[16,16,256]{2,1,0:T(8,128)S(1)} custom-call(f32[256,64,128]{2,1,0:T(8,128)} %all-gather.2.cloned.1.call-done.u_ref.refs_0_, f32[16,64,128]{2,1,0:T(8,128)S(1)} %all-to-all-done.2.g_ref), custom_call_target="tpu_custom_call" | custom-call | tf_op jit(solution)/shard_map/gram/pallas_call | solution.py:171
  86.4 14.4 %all_to_all.27.refs_2_ = f32[16,16,256]{2,1,0:T(8,128)S(1)} all-to-all(f32[16,16,256]{2,1,0:T(8,128)S(1)} %gram.1), channel_id=1, replica_groups=mesh['x'=4,'z'=8,'c'=2,'y'=4] {'x','y'}, dimensions={0} | all-to-all | bytes 524288 | tf_op jit(solution)/shard_map/all_to_all | solution.py:294
  100.8 0.0 copy-done
  100.8 8.0 %move.1 = f32[16,64,128]{2,1,0:T(8,128)S(1)} custom-call(f32[256,64,128]{2,1,0:T(8,128)} %all-gather.2.cloned.1.call-done.u_ref.refs_0_, f32[16,64,128]{2,1,0:T(8,128)S(1)} %bitcast.15, f32[16,16,256]{2,1,0:T(8,128)S(1)} %all_to_all.27.refs_2_, f32[16,256]{1,0:T(8,128)S(1)} %noise.1.refs_3_), custom_call_target="tpu_custom_call" | custom-call | tf_op jit(solution)/shard_map/move/pallas_call | solution.py:211
  108.8 11.2 %all_to_all.28 = f32[4,4,64,128]{3,2,1,0:T(8,128)S(1)} all-to-all(f32[4,4,64,128]{3,2,1,0:T(8,128)S(1)} %bitcast.16), channel_id=1, replica_groups=mesh['x'=4,'z'=8,'c'=2,'y'=4] {'x'}, dimensions={0} | all-to-all | bytes 1048576 | tf_op jit(solution)/shard_map/all_to_all | solution.py:297
  120.0 0.8 copy.8
  (1 shorter events, 0.0 us)
Async XLA Ops:
  6.5 15.0 %copy-start.4 = (f32[4,64,128]{2,1,0:T(8,128)S(1)}, f32[4,64,128]{2,1,0:T(8,128)}, u32[]{:S(2)}) copy-start(f32[4,64,128]{2,1,0:T(8,128)} %param.5) | copy-start | bytes 393220
  6.5 15.0 %copy-start.3 = (f32[4,64,128]{2,1,0:T(8,128)S(1)}, f32[4,64,128]{2,1,0:T(8,128)}, u32[]{:S(2)}) copy-start(f32[4,64,128]{2,1,0:T(8,128)} %param.6) | copy-start | bytes 393220
  6.5 72.1 %all-gather.2.cloned.1.call-start = ((), (), s32[]{:S(2)}) async-start(), calls=%async_computation.5 | async-start | bytes 8912896 | tf_op jit(solution)/shard_map/all_gather | solution.py:274
  7.7 14.0 %copy-start.2 = (f32[4,4,64,128]{3,2,1,0:T(8,128)S(1)}, f32[4,4,64,128]{3,2,1,0:T(8,128)}, u32[]{:S(2)}) copy-start(f32[4,4,64,128]{3,2,1,0:T(8,128)} %param.4) | copy-start | bytes 1572868
  44.7 20.0 %copy-start.1 = (f32[256,256]{1,0:T(8,128)S(1)}, f32[256,256]{1,0:T(8,128)}, u32[]{:S(2)}) copy-start(f32[256,256]{1,0:T(8,128)} %refs_1_.1) | copy-start | bytes 786436
  59.9 13.6 %all-to-all-start.2 = ((f32[16,64,128]{2,1,0:T(8,128)}), f32[16,64,128]{2,1,0:T(8,128)S(1)}, u32[]{:S(2)}, u32[]{:S(2)}) async-start(f32[16,64,128]{2,1,0:T(8,128)} %darcy.1), calls=%async_computation.2 | async-start | bytes 1048576 | tf_op jit(solution)/shard_map/all_to_all | solution.py:285
  65.5 35.3 %copy-start = (f32[4,4,64,128]{3,2,1,0:T(8,128)S(1)}, f32[4,4,64,128]{3,2,1,0:T(8,128)}, u32[]{:S(2)}) copy-start(f32[4,4,64,128]{3,2,1,0:T(8,128)} %all_to_all.25) | copy-start | bytes 1572868
Sparse Core Ops, SparseCore 0:
  21.6 56.9 all-gather.1

commit v3 on v1

v3 whole, which is shorter than its diff:
```python
import math

import jax
import jax.numpy as jnp
from jax import lax
from jax.experimental import pallas as pl
from jax.experimental.pallas import tpu as pltpu
from jax.sharding import Mesh
from jax.sharding import PartitionSpec as P

SWEEPS = 8
MISFIT_WEIGHT = 1000.0
PAD = 8
SPREAD_AXIS = "x"
GATHER_AXES = ("z", "c")
VMEM_LIMIT = 32 << 20


def member(group, spot, particle):
    if SPREAD_AXIS == "x":
        return spot * 64 + group * 4 + particle
    return (group // 2) * 64 + spot * 8 + (group % 2) * 4 + particle


def darcy_kernel(
    y_ref, u_ref, src_ref, obs_ref, r1_ref, r2_ref, r3_ref, g_ref,
    e_s, w0, w1, p_s, inv_s, b_s, a_s, src_s, obs_s,
):
    slabs, width, rows, lanes = u_ref.shape
    layers = slabs * width
    lane = lax.broadcasted_iota(jnp.int32, (rows, lanes), 1)
    first = lane == 0
    last = lane == lanes - 1
    mid = pl.ds(PAD, rows)
    up = pl.ds(PAD - 1, rows)
    down = pl.ds(PAD + 1, rows)

    def before(v, fill):
        return jnp.where(first, fill, pltpu.roll(v, 1, 1))

    def after(v, fill):
        return jnp.where(last, fill, pltpu.roll(v, lanes - 1, 1))

    def neighbors(ref, i, fill):
        core = ref[i + 1, mid, :]
        return (
            (ref[i, mid, :] + ref[i + 2, mid, :])
            + (ref[i + 1, up, :] + ref[i + 1, down, :])
            + (before(core, fill) + after(core, fill))
        )

    for ref, fill in ((e_s, 1.0), (w0, 0.0), (w1, 0.0), (p_s, 0.0)):
        ref[:, :PAD, :] = jnp.full((layers + 2, PAD, lanes), fill, jnp.float32)
        ref[:, PAD + rows :, :] = jnp.full((layers + 2, PAD, lanes), fill, jnp.float32)
        for outside in (0, layers + 1):
            ref[outside, mid, :] = jnp.full((rows, lanes), fill, jnp.float32)

    y = y_ref[0]
    for w in range(width):
        e_s[y * width + w + 1, mid, :] = jnp.exp(0.5 * u_ref[y, w])
        src_s[y * width + w] = src_ref[w]
        obs_s[y * width + w] = obs_ref[w]
    for shift, ref in ((1, r1_ref), (2, r2_ref), (3, r3_ref)):
        slab = lax.rem(y + slabs - shift, slabs)
        for w in range(width):
            e_s[slab * width + w + 1, mid, :] = jnp.exp(0.5 * ref[0, w])
            src_s[slab * width + w] = ref[1, w]
            obs_s[slab * width + w] = ref[2, w]

    for i in range(layers):
        inverse = 1.0 / neighbors(e_s, i, 1.0)
        inv_s[i] = inverse
        b_s[i] = inverse * e_s[i + 1, mid, :]
        start = inverse * src_s[i]
        a_s[i] = start
        w0[i + 1, mid, :] = start

    def sweep(now, new):
        for i in range(layers):
            new[i + 1, mid, :] = a_s[i] + b_s[i] * neighbors(now, i, 0.0)

    def relax():
        def two(_, carry):
            sweep(w0, w1)
            sweep(w1, w0)
            return carry

        lax.fori_loop(0, (SWEEPS - 1) // 2, two, 0)
        sweep(w0, w1)

    relax()
    for i in range(layers):
        pressure = w1[i + 1, mid, :] / e_s[i + 1, mid, :]
        p_s[i + 1, mid, :] = pressure
        start = inv_s[i] * (MISFIT_WEIGHT * (pressure - obs_s[i]))
        a_s[i] = start
        w0[i + 1, mid, :] = start
    relax()
    for i in range(layers):
        w1[i + 1, mid, :] = w1[i + 1, mid, :] / e_s[i + 1, mid, :]

    chunk = g_ref.shape[1]
    per_layer = rows // chunk
    for i in range(layers):
        e = e_s[i + 1, mid, :]
        p = p_s[i + 1, mid, :]
        q = w1[i + 1, mid, :]
        total = None
        for at, where in ((i, mid), (i + 2, mid), (i + 1, up), (i + 1, down)):
            term = e_s[at, where, :] * (p - p_s[at, where, :]) * (q - w1[at, where, :])
            total = term if total is None else total + term
        for shift in (before, after):
            total = total + shift(e, 1.0) * (p - shift(p, 0.0)) * (q - shift(q, 0.0))
        gradient = -0.5 * e * total
        for h in range(per_layer):
            spot = (i % width) * per_layer + h
            g_ref[spot * slabs + i // width] = gradient[h * chunk : (h + 1) * chunk]


def darcy(y, u, source, observed, received, chunk):
    slabs, width, rows, lanes = u.shape
    layers = slabs * width
    padded = pltpu.VMEM((layers + 2, rows + 2 * PAD, lanes), jnp.float32)
    plain = pltpu.VMEM((layers, rows, lanes), jnp.float32)
    whole = pl.BlockSpec(memory_space=pltpu.VMEM)
    return pl.pallas_call(
        darcy_kernel,
        in_specs=[pl.BlockSpec(memory_space=pltpu.SMEM)] + [whole] * 6,
        out_specs=whole,
        out_shape=jax.ShapeDtypeStruct((layers * rows // chunk, chunk, lanes), jnp.float32),
        scratch_shapes=[padded] * 4 + [plain] * 5,
        compiler_params=pltpu.CompilerParams(vmem_limit_bytes=VMEM_LIMIT),
        name="darcy",
    )(y.reshape(1), u, source, observed, *received)


def split(v):
    high = v.astype(jnp.bfloat16)
    low = (v - high.astype(jnp.float32)).astype(jnp.bfloat16)
    return high, low


def gram_kernel(u_ref, g_ref, o_ref):
    @pl.when(pl.program_id(0) == 0)
    def _():
        o_ref[...] = jnp.zeros_like(o_ref)

    members = u_ref.shape[0]
    block = g_ref.shape[0]
    u = u_ref[...]
    s = u - jnp.sum(u, axis=0, keepdims=True) * (1.0 / members)
    s_high, s_low = split(s)
    pair = jnp.concatenate(split(g_ref[...]), axis=0)
    dims = (((1,), (1,)), ((), ()))
    out = lax.dot_general(pair, s_high, dims, preferred_element_type=jnp.float32)
    out = out + lax.dot_general(pair, s_low, dims, preferred_element_type=jnp.float32)
    o_ref[...] += out[:block] + out[block:]


def gram_product(u_all, g, tile):
    members, cells = u_all.shape
    block = g.shape[0]
    return pl.pallas_call(
        gram_kernel,
        grid=(cells // tile,),
        in_specs=[
            pl.BlockSpec((members, tile), lambda i: (0, i)),
            pl.BlockSpec((block, tile), lambda i: (0, i)),
        ],
        out_specs=pl.BlockSpec((block, members), lambda i: (0, 0)),
        out_shape=jax.ShapeDtypeStruct((block, members), jnp.float32),
        compiler_params=pltpu.CompilerParams(vmem_limit_bytes=VMEM_LIMIT),
        name="gram",
    )(u_all, g)


def move_kernel(u_ref, own_ref, parts_ref, noise_ref, o_ref, pair_s, *, scale):
    @pl.when(pl.program_id(0) == 0)
    def _():
        total = parts_ref[0]
        for d in range(1, parts_ref.shape[0]):
            total = total + parts_ref[d]
        pair_s[...] = jnp.concatenate(split(noise_ref[...] - scale * total), axis=0)

    members = u_ref.shape[0]
    block, groups, lanes = o_ref.shape
    u = u_ref[...]
    centre = jnp.sum(u, axis=0, keepdims=True) * (1.0 / members)
    s_high, s_low = split(u - centre)
    dims = (((1,), (0,)), ((), ()))
    out = lax.dot_general(pair_s[...], s_high, dims, preferred_element_type=jnp.float32)
    out = out + lax.dot_general(pair_s[...], s_low, dims, preferred_element_type=jnp.float32)
    moved = centre + 1.25 * (own_ref[...] - centre) + (out[:block] + out[block:])
    for r in range(groups):
        o_ref[:, r, :] = moved[:, r * lanes : (r + 1) * lanes]


def move(u_all, own, parts, noise, scale, tile):
    members, cells = u_all.shape
    block = own.shape[0]
    lanes = 128
    return pl.pallas_call(
        lambda *refs: move_kernel(*refs, scale=scale),
        grid=(cells // tile,),
        in_specs=[
            pl.BlockSpec((members, tile), lambda i: (0, i)),
            pl.BlockSpec((block, tile), lambda i: (0, i)),
            pl.BlockSpec(parts.shape, lambda i: (0, 0, 0)),
            pl.BlockSpec(noise.shape, lambda i: (0, 0)),
        ],
        out_specs=pl.BlockSpec((block, tile // lanes, lanes), lambda i: (0, i, 0)),
        out_shape=jax.ShapeDtypeStruct((block, cells // lanes, lanes), jnp.float32),
        scratch_shapes=[pltpu.VMEM((2 * block, members), jnp.bfloat16)],
        compiler_params=pltpu.CompilerParams(vmem_limit_bytes=VMEM_LIMIT),
        name="move",
    )(u_all, own, parts, noise)


def noise_kernel(at_ref, b_ref, o_ref, *, spots, particles, scale):
    block, members = o_ref.shape
    t = lax.broadcasted_iota(jnp.int32, (block, members), 0)
    j = lax.broadcasted_iota(jnp.int32, (block, members), 1)
    column = member(at_ref[0], t // particles, t % particles)
    chosen = jnp.where(j == column, scale, 0.0)
    k = lax.broadcasted_iota(jnp.int32, (members, members), 0)
    m = lax.broadcasted_iota(jnp.int32, (members, members), 1)
    row = member(m // (spots * particles), (m // particles) % spots, m % particles)
    order = jnp.where(k == row, 1.0, 0.0)
    picked = lax.dot_general(
        chosen, b_ref[...], (((1,), (1,)), ((), ())),
        precision=lax.Precision.HIGHEST, preferred_element_type=jnp.float32,
    )
    o_ref[...] = lax.dot_general(
        picked, order, (((1,), (0,)), ((), ())),
        precision=lax.Precision.HIGHEST, preferred_element_type=jnp.float32,
    )


def ordered_noise(brownian, at, spots, particles, scale):
    return pl.pallas_call(
        lambda *refs: noise_kernel(*refs, spots=spots, particles=particles, scale=scale),
        in_specs=[
            pl.BlockSpec(memory_space=pltpu.SMEM),
            pl.BlockSpec(memory_space=pltpu.VMEM),
        ],
        out_shape=jax.ShapeDtypeStruct((spots * particles, brownian.shape[0]), jnp.float32),
        compiler_params=pltpu.CompilerParams(vmem_limit_bytes=VMEM_LIMIT),
        name="noise",
    )(at.reshape(1), brownian)


def shifted(block, axis, shift):
    count = lax.axis_size(axis)
    return lax.ppermute(block, axis, [(i, (i + shift) % count) for i in range(count)])


def on_device(logperm, source, observed, brownian):
    particles, width, rows, lanes = logperm.shape
    slabs = lax.axis_size("y")
    spots = lax.axis_size(SPREAD_AXIS)
    ensemble = particles * spots * lax.axis_size(GATHER_AXES)
    chunk = width * rows // spots
    cells = width * slabs * rows * lanes

    y = lax.axis_index("y")
    fields = jnp.stack([source, observed])
    received = []
    for shift in range(1, slabs):
        mine = lax.dynamic_slice_in_dim(logperm, (y + shift) % slabs, 1, axis=0)
        received.append(shifted(jnp.concatenate([mine, fields], axis=0), "y", shift))

    chunks = jnp.swapaxes(logperm.reshape(particles, spots, chunk, lanes), 0, 1)
    own = lax.all_to_all(chunks, SPREAD_AXIS, split_axis=0, concat_axis=0, tiled=True)
    own = own.reshape(spots * particles, chunk * lanes)
    u_all = lax.all_gather(own, GATHER_AXES, axis=0, tiled=True)
    u_all = pltpu.with_memory_space_constraint(u_all, pltpu.HBM)

    gradient = darcy(y, logperm, source, observed, received, chunk)
    g = lax.all_to_all(gradient, (SPREAD_AXIS, "y"), split_axis=0, concat_axis=0, tiled=True)
    g = g.reshape(spots * particles, chunk * lanes)

    step_size = ensemble / (4.0 * (cells + 1))
    noise_scale = math.sqrt(2.0 * step_size / ensemble)
    noise = ordered_noise(brownian, lax.axis_index(GATHER_AXES), spots, particles, noise_scale)
    g, noise = lax.optimization_barrier((g, noise))

    tile = chunk * lanes // 2
    part = gram_product(u_all, g, tile)
    parts = jnp.broadcast_to(part[None], (spots * slabs,) + part.shape)
    parts = lax.all_to_all(parts, (SPREAD_AXIS, "y"), split_axis=0, concat_axis=0, tiled=True)
    moved = move(u_all, own, parts, noise, step_size / ensemble, tile)
    moved = moved.reshape(spots, particles, chunk, lanes)
    returned = lax.all_to_all(moved, SPREAD_AXIS, split_axis=0, concat_axis=0, tiled=True)
    return jnp.swapaxes(returned, 0, 1).reshape(logperm.shape)


def solution(mesh):
    fine = Mesh(mesh.devices.reshape(4, 8, 2, 4), ("x", "z", "c", "y"))
    dom = ("x", "z", "c")
    return jax.shard_map(
        on_device,
        mesh=fine,
        in_specs=(P(dom, "y", None, None), P("y", None, None), P("y", None, None), P()),
        out_specs=P(dom, "y", None, None),
        check_vma=False,
    )
```

time: 140 us -> 123 us (0.88)
  waiting for transfers between devices: 6.16 us -> 34.2 us
  blocking collectives: 62.9 us -> 39.2 us
  local copies, waits for them, and re-layouts: 23.9 us -> 7.33 us
  Pallas kernels: 23.1 us -> 17.2 us
  starting transfers between devices: 7.26 us -> 10.3 us
  other arithmetic: 3.03 us -> 1.13 us
    all_to_all x4 -> x3, blocking collectives: 62.9 us -> 39.2 us  [the longest x1 14.4 us: on_device(): lax.all_to_all(parts, (SPREAD_AXIS, 'y'), split_axis=0, concat_axis=0, ti...]
    ppermute x0 -> x3, waiting for transfers between devices: none -> 15.3 us  [shifted(): lax.ppermute(block, axis, [(i, (i + shift) % count) for i in range(count)])]
    reshape x4 -> x0, local copies, waits for them, and re-layouts: 12.5 us -> none  [the longest x1 9.98 us: on_device(): noise = brownian.reshape(xs, groups, particles, xs, groups, particles)]
    all_to_all x1, waiting for transfers between devices: 0.01 us -> 9.23 us  [on_device(): lax.all_to_all(gradient, (SPREAD_AXIS, 'y'), split_axis=0, concat_axis=0,...]
    pallas_call x2 -> x3, Pallas kernels: 18.8 us -> 12.3 us  [the longest x1 6.47 us: darcy(): pl.pallas_call(darcy_kernel, in_specs=[pl.BlockSpec(memory_space=pltpu.SM...]
    ppermute x0 -> x3, starting transfers between devices: none -> 5 us  [shifted(): lax.ppermute(block, axis, [(i, (i + shift) % count) for i in range(count)])]
    all_gather x1, waiting for transfers between devices: 6.14 us -> 9.63 us  [on_device(): u_all = lax.all_gather(own, GATHER_AXES, axis=0, tiled=True)]
    mul x1 -> x0, other arithmetic: 2.83 us -> none  [on_device(): noise = math.sqrt(2.0 * step_size / ensemble) * noise]
  transfers between devices with their start and end apart: 2 -> 5, of which waited for: 1 -> 5; matrix products, arithmetic and copies ran while one was open for 11% -> 2% of each run, Pallas kernels for 10% -> 6%
where the time goes in v3:
time: 123 us
  blocking collectives  39.2 us (32%)
  waiting for transfers between devices  34.2 us (28%)
  Pallas kernels  17.2 us (14%)
  between operations  13.5 us (11%)
  starting transfers between devices  10.3 us (8%)
  local copies, waits for them, and re-layouts  7.33 us (6%)
    ppermute x3, waiting for transfers between devices, shifted(): lax.ppermute(block, axis, [(i, (i + shift) % count) for i in range(count)])  15.3 us
    all_to_all x1, blocking collectives, on_device(): lax.all_to_all(parts, (SPREAD_AXIS, 'y'), split_axis=0, concat_axis=0, ti...  14.4 us
    all_to_all x1, blocking collectives, on_device(): lax.all_to_all(chunks, SPREAD_AXIS, split_axis=0, concat_axis=0, tiled=True)  13.6 us
    all_to_all x1, blocking collectives, on_device(): lax.all_to_all(moved, SPREAD_AXIS, split_axis=0, concat_axis=0, tiled=True)  11.2 us
    all_gather x1, waiting for transfers between devices, on_device(): u_all = lax.all_gather(own, GATHER_AXES, axis=0, tiled=True)  9.63 us
    all_to_all x1, waiting for transfers between devices, on_device(): lax.all_to_all(gradient, (SPREAD_AXIS, 'y'), split_axis=0, concat_axis=0,...  9.23 us
    pallas_call x1, Pallas kernels, darcy(): pl.pallas_call(darcy_kernel, in_specs=[pl.BlockSpec(memory_space=pltpu.SM...  6.47 us
    unnamed x13, local copies, waits for them, and re-layouts  5.4 us
  transfers between devices with their start and end apart: 5, of which 5 were waited for; matrix products, arithmetic and copies ran while one was open for 2% of the time, Pallas kernels for 6%

profile of v3, /device:TPU:8, one launch (start us, length us, event | category | flops | bytes accessed | tf_op | source)
XLA Modules:
  0.0 122.8 jit_solution(742840753172436170)
XLA Ops:
  6.5 0.0 copy-start.4
  6.5 0.0 all-gather.2.cloned.1.call-start
  6.5 1.1 copy.16
  7.7 13.6 %all_to_all.20 = f32[4,4,64,128]{3,2,1,0:T(8,128)S(1)} all-to-all(f32[4,4,64,128]{3,2,1,0:T(8,128)S(1)} %bitcast.27), channel_id=1, replica_groups=mesh['x'=4,'z'=8,'c'=2,'y'=4] {'x'}, dimensions={0} | all-to-all | bytes 1048576 | tf_op jit(solution)/shard_map/all_to_all | solution.py:273
  21.2 1.1 copy.15
  22.3 0.0 all-gather.2.cloned.1.call-update
  22.4 1.1 constant_dynamic-slice_fusion
  23.5 0.0 copy-start
  23.5 1.1 pad_maximum_fusion
  24.6 1.7 %collective-permute-start = (f32[3,4,64,128]{3,2,1,0:T(8,128)S(1)}, f32[3,4,64,128]{3,2,1,0:T(8,128)S(1)}, u32[]{:S(2)}, u32[]{:S(2)}) collective-permute-start(f32[3,4,64,128]{3,2,1,0:T(8,128)S(1)} %get-tuple-element.14), channel_id=1, source_target_pairs={{0,1},{1,2},{2,3},{3,0},{4,5},{5,6},{6,7},{7,4},{8,9},{9,10},{10,1... | collective-permute-start | bytes 1179656 | tf_op jit(solution)/shard_map/ppermute | solution.py:254
  26.3 0.9 collective-permute-start.1
  27.2 2.4 %collective-permute-start.2 = (f32[3,4,64,128]{3,2,1,0:T(8,128)S(1)}, f32[3,4,64,128]{3,2,1,0:T(8,128)S(1)}, u32[]{:S(2)}, u32[]{:S(2)}) collective-permute-start(f32[3,4,64,128]{3,2,1,0:T(8,128)S(1)} %get-tuple-element.12), channel_id=1, source_target_pairs={{0,3},{1,0},{2,1},{3,2},{4,7},{5,4},{6,5},{7,6},{8,11},{9,8},{10,9... | collective-permute-start | bytes 1179656 | tf_op jit(solution)/shard_map/ppermute | solution.py:254
  29.6 7.1 %collective-permute-done.r1_ref = f32[3,4,64,128]{3,2,1,0:T(8,128)S(1)} collective-permute-done((f32[3,4,64,128]{3,2,1,0:T(8,128)S(1)}, f32[3,4,64,128]{3,2,1,0:T(8,128)S(1)}, u32[]{:S(2)}, u32[]{:S(2)}) %collective-permute-start) | collective-permute-done | bytes 393248 | tf_op jit(solution)/shard_map/ppermute | solution.py:254
  36.8 3.1 %collective-permute-done.1.r2_ref = f32[3,4,64,128]{3,2,1,0:T(8,128)S(1)} collective-permute-done((f32[3,4,64,128]{3,2,1,0:T(8,128)S(1)}, f32[3,4,64,128]{3,2,1,0:T(8,128)S(1)}, u32[]{:S(2)}, u32[]{:S(2)}) %collective-permute-start.1) | collective-permute-done | bytes 393248 | tf_op jit(solution)/shard_map/ppermute | solution.py:254
  39.8 5.1 %collective-permute-done.2.r3_ref = f32[3,4,64,128]{3,2,1,0:T(8,128)S(1)} collective-permute-done((f32[3,4,64,128]{3,2,1,0:T(8,128)S(1)}, f32[3,4,64,128]{3,2,1,0:T(8,128)S(1)}, u32[]{:S(2)}, u32[]{:S(2)}) %collective-permute-start.2) | collective-permute-done | bytes 393248 | tf_op jit(solution)/shard_map/ppermute | solution.py:254
  44.9 0.0 copy-start.1
  44.9 1.1 copy-done.1
  46.0 0.0 copy-start.2
  46.0 0.9 copy-done.2
  46.9 0.0 copy-start.3
  46.9 0.9 copy-done.3
  47.8 6.5 %darcy.1 = f32[16,64,128]{2,1,0:T(8,128)} custom-call(s32[1]{0:T(128)} %bitcast.1.y_ref, f32[4,4,64,128]{3,2,1,0:T(8,128)S(1)} %copy-done.1, f32[4,64,128]{2,1,0:T(8,128)S(1)} %copy-done.2, f32[4,64,128]{2,1,0:T(8,128)S(1)} %copy-done.3, f32[3,4,64,128]{3,2,1,0:T(8,128)S(1)} %collective-permute-done.r1_ref, ...), custom_call_target="tpu_custom_call" | custom-call | tf_op jit(solution)/shard_map/darcy/pallas_call | solution.py:126
  54.2 5.3 %all-to-all-start.1 = ((f32[16,64,128]{2,1,0:T(8,128)}), f32[16,64,128]{2,1,0:T(8,128)S(1)}, u32[]{:S(2)}, u32[]{:S(2)}) async-start(f32[16,64,128]{2,1,0:T(8,128)} %darcy.1), calls=%async_computation.1 | async-start | bytes 1048576 | tf_op jit(solution)/shard_map/all_to_all | solution.py:279
  59.5 0.0 copy-done.4
  59.5 0.7 noise.1.refs_3_
  60.3 9.2 %all-to-all-done.1 = f32[16,64,128]{2,1,0:T(8,128)S(1)} async-done(((f32[16,64,128]{2,1,0:T(8,128)}), f32[16,64,128]{2,1,0:T(8,128)S(1)}, u32[]{:S(2)}, u32[]{:S(2)}) %all-to-all-start.1) | async-done | bytes 524320 | tf_op jit(solution)/shard_map/all_to_all | solution.py:279
  69.5 0.3 copy.14
  69.8 9.6 %all-gather.2.cloned.1.call-done.u_ref.refs_0_ = f32[256,8192]{1,0:T(8,128)} async-done(((f32[16,8192]{1,0:T(8,128)}), f32[256,8192]{1,0:T(8,128)}) %all-gather.2.cloned.1.call-update) | async-done | bytes 8388624 | tf_op jit(solution)/shard_map/all_gather | solution.py:275
  79.5 4.9 %gram.1 = f32[16,256]{1,0:T(8,128)S(1)} custom-call(f32[256,8192]{1,0:T(8,128)} %all-gather.2.cloned.1.call-done.u_ref.refs_0_, f32[16,8192]{1,0:T(8,128)S(1)} %bitcast.20), custom_call_target="tpu_custom_call" | custom-call | tf_op jit(solution)/shard_map/gram/pallas_call | solution.py:163
  84.4 14.4 %all_to_all.21.refs_2_ = f32[16,16,256]{2,1,0:T(8,128)S(1)} all-to-all(f32[16,16,256]{2,1,0:T(8,128)S(1)} %broadcast_in_dim.2), channel_id=1, replica_groups=mesh['x'=4,'z'=8,'c'=2,'y'=4] {'x','y'}, dimensions={0} | all-to-all | bytes 524288 | tf_op jit(solution)/shard_map/all_to_all | solution.py:290
  98.8 0.0 copy-done
  98.8 5.1 %move.1 = f32[16,64,128]{2,1,0:T(8,128)S(1)} custom-call(f32[256,8192]{1,0:T(8,128)} %all-gather.2.cloned.1.call-done.u_ref.refs_0_, f32[16,8192]{1,0:T(8,128)S(1)} %bitcast.19, f32[16,16,256]{2,1,0:T(8,128)S(1)} %all_to_all.21.refs_2_, f32[16,256]{1,0:T(8,128)S(1)} %noise.1.refs_3_), custom_call_target="tpu_custom_call" | custom-call | tf_op jit(solution)/shard_map/move/pallas_call | solution.py:202
  103.9 11.2 %all_to_all.22 = f32[4,4,64,128]{3,2,1,0:T(8,128)S(1)} all-to-all(f32[4,4,64,128]{3,2,1,0:T(8,128)S(1)} %bitcast.21), channel_id=1, replica_groups=mesh['x'=4,'z'=8,'c'=2,'y'=4] {'x'}, dimensions={0} | all-to-all | bytes 1048576 | tf_op jit(solution)/shard_map/all_to_all | solution.py:293
  115.2 0.8 copy.8
  (1 shorter events, 0.0 us)
Async XLA Ops:
  6.5 53.0 %copy-start.4 = (f32[256,256]{1,0:T(8,128)S(1)}, f32[256,256]{1,0:T(8,128)}, u32[]{:S(2)}) copy-start(f32[256,256]{1,0:T(8,128)} %refs_1_.1) | copy-start | bytes 786436
  6.5 72.9 %all-gather.2.cloned.1.call-start = ((), (), s32[]{:S(2)}) async-start(), calls=%async_computation.4 | async-start | bytes 8912896 | tf_op jit(solution)/shard_map/all_gather | solution.py:275
  23.5 75.3 %copy-start = (f32[2,8,64,128]{3,1,2,0:T(8,128)S(1)}, f32[2,8,64,128]{3,1,2,0:T(8,128)}, u32[]{:S(2)}) copy-start(f32[2,8,64,128]{3,1,2,0:T(8,128)} %copy.15) | copy-start | bytes 1572868
  24.6 12.1 %collective-permute-start = (f32[3,4,64,128]{3,2,1,0:T(8,128)S(1)}, f32[3,4,64,128]{3,2,1,0:T(8,128)S(1)}, u32[]{:S(2)}, u32[]{:S(2)}) collective-permute-start(f32[3,4,64,128]{3,2,1,0:T(8,128)S(1)} %get-tuple-element.14), channel_id=1, source_target_pairs={{0,1},{1,2},{2,3},{3,0},{4,5},{5,6},{6,7},{7,4},{8,9},{9,10},{10,1... | collective-permute-start | bytes 1179656 | tf_op jit(solution)/shard_map/ppermute | solution.py:254
  26.3 13.6 %collective-permute-start.1 = (f32[3,4,64,128]{3,2,1,0:T(8,128)S(1)}, f32[3,4,64,128]{3,2,1,0:T(8,128)S(1)}, u32[]{:S(2)}, u32[]{:S(2)}) collective-permute-start(f32[3,4,64,128]{3,2,1,0:T(8,128)S(1)} %get-tuple-element.13), channel_id=1, source_target_pairs={{0,2},{1,3},{2,0},{3,1},{4,6},{5,7},{6,4},{7,5},{8,10},{9,11},{10,... | collective-permute-start | bytes 1179656 | tf_op jit(solution)/shard_map/ppermute | solution.py:254
  27.2 17.7 %collective-permute-start.2 = (f32[3,4,64,128]{3,2,1,0:T(8,128)S(1)}, f32[3,4,64,128]{3,2,1,0:T(8,128)S(1)}, u32[]{:S(2)}, u32[]{:S(2)}) collective-permute-start(f32[3,4,64,128]{3,2,1,0:T(8,128)S(1)} %get-tuple-element.12), channel_id=1, source_target_pairs={{0,3},{1,0},{2,1},{3,2},{4,7},{5,4},{6,5},{7,6},{8,11},{9,8},{10,9... | collective-permute-start | bytes 1179656 | tf_op jit(solution)/shard_map/ppermute | solution.py:254
  44.9 1.1 copy-start.1
  46.0 0.9 copy-start.2
  46.9 0.9 copy-start.3
  54.2 15.3 %all-to-all-start.1 = ((f32[16,64,128]{2,1,0:T(8,128)}), f32[16,64,128]{2,1,0:T(8,128)S(1)}, u32[]{:S(2)}, u32[]{:S(2)}) async-start(f32[16,64,128]{2,1,0:T(8,128)} %darcy.1), calls=%async_computation.1 | async-start | bytes 1048576 | tf_op jit(solution)/shard_map/all_to_all | solution.py:279
Sparse Core Ops, SparseCore 0:
  22.5 56.9 all-gather.1

commit v4 on v3

v4 whole, which is shorter than its diff:
```python
import math

import jax
import jax.numpy as jnp
from jax import lax
from jax.experimental import pallas as pl
from jax.experimental.pallas import tpu as pltpu
from jax.sharding import Mesh
from jax.sharding import PartitionSpec as P

SWEEPS = 8
MISFIT_WEIGHT = 1000.0
PAD = 8
SPREAD_AXES = ("x", "zh")
VMEM_LIMIT = 40 << 20


def offset(order):
    half = (order + 1) // 2
    return jnp.where(order % 2 == 0, half, -half)


def member(zl, core, spot, particle):
    return (spot // 2) * 64 + (zl * 2 + spot % 2) * 8 + core * 4 + particle


def darcy_kernel(
    y_ref, u_ref, src_ref, obs_ref, r1_ref, r2_ref, r3_ref, g_ref,
    e_s, w0, w1, p_s, inv_s, b_s, a_s, src_s, obs_s,
):
    slabs, width, rows, lanes = u_ref.shape
    layers = slabs * width
    lane = lax.broadcasted_iota(jnp.int32, (rows, lanes), 1)
    first = lane == 0
    last = lane == lanes - 1
    mid = pl.ds(PAD, rows)
    up = pl.ds(PAD - 1, rows)
    down = pl.ds(PAD + 1, rows)

    def before(v, fill):
        return jnp.where(first, fill, pltpu.roll(v, 1, 1))

    def after(v, fill):
        return jnp.where(last, fill, pltpu.roll(v, lanes - 1, 1))

    def neighbors(ref, i, fill):
        core = ref[i + 1, mid, :]
        return (
            (ref[i, mid, :] + ref[i + 2, mid, :])
            + (ref[i + 1, up, :] + ref[i + 1, down, :])
            + (before(core, fill) + after(core, fill))
        )

    for ref, fill in ((e_s, 1.0), (w0, 0.0), (w1, 0.0), (p_s, 0.0)):
        ref[:, :PAD, :] = jnp.full((layers + 2, PAD, lanes), fill, jnp.float32)
        ref[:, PAD + rows :, :] = jnp.full((layers + 2, PAD, lanes), fill, jnp.float32)
        for outside in (0, layers + 1):
            ref[outside, mid, :] = jnp.full((rows, lanes), fill, jnp.float32)

    y = y_ref[0]
    for w in range(width):
        e_s[y * width + w + 1, mid, :] = jnp.exp(0.5 * u_ref[y, w])
        src_s[y * width + w] = src_ref[w]
        obs_s[y * width + w] = obs_ref[w]
    for shift, ref in ((1, r1_ref), (2, r2_ref), (3, r3_ref)):
        slab = lax.rem(y + slabs - shift, slabs)
        for w in range(width):
            e_s[slab * width + w + 1, mid, :] = jnp.exp(0.5 * ref[0, w])
            src_s[slab * width + w] = ref[1, w]
            obs_s[slab * width + w] = ref[2, w]

    for i in range(layers):
        inverse = 1.0 / neighbors(e_s, i, 1.0)
        inv_s[i] = inverse
        b_s[i] = inverse * e_s[i + 1, mid, :]
        start = inverse * src_s[i]
        a_s[i] = start
        w0[i + 1, mid, :] = start

    def sweep(now, new):
        for i in range(layers):
            new[i + 1, mid, :] = a_s[i] + b_s[i] * neighbors(now, i, 0.0)

    def relax():
        def two(_, carry):
            sweep(w0, w1)
            sweep(w1, w0)
            return carry

        lax.fori_loop(0, (SWEEPS - 1) // 2, two, 0)
        sweep(w0, w1)

    relax()
    for i in range(layers):
        pressure = w1[i + 1, mid, :] / e_s[i + 1, mid, :]
        p_s[i + 1, mid, :] = pressure
        start = inv_s[i] * (MISFIT_WEIGHT * (pressure - obs_s[i]))
        a_s[i] = start
        w0[i + 1, mid, :] = start
    relax()
    for i in range(layers):
        w1[i + 1, mid, :] = w1[i + 1, mid, :] / e_s[i + 1, mid, :]

    chunk = g_ref.shape[1]
    per_layer = rows // chunk
    for i in range(layers):
        e = e_s[i + 1, mid, :]
        p = p_s[i + 1, mid, :]
        q = w1[i + 1, mid, :]
        total = None
        for at, where in ((i, mid), (i + 2, mid), (i + 1, up), (i + 1, down)):
            term = e_s[at, where, :] * (p - p_s[at, where, :]) * (q - w1[at, where, :])
            total = term if total is None else total + term
        for shift in (before, after):
            total = total + shift(e, 1.0) * (p - shift(p, 0.0)) * (q - shift(q, 0.0))
        gradient = -0.5 * e * total
        for h in range(per_layer):
            spot = (i % width) * per_layer + h
            g_ref[spot * slabs + i // width] = gradient[h * chunk : (h + 1) * chunk]


def darcy(y, u, source, observed, received, chunk):
    slabs, width, rows, lanes = u.shape
    layers = slabs * width
    padded = pltpu.VMEM((layers + 2, rows + 2 * PAD, lanes), jnp.float32)
    plain = pltpu.VMEM((layers, rows, lanes), jnp.float32)
    whole = pl.BlockSpec(memory_space=pltpu.VMEM)
    return pl.pallas_call(
        darcy_kernel,
        in_specs=[pl.BlockSpec(memory_space=pltpu.SMEM)] + [whole] * 6,
        out_specs=whole,
        out_shape=jax.ShapeDtypeStruct((layers * rows // chunk, chunk, lanes), jnp.float32),
        scratch_shapes=[padded] * 4 + [plain] * 5,
        compiler_params=pltpu.CompilerParams(vmem_limit_bytes=VMEM_LIMIT),
        name="darcy",
    )(y.reshape(1), u, source, observed, *received)


def split(v):
    high = v.astype(jnp.bfloat16)
    low = (v - high.astype(jnp.float32)).astype(jnp.bfloat16)
    return high, low


def columns(refs, start, size):
    return jnp.concatenate([ref[:, start : start + size] for ref in refs], axis=0)


def gram_kernel(*refs, tile):
    *u_refs, g_ref, o_ref = refs
    block, cells = g_ref.shape
    members = o_ref.shape[1]
    dims = (((1,), (1,)), ((), ()))
    total = jnp.zeros((2 * block, members), jnp.float32)
    for start in range(0, cells, tile):
        u = columns(u_refs, start, tile)
        s_high, s_low = split(u - jnp.sum(u, axis=0, keepdims=True) * (1.0 / members))
        pair = jnp.concatenate(split(g_ref[:, start : start + tile]), axis=0)
        total = total + lax.dot_general(pair, s_high, dims, preferred_element_type=jnp.float32)
        total = total + lax.dot_general(pair, s_low, dims, preferred_element_type=jnp.float32)
    o_ref[...] = total[:block] + total[block:]


def gram_product(blocks, g, tile):
    members = sum(b.shape[0] for b in blocks)
    whole = pl.BlockSpec(memory_space=pltpu.VMEM)
    return pl.pallas_call(
        lambda *refs: gram_kernel(*refs, tile=tile),
        in_specs=[whole] * (len(blocks) + 1),
        out_specs=whole,
        out_shape=jax.ShapeDtypeStruct((g.shape[0], members), jnp.float32),
        compiler_params=pltpu.CompilerParams(vmem_limit_bytes=VMEM_LIMIT),
        name="gram",
    )(*blocks, g)


def move_kernel(*refs, scale, tile):
    *u_refs, parts_ref, noise_ref, o_ref = refs
    block, _, lanes = o_ref.shape
    cells = u_refs[0].shape[1]
    members = noise_ref.shape[1]
    total = parts_ref[0]
    for d in range(1, parts_ref.shape[0]):
        total = total + parts_ref[d]
    pair = jnp.concatenate(split(noise_ref[...] - scale * total), axis=0)
    dims = (((1,), (0,)), ((), ()))
    for start in range(0, cells, tile):
        u = columns(u_refs, start, tile)
        s = u - jnp.sum(u, axis=0, keepdims=True) * (1.0 / members)
        s_high, s_low = split(s)
        out = lax.dot_general(pair, s_high, dims, preferred_element_type=jnp.float32)
        out = out + lax.dot_general(pair, s_low, dims, preferred_element_type=jnp.float32)
        moved = u[:block] + 0.25 * s[:block] + (out[:block] + out[block:])
        for r in range(tile // lanes):
            o_ref[:, start // lanes + r, :] = moved[:, r * lanes : (r + 1) * lanes]


def move(blocks, parts, noise, scale, tile):
    block, cells = blocks[0].shape
    lanes = 128
    whole = pl.BlockSpec(memory_space=pltpu.VMEM)
    return pl.pallas_call(
        lambda *refs: move_kernel(*refs, scale=scale, tile=tile),
        in_specs=[whole] * (len(blocks) + 2),
        out_specs=whole,
        out_shape=jax.ShapeDtypeStruct((block, cells // lanes, lanes), jnp.float32),
        compiler_params=pltpu.CompilerParams(vmem_limit_bytes=VMEM_LIMIT),
        name="move",
    )(*blocks, parts, noise)


def noise_kernel(at_ref, b_ref, o_ref, *, spots, particles, depth, scale):
    block, members = o_ref.shape
    zl, core = at_ref[0], at_ref[1]
    t = lax.broadcasted_iota(jnp.int32, (block, members), 0)
    j = lax.broadcasted_iota(jnp.int32, (block, members), 1)
    column = member(zl, core, t // particles, t % particles)
    chosen = jnp.where(j == column, scale, 0.0)
    k = lax.broadcasted_iota(jnp.int32, (members, members), 0)
    m = lax.broadcasted_iota(jnp.int32, (members, members), 1)
    order = (m // block) % depth
    m_zl = (zl + offset(order) + depth) % depth
    m_core = (core + m // (block * depth)) % 2
    row = member(m_zl, m_core, (m // particles) % spots, m % particles)
    chosen_row = jnp.where(k == row, 1.0, 0.0)
    picked = lax.dot_general(
        chosen, b_ref[...], (((1,), (1,)), ((), ())),
        precision=lax.Precision.HIGHEST, preferred_element_type=jnp.float32,
    )
    o_ref[...] = lax.dot_general(
        picked, chosen_row, (((1,), (0,)), ((), ())),
        precision=lax.Precision.HIGHEST, preferred_element_type=jnp.float32,
    )


def ordered_noise(brownian, at, spots, particles, depth, scale):
    return pl.pallas_call(
        lambda *refs: noise_kernel(
            *refs, spots=spots, particles=particles, depth=depth, scale=scale
        ),
        in_specs=[
            pl.BlockSpec(memory_space=pltpu.SMEM),
            pl.BlockSpec(memory_space=pltpu.VMEM),
        ],
        out_shape=jax.ShapeDtypeStruct((spots * particles, brownian.shape[0]), jnp.float32),
        compiler_params=pltpu.CompilerParams(vmem_limit_bytes=VMEM_LIMIT),
        name="noise",
    )(at, brownian)


def shifted(block, axis, shift):
    count = lax.axis_size(axis)
    return lax.ppermute(block, axis, [(i, (i + shift) % count) for i in range(count)])


def on_device(logperm, source, observed, brownian):
    particles, width, rows, lanes = logperm.shape
    slabs = lax.axis_size("y")
    spots = lax.axis_size(SPREAD_AXES)
    depth = lax.axis_size("zl")
    cores = lax.axis_size("c")
    ensemble = particles * spots * depth * cores
    chunk = width * rows // spots
    cells = width * slabs * rows * lanes

    chunks = jnp.swapaxes(logperm.reshape(particles, spots, chunk, lanes), 0, 1)
    own = lax.all_to_all(chunks, SPREAD_AXES, split_axis=0, concat_axis=0, tiled=True)
    own = own.reshape(spots * particles, chunk * lanes)

    y = lax.axis_index("y")
    fields = jnp.stack([source, observed])
    received = []
    for shift in range(1, slabs):
        mine = lax.dynamic_slice_in_dim(logperm, (y + shift) % slabs, 1, axis=0)
        received.append(shifted(jnp.concatenate([mine, fields], axis=0), "y", shift))

    blocks = [own]
    ahead, back = own, own
    for _ in range(depth // 2 - 1):
        ahead, back = shifted(ahead, "zl", 1), shifted(back, "zl", depth - 1)
        blocks += [ahead, back]
    half = own.shape[0] // 2
    blocks += [shifted(ahead[:half], "zl", 1), shifted(back[half:], "zl", depth - 1)]
    blocks += [shifted(block, "c", 1) for block in blocks]

    gradient = darcy(y, logperm, source, observed, received, chunk)
    g = lax.all_to_all(gradient, SPREAD_AXES + ("y",), split_axis=0, concat_axis=0, tiled=True)
    g = g.reshape(spots * particles, chunk * lanes)

    step_size = ensemble / (4.0 * (cells + 1))
    noise_scale = math.sqrt(2.0 * step_size / ensemble)
    at = jnp.stack([lax.axis_index("zl"), lax.axis_index("c")])
    noise = ordered_noise(brownian, at, spots, particles, depth, noise_scale)
    g, noise = lax.optimization_barrier((g, noise))

    part = gram_product(blocks, g, 1024)
    part = part + shifted(part, "zh", 1)
    copies = spots * slabs // 2
    parts = jnp.broadcast_to(part[None], (copies,) + part.shape)
    parts = lax.all_to_all(parts, ("x", "y"), split_axis=0, concat_axis=0, tiled=True)
    moved = move(blocks, parts, noise, step_size / ensemble, 1024)
    moved = moved.reshape(spots, particles, chunk, lanes)
    returned = lax.all_to_all(moved, SPREAD_AXES, split_axis=0, concat_axis=0, tiled=True)
    return jnp.swapaxes(returned, 0, 1).reshape(logperm.shape)


def solution(mesh):
    fine = Mesh(mesh.devices.reshape(4, 4, 2, 2, 4), ("x", "zl", "zh", "c", "y"))
    dom = ("x", "zl", "zh", "c")
    return jax.shard_map(
        on_device,
        mesh=fine,
        in_specs=(P(dom, "y", None, None), P("y", None, None), P("y", None, None), P()),
        out_specs=P(dom, "y", None, None),
        check_vma=False,
    )
```

time: 123 us -> 110 us (0.89)
  starting transfers between devices: 10.3 us -> 31 us
  between operations: 13.5 us -> 0.17 us
  blocking collectives: 39.2 us -> 27.3 us
  Pallas kernels: 17.2 us -> 12.9 us
  waiting for transfers between devices: 34.2 us -> 30.9 us
    ppermute x3 -> x13, waiting for transfers between devices: 15.3 us -> 27.3 us  [shifted(): lax.ppermute(block, axis, [(i, (i + shift) % count) for i in range(count)])]
    all_to_all x3 -> x2, blocking collectives: 39.2 us -> 27.3 us  [the longest x1 16.2 us: on_device(): lax.all_to_all(parts, ('x', 'y'), split_axis=0, concat_axis=0, tiled=True)]
    ppermute x3 -> x13, starting transfers between devices: 5 us -> 16.7 us  [shifted(): lax.ppermute(block, axis, [(i, (i + shift) % count) for i in range(count)])]
    all_gather x1 -> x0, waiting for transfers between devices: 9.63 us -> none  [on_device(): u_all = lax.all_gather(own, GATHER_AXES, axis=0, tiled=True)]
    all_to_all x1 -> x2, starting transfers between devices: 5.29 us -> 14.3 us  [the longest x1 8.55 us: on_device(): lax.all_to_all(gradient, SPREAD_AXES + ('y',), split_axis=0, concat_axis=...]
    all_to_all x1 -> x2, waiting for transfers between devices: 9.23 us -> 3.65 us  [the longest x1 3.64 us: on_device(): lax.all_to_all(chunks, SPREAD_AXES, split_axis=0, concat_axis=0, tiled=True)]
    pallas_call x2, Pallas kernels: 9.97 us -> 5.22 us  [the longest x1 2.62 us: move(): pl.pallas_call(lambda *refs: move_kernel(*refs, scale=scale, tile=tile),...]
    reshape x0 -> x1, local copies, waits for them, and re-layouts: none -> 1.87 us  [on_device(): chunks = jnp.swapaxes(logperm.reshape(particles, spots, chunk, lanes), 0, 1)]
  transfers between devices with their start and end apart: 5 -> 15, of which waited for: 5 -> 5; matrix products, arithmetic and copies ran while one was open for 2% -> 3% of each run, Pallas kernels for 6% -> 7%
where the time goes in v4:
time: 110 us
  starting transfers between devices  31 us (28%)
  waiting for transfers between devices  30.9 us (28%)
  blocking collectives  27.3 us (25%)
  Pallas kernels  12.9 us (12%)
  local copies, waits for them, and re-layouts  6.35 us (6%)
  other arithmetic  1.22 us (1%)
    ppermute x13, waiting for transfers between devices, shifted(): lax.ppermute(block, axis, [(i, (i + shift) % count) for i in range(count)])  27.3 us
    ppermute x13, starting transfers between devices, shifted(): lax.ppermute(block, axis, [(i, (i + shift) % count) for i in range(count)])  16.7 us
    all_to_all x1, blocking collectives, on_device(): lax.all_to_all(parts, ('x', 'y'), split_axis=0, concat_axis=0, tiled=True)  16.2 us
    all_to_all x1, blocking collectives, on_device(): lax.all_to_all(moved, SPREAD_AXES, split_axis=0, concat_axis=0, tiled=True)  11.1 us
    all_to_all x1, starting transfers between devices, on_device(): lax.all_to_all(gradient, SPREAD_AXES + ('y',), split_axis=0, concat_axis=...  8.55 us
    pallas_call x1, Pallas kernels, darcy(): pl.pallas_call(darcy_kernel, in_specs=[pl.BlockSpec(memory_space=pltpu.SM...  6.44 us
    all_to_all x1, starting transfers between devices, on_device(): lax.all_to_all(chunks, SPREAD_AXES, split_axis=0, concat_axis=0, tiled=True)  5.79 us
    all_to_all x1, waiting for transfers between devices, on_device(): lax.all_to_all(chunks, SPREAD_AXES, split_axis=0, concat_axis=0, tiled=True)  3.64 us
  transfers between devices with their start and end apart: 15, of which 5 were waited for; matrix products, arithmetic and copies ran while one was open for 3% of the time, Pallas kernels for 7%

profile of v4, /device:TPU:8, one launch (start us, length us, event | category | flops | bytes accessed | tf_op | source)
XLA Modules:
  0.0 109.9 jit_solution(3470993889303413650)
XLA Ops:
  0.0 1.9 %copy.14 = f32[4,8,32,128]{3,2,0,1:T(8,128)} copy(f32[4,8,32,128]{3,2,1,0:T(8,128)} %bitcast.26) | data formatting | bytes 1048576 | tf_op jit(solution)/shard_map/reshape | solution.py:266
  1.9 5.8 %all-to-all-start = ((f32[8,4,32,128]{3,2,1,0:T(8,128)}), f32[8,4,32,128]{3,2,1,0:T(8,128)S(1)}, u32[]{:S(2)}, u32[]{:S(2)}) async-start(f32[8,4,32,128]{3,2,1,0:T(8,128)} %bitcast.20), calls=%async_computation | async-start | bytes 1048576 | tf_op jit(solution)/shard_map/all_to_all | solution.py:267
  7.7 0.0 copy-done
  7.7 0.0 copy-start.1
  7.7 0.0 copy-start.2
  7.7 0.8 copy-done.1
  8.6 0.1 copy-done.2
  8.6 1.1 %pad_maximum_fusion = (f32[3,4,64,128]{3,2,1,0:T(8,128)}, f32[3,4,64,128]{3,2,1,0:T(8,128)}, f32[3,4,64,128]{3,2,1,0:T(8,128)}) fusion(f32[1,4,64,128]{3,2,1,0:T(8,128)S(1)} %bitcast.30, f32[1,4,64,128]{3,2,1,0:T(8,128)S(1)} %bitcast.29, f32[1,4,64,128]{3,2,1,0:T(8,128)S(1)} %get-tuple-element.9, f32[1,4,64,128]{3,2,1,0:T(8,128)S(1)} %get-tuple-element.10, ...), kind=kLoop, calls=%fused_computation | loop fusion | flops 589824 | bytes 1835008 | tf_op jit(solution)/shard_map/concatenate | solution.py:275
  9.8 2.3 %collective-permute-start.10 = (f32[3,4,64,128]{3,2,1,0:T(8,128)}, f32[3,4,64,128]{3,2,1,0:T(8,128)S(1)}, u32[]{:S(2)}, u32[]{:S(2)}) collective-permute-start(f32[3,4,64,128]{3,2,1,0:T(8,128)} %get-tuple-element.13), channel_id=1, source_target_pairs={{0,2},{1,3},{2,0},{3,1},{4,6},{5,7},{6,4},{7,5},{8,10},{9,11},{10,... | collective-permute-start | bytes 1179656 | tf_op jit(solution)/shard_map/ppermute | solution.py:253
  12.1 1.3 %collective-permute-start.11 = (f32[3,4,64,128]{3,2,1,0:T(8,128)}, f32[3,4,64,128]{3,2,1,0:T(8,128)S(1)}, u32[]{:S(2)}, u32[]{:S(2)}) collective-permute-start(f32[3,4,64,128]{3,2,1,0:T(8,128)} %get-tuple-element.12), channel_id=1, source_target_pairs={{0,3},{1,0},{2,1},{3,2},{4,7},{5,4},{6,5},{7,6},{8,11},{9,8},{10,9... | collective-permute-start | bytes 1179656 | tf_op jit(solution)/shard_map/ppermute | solution.py:253
  13.4 0.7 collective-permute-start.9
  14.1 3.6 %all-to-all-done = f32[8,4,32,128]{3,2,1,0:T(8,128)S(1)} async-done(((f32[8,4,32,128]{3,2,1,0:T(8,128)}), f32[8,4,32,128]{3,2,1,0:T(8,128)S(1)}, u32[]{:S(2)}, u32[]{:S(2)}) %all-to-all-start) | async-done | bytes 524320 | tf_op jit(solution)/shard_map/all_to_all | solution.py:267
  17.7 0.3 copy.13
  18.1 3.3 %collective-permute-start = (f32[32,4096]{1,0:T(8,128)S(1)}, f32[32,4096]{1,0:T(8,128)S(1)}, u32[]{:S(2)}, u32[]{:S(2)}) collective-permute-start(f32[32,4096]{1,0:T(8,128)S(1)} %bitcast.21), channel_id=1, source_target_pairs={{0,16},{16,32},{32,48},{48,0},{1,17},{17,33},{33,49},{49,1},{2,18}... | collective-permute-start | bytes 1572872 | tf_op jit(solution)/shard_map/ppermute | solution.py:253
  21.4 2.2 %collective-permute-start.1 = (f32[32,4096]{1,0:T(8,128)S(1)}, f32[32,4096]{1,0:T(8,128)S(1)}, u32[]{:S(2)}, u32[]{:S(2)}) collective-permute-start(f32[32,4096]{1,0:T(8,128)S(1)} %bitcast.22), channel_id=1, source_target_pairs={{0,48},{16,0},{32,16},{48,32},{1,49},{17,1},{33,17},{49,33},{2,50}... | collective-permute-start | bytes 1572872 | tf_op jit(solution)/shard_map/ppermute | solution.py:253
  23.6 0.0 collective-permute-done.10.r2_ref
  23.6 6.9 %collective-permute-done.11.r3_ref = f32[3,4,64,128]{3,2,1,0:T(8,128)S(1)} collective-permute-done((f32[3,4,64,128]{3,2,1,0:T(8,128)}, f32[3,4,64,128]{3,2,1,0:T(8,128)S(1)}, u32[]{:S(2)}, u32[]{:S(2)}) %collective-permute-start.11) | collective-permute-done | bytes 393248 | tf_op jit(solution)/shard_map/ppermute | solution.py:253
  30.5 0.2 collective-permute-done.9.r1_ref
  30.7 6.4 %darcy.1 = f32[32,32,128]{2,1,0:T(8,128)} custom-call(s32[1]{0:T(128)} %bitcast.2.y_ref, f32[4,4,64,128]{3,2,1,0:T(8,128)S(1)} %copy-done, f32[4,64,128]{2,1,0:T(8,128)S(1)} %copy-done.1, f32[4,64,128]{2,1,0:T(8,128)S(1)} %copy-done.2, f32[3,4,64,128]{3,2,1,0:T(8,128)S(1)} %collective-permute-done.9.r1_ref, ...), custom_call_target="tpu_custom_call" | custom-call | tf_op jit(solution)/shard_map/darcy/pallas_call | solution.py:128
  37.1 8.5 %all-to-all-start.1 = ((f32[32,32,128]{2,1,0:T(8,128)}), f32[32,32,128]{2,1,0:T(8,128)}, u32[]{:S(2)}, u32[]{:S(2)}) async-start(f32[32,32,128]{2,1,0:T(8,128)} %darcy.1), calls=%async_computation.1 | async-start | bytes 1048576 | tf_op jit(solution)/shard_map/all_to_all | solution.py:287
  45.7 0.1 collective-permute-start.4
  45.8 0.0 collective-permute-done.refs_1_
  45.8 3.3 %collective-permute-start.2 = (f32[16,4096]{1,0:T(8,128)S(1)}, f32[16,4096]{1,0:T(8,128)S(1)}, u32[]{:S(2)}, u32[]{:S(2)}) collective-permute-start(f32[16,4096]{1,0:T(8,128)S(1)} %slice.8), channel_id=1, source_target_pairs={{0,16},{16,32},{32,48},{48,0},{1,17},{17,33},{33,49},{49,1},{2,18}... | collective-permute-start | bytes 786440 | tf_op jit(solution)/shard_map/ppermute | solution.py:253
  49.1 0.0 collective-permute-done.1.refs_2_
  49.2 2.2 %collective-permute-start.3 = (f32[16,4096]{1,0:T(8,128)S(1)}, f32[16,4096]{1,0:T(8,128)}, u32[]{:S(2)}, u32[]{:S(2)}) collective-permute-start(f32[16,4096]{1,0:T(8,128)S(1)} %slice.9), channel_id=1, source_target_pairs={{0,48},{16,0},{32,16},{48,32},{1,49},{17,1},{33,17},{49,33},{2,50}... | collective-permute-start | bytes 786440 | tf_op jit(solution)/shard_map/ppermute | solution.py:253
  51.4 0.2 collective-permute-start.5
  51.6 0.3 collective-permute-start.6
  51.9 16.3 %collective-permute-done.2.refs_3_ = f32[16,4096]{1,0:T(8,128)S(1)} collective-permute-done((f32[16,4096]{1,0:T(8,128)S(1)}, f32[16,4096]{1,0:T(8,128)S(1)}, u32[]{:S(2)}, u32[]{:S(2)}) %collective-permute-start.2) | collective-permute-done | bytes 262176 | tf_op jit(solution)/shard_map/ppermute | solution.py:253
  68.3 0.0 collective-permute-start.7
  68.3 0.0 collective-permute-done.3.refs_4_
  68.3 0.5 collective-permute-start.8
  68.8 0.1 pad_add_fusion.refs_0_
  68.8 0.9 copy-done.3
  69.8 1.3 %noise.1.refs_11_ = f32[32,256]{1,0:T(8,128)S(1)} custom-call(s32[2]{0:T(128)S(1)} %pad_add_fusion.refs_0_, f32[256,256]{1,0:T(8,128)S(1)} %copy-done.3), custom_call_target="tpu_custom_call" | custom-call | tf_op jit(solution)/shard_map/noise/pallas_call | solution.py:237
  71.1 0.0 all-to-all-done.1
  71.1 1.3 %copy.12 = f32[4,8,32,128]{3,1,2,0:T(8,128)S(1)} copy(f32[4,8,32,128]{3,2,1,0:T(8,128)} %bitcast.13) | data formatting | bytes 1048576
  72.4 0.0 collective-permute-done.4.refs_5_
  72.5 0.0 collective-permute-done.7.refs_8_
  72.5 0.0 collective-permute-done.8.refs_9_
  72.5 0.0 collective-permute-done.5.refs_6_
  72.5 0.0 collective-permute-done.6.refs_7_
  72.5 2.6 %gram.1 = f32[32,256]{1,0:T(8,128)S(1)} custom-call(f32[32,4096]{1,0:T(8,128)S(1)} %bitcast.24, f32[32,4096]{1,0:T(8,128)S(1)} %collective-permute-done.refs_1_, f32[32,4096]{1,0:T(8,128)S(1)} %collective-permute-done.1.refs_2_, f32[16,4096]{1,0:T(8,128)S(1)} %collective-permute-done.2.refs_3_, f32[16,4096]{1,0:T(8,128)} %collective-permute-done.3.refs_4_, ...), custom_call_target="tpu_custom_call" | custom-call | tf_op jit(solution)/shard_map/gram/pallas_call | solution.py:167
  75.1 0.1 collective-permute-start.12
  75.2 3.9 %collective-permute-done.12 = f32[32,256]{1,0:T(8,128)S(1)} collective-permute-done((f32[32,256]{1,0:T(8,128)S(1)}, f32[32,256]{1,0:T(8,128)S(1)}, u32[]{:S(2)}, u32[]{:S(2)}) %collective-permute-start.12) | collective-permute-done | bytes 32800 | tf_op jit(solution)/shard_map/ppermute | solution.py:253
  79.2 16.2 %all_to_all.20.refs_10_ = f32[16,32,256]{2,1,0:T(8,128)S(1)} all-to-all(f32[16,32,256]{2,1,0:T(8,128)S(1)} %broadcast_in_dim.2), channel_id=1, replica_groups=mesh['x'=4,'zl'=4,'zh'=2,'c'=2,'y'=4] {'x','y'}, dimensions={0} | all-to-all | bytes 1048576 | tf_op jit(solution)/shard_map/all_to_all | solution.py:300
  95.3 2.6 %move.1 = f32[32,32,128]{2,1,0:T(8,128)S(1)} custom-call(f32[32,4096]{1,0:T(8,128)S(1)} %bitcast.25, f32[32,4096]{1,0:T(8,128)S(1)} %collective-permute-done.refs_1_, f32[32,4096]{1,0:T(8,128)S(1)} %collective-permute-done.1.refs_2_, f32[16,4096]{1,0:T(8,128)S(1)} %collective-permute-done.2.refs_3_, f32[16,4096]{1,0:T(8,128)} %collective-permute-done.3.refs_4_, ...), custom_call_target="tpu_custom_call" | custom-call | tf_op jit(solution)/shard_map/move/pallas_call | solution.py:202
  98.0 11.1 %all_to_all.21 = f32[8,4,32,128]{3,2,1,0:T(8,128)S(1)} all-to-all(f32[8,4,32,128]{3,2,1,0:T(8,128)S(1)} %bitcast.28), channel_id=1, replica_groups=mesh['x'=4,'zl'=4,'zh'=2,'c'=2,'y'=4] {'x','zh'}, dimensions={0} | all-to-all | bytes 1048576 | tf_op jit(solution)/shard_map/all_to_all | solution.py:303
  109.1 0.8 copy.6
  (7 shorter events, 0.1 us)
Async XLA Ops:
  1.9 5.8 %copy-start = (f32[4,4,64,128]{3,2,1,0:T(8,128)S(1)}, f32[4,4,64,128]{3,2,1,0:T(8,128)}, u32[]{:S(2)}) copy-start(f32[4,4,64,128]{3,2,1,0:T(8,128)} %u_ref.1) | copy-start | bytes 1572868
  1.9 15.9 %all-to-all-start = ((f32[8,4,32,128]{3,2,1,0:T(8,128)}), f32[8,4,32,128]{3,2,1,0:T(8,128)S(1)}, u32[]{:S(2)}, u32[]{:S(2)}) async-start(f32[8,4,32,128]{3,2,1,0:T(8,128)} %bitcast.20), calls=%async_computation | async-start | bytes 1048576 | tf_op jit(solution)/shard_map/all_to_all | solution.py:267
  7.7 0.9 copy-start.1
  7.7 1.0 copy-start.2
  9.8 13.8 %collective-permute-start.10 = (f32[3,4,64,128]{3,2,1,0:T(8,128)}, f32[3,4,64,128]{3,2,1,0:T(8,128)S(1)}, u32[]{:S(2)}, u32[]{:S(2)}) collective-permute-start(f32[3,4,64,128]{3,2,1,0:T(8,128)} %get-tuple-element.13), channel_id=1, source_target_pairs={{0,2},{1,3},{2,0},{3,1},{4,6},{5,7},{6,4},{7,5},{8,10},{9,11},{10,... | collective-permute-start | bytes 1179656 | tf_op jit(solution)/shard_map/ppermute | solution.py:253
  12.1 18.4 %collective-permute-start.11 = (f32[3,4,64,128]{3,2,1,0:T(8,128)}, f32[3,4,64,128]{3,2,1,0:T(8,128)S(1)}, u32[]{:S(2)}, u32[]{:S(2)}) collective-permute-start(f32[3,4,64,128]{3,2,1,0:T(8,128)} %get-tuple-element.12), channel_id=1, source_target_pairs={{0,3},{1,0},{2,1},{3,2},{4,7},{5,4},{6,5},{7,6},{8,11},{9,8},{10,9... | collective-permute-start | bytes 1179656 | tf_op jit(solution)/shard_map/ppermute | solution.py:253
  13.4 17.2 %collective-permute-start.9 = (f32[3,4,64,128]{3,2,1,0:T(8,128)}, f32[3,4,64,128]{3,2,1,0:T(8,128)S(1)}, u32[]{:S(2)}, u32[]{:S(2)}) collective-permute-start(f32[3,4,64,128]{3,2,1,0:T(8,128)} %get-tuple-element.14), channel_id=1, source_target_pairs={{0,1},{1,2},{2,3},{3,0},{4,5},{5,6},{6,7},{7,4},{8,9},{9,10},{10,1... | collective-permute-start | bytes 1179656 | tf_op jit(solution)/shard_map/ppermute | solution.py:253
  18.1 27.7 %collective-permute-start = (f32[32,4096]{1,0:T(8,128)S(1)}, f32[32,4096]{1,0:T(8,128)S(1)}, u32[]{:S(2)}, u32[]{:S(2)}) collective-permute-start(f32[32,4096]{1,0:T(8,128)S(1)} %bitcast.21), channel_id=1, source_target_pairs={{0,16},{16,32},{32,48},{48,0},{1,17},{17,33},{33,49},{49,1},{2,18}... | collective-permute-start | bytes 1572872 | tf_op jit(solution)/shard_map/ppermute | solution.py:253
  21.4 27.7 %collective-permute-start.1 = (f32[32,4096]{1,0:T(8,128)S(1)}, f32[32,4096]{1,0:T(8,128)S(1)}, u32[]{:S(2)}, u32[]{:S(2)}) collective-permute-start(f32[32,4096]{1,0:T(8,128)S(1)} %bitcast.22), channel_id=1, source_target_pairs={{0,48},{16,0},{32,16},{48,32},{1,49},{17,1},{33,17},{49,33},{2,50}... | collective-permute-start | bytes 1572872 | tf_op jit(solution)/shard_map/ppermute | solution.py:253
  37.1 34.0 %all-to-all-start.1 = ((f32[32,32,128]{2,1,0:T(8,128)}), f32[32,32,128]{2,1,0:T(8,128)}, u32[]{:S(2)}, u32[]{:S(2)}) async-start(f32[32,32,128]{2,1,0:T(8,128)} %darcy.1), calls=%async_computation.1 | async-start | bytes 1048576 | tf_op jit(solution)/shard_map/all_to_all | solution.py:287
  45.7 26.8 %collective-permute-start.4 = (f32[32,4096]{1,0:T(8,128)S(1)}, f32[32,4096]{1,0:T(8,128)S(1)}, u32[]{:S(2)}, u32[]{:S(2)}) collective-permute-start(f32[32,4096]{1,0:T(8,128)S(1)} %bitcast.23), channel_id=1, source_target_pairs={{0,4},{4,0},{1,5},{5,1},{2,6},{6,2},{3,7},{7,3},{8,12},{12,8},{9,1... | collective-permute-start | bytes 1572872 | tf_op jit(solution)/shard_map/ppermute | solution.py:253
  45.8 22.5 %collective-permute-start.2 = (f32[16,4096]{1,0:T(8,128)S(1)}, f32[16,4096]{1,0:T(8,128)S(1)}, u32[]{:S(2)}, u32[]{:S(2)}) collective-permute-start(f32[16,4096]{1,0:T(8,128)S(1)} %slice.8), channel_id=1, source_target_pairs={{0,16},{16,32},{32,48},{48,0},{1,17},{17,33},{33,49},{49,1},{2,18}... | collective-permute-start | bytes 786440 | tf_op jit(solution)/shard_map/ppermute | solution.py:253
  49.2 19.1 %collective-permute-start.3 = (f32[16,4096]{1,0:T(8,128)S(1)}, f32[16,4096]{1,0:T(8,128)}, u32[]{:S(2)}, u32[]{:S(2)}) collective-permute-start(f32[16,4096]{1,0:T(8,128)S(1)} %slice.9), channel_id=1, source_target_pairs={{0,48},{16,0},{32,16},{48,32},{1,49},{17,1},{33,17},{49,33},{2,50}... | collective-permute-start | bytes 786440 | tf_op jit(solution)/shard_map/ppermute | solution.py:253
  51.4 21.1 %collective-permute-start.5 = (f32[32,4096]{1,0:T(8,128)S(1)}, f32[32,4096]{1,0:T(8,128)S(1)}, u32[]{:S(2)}, u32[]{:S(2)}) collective-permute-start(f32[32,4096]{1,0:T(8,128)S(1)} %collective-permute-done.refs_1_), channel_id=1, source_target_pairs={{0,4},{4,0},{1,5},{5,1},{2,6},{6,2},{3,7},{7,3},{8,12},{12,8},{9,1... | collective-permute-start | bytes 1572872 | tf_op jit(solution)/shard_map/ppermute | solution.py:253
  51.6 20.9 %collective-permute-start.6 = (f32[32,4096]{1,0:T(8,128)S(1)}, f32[32,4096]{1,0:T(8,128)S(1)}, u32[]{:S(2)}, u32[]{:S(2)}) collective-permute-start(f32[32,4096]{1,0:T(8,128)S(1)} %collective-permute-done.1.refs_2_), channel_id=1, source_target_pairs={{0,4},{4,0},{1,5},{5,1},{2,6},{6,2},{3,7},{7,3},{8,12},{12,8},{9,1... | collective-permute-start | bytes 1572872 | tf_op jit(solution)/shard_map/ppermute | solution.py:253
  68.3 4.2 %collective-permute-start.7 = (f32[16,4096]{1,0:T(8,128)S(1)}, f32[16,4096]{1,0:T(8,128)}, u32[]{:S(2)}, u32[]{:S(2)}) collective-permute-start(f32[16,4096]{1,0:T(8,128)S(1)} %collective-permute-done.2.refs_3_), channel_id=1, source_target_pairs={{0,4},{4,0},{1,5},{5,1},{2,6},{6,2},{3,7},{7,3},{8,12},{12,8},{9,1... | collective-permute-start | bytes 786440 | tf_op jit(solution)/shard_map/ppermute | solution.py:253
  68.3 4.2 %collective-permute-start.8 = (f32[16,4096]{1,0:T(8,128)}, f32[16,4096]{1,0:T(8,128)}, u32[]{:S(2)}, u32[]{:S(2)}) collective-permute-start(f32[16,4096]{1,0:T(8,128)} %collective-permute-done.3.refs_4_), channel_id=1, source_target_pairs={{0,4},{4,0},{1,5},{5,1},{2,6},{6,2},{3,7},{7,3},{8,12},{12,8},{9,1... | collective-permute-start | bytes 786440 | tf_op jit(solution)/shard_map/ppermute | solution.py:253
  68.8 0.9 copy-start.3
  75.1 4.0 %collective-permute-start.12 = (f32[32,256]{1,0:T(8,128)S(1)}, f32[32,256]{1,0:T(8,128)S(1)}, u32[]{:S(2)}, u32[]{:S(2)}) collective-permute-start(f32[32,256]{1,0:T(8,128)S(1)} %gram.1), channel_id=1, source_target_pairs={{0,8},{8,0},{1,9},{9,1},{2,10},{10,2},{3,11},{11,3},{4,12},{12,4},... | collective-permute-start | bytes 98312 | tf_op jit(solution)/shard_map/ppermute | solution.py:253

commit v5 on v4

--- a/solution.py
+++ b/solution.py
@@ -274,10 +274,15 @@
         mine = lax.dynamic_slice_in_dim(logperm, (y + shift) % slabs, 1, axis=0)
         received.append(shifted(jnp.concatenate([mine, fields], axis=0), "y", shift))
 
+    step_size = ensemble / (4.0 * (cells + 1))
+    noise_scale = math.sqrt(2.0 * step_size / ensemble)
+    at = jnp.stack([lax.axis_index("zl"), lax.axis_index("c")])
+    noise = ordered_noise(brownian, at, spots, particles, depth, noise_scale)
     blocks = [own]
     ahead, back = own, own
     for _ in range(depth // 2 - 1):
         ahead, back = shifted(ahead, "zl", 1), shifted(back, "zl", depth - 1)
+        ahead, back, noise = lax.optimization_barrier((ahead, back, noise))
         blocks += [ahead, back]
     half = own.shape[0] // 2
     blocks += [shifted(ahead[:half], "zl", 1), shifted(back[half:], "zl", depth - 1)]
@@ -286,12 +291,6 @@
     gradient = darcy(y, logperm, source, observed, received, chunk)
     g = lax.all_to_all(gradient, SPREAD_AXES + ("y",), split_axis=0, concat_axis=0, tiled=True)
     g = g.reshape(spots * particles, chunk * lanes)
-
-    step_size = ensemble / (4.0 * (cells + 1))
-    noise_scale = math.sqrt(2.0 * step_size / ensemble)
-    at = jnp.stack([lax.axis_index("zl"), lax.axis_index("c")])
-    noise = ordered_noise(brownian, at, spots, particles, depth, noise_scale)
-    g, noise = lax.optimization_barrier((g, noise))
 
     part = gram_product(blocks, g, 1024)
     part = part + shifted(part, "zh", 1)

time: 110 us -> 109 us (level)
  transfers between devices with their start and end apart: 15 -> 15, of which waited for: 5 -> 7; matrix products, arithmetic and copies ran while one was open for 3% -> 3% of each run, Pallas kernels for 7% -> 7%
where the time goes in v5:
time: 109 us; the launch traced here: 108 us
  starting transfers between devices  31.1 us (29%)
  waiting for transfers between devices  30 us (28%)
  blocking collectives  27.4 us (25%)
  Pallas kernels  12.9 us (12%)
  local copies, waits for them, and re-layouts  5.4 us (5%)
  other arithmetic  1.22 us (1%)
    ppermute x13, waiting for transfers between devices, shifted(): lax.ppermute(block, axis, [(i, (i + shift) % count) for i in range(count)])  26.4 us
    ppermute x13, starting transfers between devices, shifted(): lax.ppermute(block, axis, [(i, (i + shift) % count) for i in range(count)])  16.6 us
    all_to_all x1, blocking collectives, on_device(): lax.all_to_all(parts, ('x', 'y'), split_axis=0, concat_axis=0, tiled=True)  16.3 us
    all_to_all x1, blocking collectives, on_device(): lax.all_to_all(moved, SPREAD_AXES, split_axis=0, concat_axis=0, tiled=True)  11.1 us
    all_to_all x1, starting transfers between devices, on_device(): lax.all_to_all(gradient, SPREAD_AXES + ('y',), split_axis=0, concat_axis=...  8.68 us
    pallas_call x1, Pallas kernels, darcy(): pl.pallas_call(darcy_kernel, in_specs=[pl.BlockSpec(memory_space=pltpu.SM...  6.44 us
    all_to_all x1, starting transfers between devices, on_device(): lax.all_to_all(chunks, SPREAD_AXES, split_axis=0, concat_axis=0, tiled=True)  5.79 us
    all_to_all x1, waiting for transfers between devices, on_device(): lax.all_to_all(chunks, SPREAD_AXES, split_axis=0, concat_axis=0, tiled=True)  3.64 us
  transfers between devices with their start and end apart: 15, of which 7 were waited for; matrix products, arithmetic and copies ran while one was open for 3% of the time, Pallas kernels for 7%

profile of v5, /device:TPU:8, one launch (start us, length us, event | category | flops | bytes accessed | tf_op | source)
XLA Modules:
  0.0 108.2 jit_solution(7644749529896042244)
XLA Ops:
  0.0 1.9 %copy.14 = f32[4,8,32,128]{3,2,0,1:T(8,128)} copy(f32[4,8,32,128]{3,2,1,0:T(8,128)} %bitcast.26) | data formatting | bytes 1048576 | tf_op jit(solution)/shard_map/reshape | solution.py:266
  1.9 5.8 %all-to-all-start = ((f32[8,4,32,128]{3,2,1,0:T(8,128)}), f32[8,4,32,128]{3,2,1,0:T(8,128)S(1)}, u32[]{:S(2)}, u32[]{:S(2)}) async-start(f32[8,4,32,128]{3,2,1,0:T(8,128)} %bitcast.20), calls=%async_computation | async-start | bytes 1048576 | tf_op jit(solution)/shard_map/all_to_all | solution.py:267
  7.7 0.0 copy-done
  7.7 0.0 copy-start.1
  7.7 0.0 copy-start.2
  7.7 0.8 copy-done.1
  8.6 0.1 copy-done.2
  8.6 1.1 %pad_maximum_fusion = (f32[3,4,64,128]{3,2,1,0:T(8,128)}, f32[3,4,64,128]{3,2,1,0:T(8,128)}, f32[3,4,64,128]{3,2,1,0:T(8,128)}) fusion(f32[1,4,64,128]{3,2,1,0:T(8,128)S(1)} %bitcast.30, f32[1,4,64,128]{3,2,1,0:T(8,128)S(1)} %bitcast.29, f32[1,4,64,128]{3,2,1,0:T(8,128)S(1)} %get-tuple-element.11, f32[1,4,64,128]{3,2,1,0:T(8,128)S(1)} %get-tuple-element.12, ...), kind=kLoop, calls=%fused_computation | loop fusion | flops 589824 | bytes 1835008 | tf_op jit(solution)/shard_map/concatenate | solution.py:275
  9.8 2.3 %collective-permute-start.10 = (f32[3,4,64,128]{3,2,1,0:T(8,128)}, f32[3,4,64,128]{3,2,1,0:T(8,128)S(1)}, u32[]{:S(2)}, u32[]{:S(2)}) collective-permute-start(f32[3,4,64,128]{3,2,1,0:T(8,128)} %get-tuple-element.15), channel_id=1, source_target_pairs={{0,2},{1,3},{2,0},{3,1},{4,6},{5,7},{6,4},{7,5},{8,10},{9,11},{10,... | collective-permute-start | bytes 1179656 | tf_op jit(solution)/shard_map/ppermute | solution.py:253
  12.1 1.3 %collective-permute-start.11 = (f32[3,4,64,128]{3,2,1,0:T(8,128)}, f32[3,4,64,128]{3,2,1,0:T(8,128)S(1)}, u32[]{:S(2)}, u32[]{:S(2)}) collective-permute-start(f32[3,4,64,128]{3,2,1,0:T(8,128)} %get-tuple-element.14), channel_id=1, source_target_pairs={{0,3},{1,0},{2,1},{3,2},{4,7},{5,4},{6,5},{7,6},{8,11},{9,8},{10,9... | collective-permute-start | bytes 1179656 | tf_op jit(solution)/shard_map/ppermute | solution.py:253
  13.4 0.7 collective-permute-start.9
  14.1 3.6 %all-to-all-done = f32[8,4,32,128]{3,2,1,0:T(8,128)S(1)} async-done(((f32[8,4,32,128]{3,2,1,0:T(8,128)}), f32[8,4,32,128]{3,2,1,0:T(8,128)S(1)}, u32[]{:S(2)}, u32[]{:S(2)}) %all-to-all-start) | async-done | bytes 524320 | tf_op jit(solution)/shard_map/all_to_all | solution.py:267
  17.7 0.3 copy.13
  18.1 3.3 %collective-permute-start = (f32[32,4096]{1,0:T(8,128)S(1)}, f32[32,4096]{1,0:T(8,128)S(1)}, u32[]{:S(2)}, u32[]{:S(2)}) collective-permute-start(f32[32,4096]{1,0:T(8,128)S(1)} %bitcast.21), channel_id=1, source_target_pairs={{0,16},{16,32},{32,48},{48,0},{1,17},{17,33},{33,49},{49,1},{2,18}... | collective-permute-start | bytes 1572872 | tf_op jit(solution)/shard_map/ppermute | solution.py:253
  21.4 2.2 %collective-permute-start.1 = (f32[32,4096]{1,0:T(8,128)S(1)}, f32[32,4096]{1,0:T(8,128)S(1)}, u32[]{:S(2)}, u32[]{:S(2)}) collective-permute-start(f32[32,4096]{1,0:T(8,128)S(1)} %bitcast.22), channel_id=1, source_target_pairs={{0,48},{16,0},{32,16},{48,32},{1,49},{17,1},{33,17},{49,33},{2,50}... | collective-permute-start | bytes 1572872 | tf_op jit(solution)/shard_map/ppermute | solution.py:253
  23.6 0.0 collective-permute-done.10.r2_ref
  23.6 6.9 %collective-permute-done.11.r3_ref = f32[3,4,64,128]{3,2,1,0:T(8,128)S(1)} collective-permute-done((f32[3,4,64,128]{3,2,1,0:T(8,128)}, f32[3,4,64,128]{3,2,1,0:T(8,128)S(1)}, u32[]{:S(2)}, u32[]{:S(2)}) %collective-permute-start.11) | collective-permute-done | bytes 393248 | tf_op jit(solution)/shard_map/ppermute | solution.py:253
  30.5 0.2 collective-permute-done.9.r1_ref
  30.7 6.4 %darcy.1 = f32[32,32,128]{2,1,0:T(8,128)} custom-call(s32[1]{0:T(128)} %bitcast.4.y_ref, f32[4,4,64,128]{3,2,1,0:T(8,128)S(1)} %copy-done, f32[4,64,128]{2,1,0:T(8,128)S(1)} %copy-done.1, f32[4,64,128]{2,1,0:T(8,128)S(1)} %copy-done.2, f32[3,4,64,128]{3,2,1,0:T(8,128)S(1)} %collective-permute-done.9.r1_ref, ...), custom_call_target="tpu_custom_call" | custom-call | tf_op jit(solution)/shard_map/darcy/pallas_call | solution.py:128
  37.1 8.7 %all-to-all-start.1 = ((f32[32,32,128]{2,1,0:T(8,128)}), f32[32,32,128]{2,1,0:T(8,128)}, u32[]{:S(2)}, u32[]{:S(2)}) async-start(f32[32,32,128]{2,1,0:T(8,128)} %darcy.1), calls=%async_computation.1 | async-start | bytes 1048576 | tf_op jit(solution)/shard_map/all_to_all | solution.py:292
  45.8 0.1 pad_add_fusion.refs_0_
  45.9 0.0 copy-done.3
  45.9 1.3 %noise.1.refs_11_ = f32[32,256]{1,0:T(8,128)S(1)} custom-call(s32[2]{0:T(128)S(1)} %pad_add_fusion.refs_0_, f32[256,256]{1,0:T(8,128)S(1)} %copy-done.3), custom_call_target="tpu_custom_call" | custom-call | tf_op jit(solution)/shard_map/noise/pallas_call | solution.py:237
  47.1 0.0 collective-permute-start.4
  47.2 0.0 collective-permute-done.refs_1_
  47.2 0.0 collective-permute-done.1.refs_2_
  47.2 3.3 %collective-permute-start.2 = (f32[16,4096]{1,0:T(8,128)S(1)}, f32[16,4096]{1,0:T(8,128)S(1)}, u32[]{:S(2)}, u32[]{:S(2)}) collective-permute-start(f32[16,4096]{1,0:T(8,128)S(1)} %slice.6), channel_id=1, source_target_pairs={{0,16},{16,32},{32,48},{48,0},{1,17},{17,33},{33,49},{49,1},{2,18}... | collective-permute-start | bytes 786440 | tf_op jit(solution)/shard_map/ppermute | solution.py:253
  50.6 2.2 %collective-permute-start.3 = (f32[16,4096]{1,0:T(8,128)S(1)}, f32[16,4096]{1,0:T(8,128)}, u32[]{:S(2)}, u32[]{:S(2)}) collective-permute-start(f32[16,4096]{1,0:T(8,128)S(1)} %slice.7), channel_id=1, source_target_pairs={{0,48},{16,0},{32,16},{48,32},{1,49},{17,1},{33,17},{49,33},{2,50}... | collective-permute-start | bytes 786440 | tf_op jit(solution)/shard_map/ppermute | solution.py:253
  52.8 0.2 collective-permute-start.5
  53.0 0.3 collective-permute-start.6
  53.3 15.1 %collective-permute-done.2.refs_3_ = f32[16,4096]{1,0:T(8,128)S(1)} collective-permute-done((f32[16,4096]{1,0:T(8,128)S(1)}, f32[16,4096]{1,0:T(8,128)S(1)}, u32[]{:S(2)}, u32[]{:S(2)}) %collective-permute-start.2) | collective-permute-done | bytes 262176 | tf_op jit(solution)/shard_map/ppermute | solution.py:253
  68.4 0.0 collective-permute-start.7
  68.4 0.0 collective-permute-done.3.refs_4_
  68.4 0.5 collective-permute-start.8
  68.9 0.0 all-to-all-done.1
  68.9 1.3 %copy.12 = f32[4,8,32,128]{3,1,2,0:T(8,128)S(1)} copy(f32[4,8,32,128]{3,2,1,0:T(8,128)} %bitcast.13) | data formatting | bytes 1048576
  70.3 0.0 collective-permute-done.4.refs_5_
  70.3 0.1 collective-permute-done.7.refs_8_
  70.3 0.3 collective-permute-done.8.refs_9_
  70.6 0.0 collective-permute-done.5.refs_6_
  70.6 0.0 collective-permute-done.6.refs_7_
  70.6 2.6 %gram.1 = f32[32,256]{1,0:T(8,128)S(1)} custom-call(f32[32,4096]{1,0:T(8,128)S(1)} %bitcast.24, f32[32,4096]{1,0:T(8,128)S(1)} %collective-permute-done.refs_1_, f32[32,4096]{1,0:T(8,128)S(1)} %collective-permute-done.1.refs_2_, f32[16,4096]{1,0:T(8,128)S(1)} %collective-permute-done.2.refs_3_, f32[16,4096]{1,0:T(8,128)} %collective-permute-done.3.refs_4_, ...), custom_call_target="tpu_custom_call" | custom-call | tf_op jit(solution)/shard_map/gram/pallas_call | solution.py:167
  73.2 0.1 collective-permute-start.12
  73.4 3.9 %collective-permute-done.12 = f32[32,256]{1,0:T(8,128)S(1)} collective-permute-done((f32[32,256]{1,0:T(8,128)S(1)}, f32[32,256]{1,0:T(8,128)S(1)}, u32[]{:S(2)}, u32[]{:S(2)}) %collective-permute-start.12) | collective-permute-done | bytes 32800 | tf_op jit(solution)/shard_map/ppermute | solution.py:253
  77.3 16.3 %all_to_all.20.refs_10_ = f32[16,32,256]{2,1,0:T(8,128)S(1)} all-to-all(f32[16,32,256]{2,1,0:T(8,128)S(1)} %broadcast_in_dim.2), channel_id=1, replica_groups=mesh['x'=4,'zl'=4,'zh'=2,'c'=2,'y'=4] {'x','y'}, dimensions={0} | all-to-all | bytes 1048576 | tf_op jit(solution)/shard_map/all_to_all | solution.py:299
  93.6 2.6 %move.1 = f32[32,32,128]{2,1,0:T(8,128)S(1)} custom-call(f32[32,4096]{1,0:T(8,128)S(1)} %bitcast.25, f32[32,4096]{1,0:T(8,128)S(1)} %collective-permute-done.refs_1_, f32[32,4096]{1,0:T(8,128)S(1)} %collective-permute-done.1.refs_2_, f32[16,4096]{1,0:T(8,128)S(1)} %collective-permute-done.2.refs_3_, f32[16,4096]{1,0:T(8,128)} %collective-permute-done.3.refs_4_, ...), custom_call_target="tpu_custom_call" | custom-call | tf_op jit(solution)/shard_map/move/pallas_call | solution.py:202
  96.2 11.1 %all_to_all.21 = f32[8,4,32,128]{3,2,1,0:T(8,128)S(1)} all-to-all(f32[8,4,32,128]{3,2,1,0:T(8,128)S(1)} %bitcast.28), channel_id=1, replica_groups=mesh['x'=4,'zl'=4,'zh'=2,'c'=2,'y'=4] {'x','zh'}, dimensions={0} | all-to-all | bytes 1048576 | tf_op jit(solution)/shard_map/all_to_all | solution.py:302
  107.3 0.8 copy.6
  (7 shorter events, 0.1 us)
Async XLA Ops:
  1.9 5.8 %copy-start = (f32[4,4,64,128]{3,2,1,0:T(8,128)S(1)}, f32[4,4,64,128]{3,2,1,0:T(8,128)}, u32[]{:S(2)}) copy-start(f32[4,4,64,128]{3,2,1,0:T(8,128)} %u_ref.1) | copy-start | bytes 1572868
  1.9 15.9 %all-to-all-start = ((f32[8,4,32,128]{3,2,1,0:T(8,128)}), f32[8,4,32,128]{3,2,1,0:T(8,128)S(1)}, u32[]{:S(2)}, u32[]{:S(2)}) async-start(f32[8,4,32,128]{3,2,1,0:T(8,128)} %bitcast.20), calls=%async_computation | async-start | bytes 1048576 | tf_op jit(solution)/shard_map/all_to_all | solution.py:267
  7.7 0.9 copy-start.1
  7.7 1.0 copy-start.2
  9.8 13.8 %collective-permute-start.10 = (f32[3,4,64,128]{3,2,1,0:T(8,128)}, f32[3,4,64,128]{3,2,1,0:T(8,128)S(1)}, u32[]{:S(2)}, u32[]{:S(2)}) collective-permute-start(f32[3,4,64,128]{3,2,1,0:T(8,128)} %get-tuple-element.15), channel_id=1, source_target_pairs={{0,2},{1,3},{2,0},{3,1},{4,6},{5,7},{6,4},{7,5},{8,10},{9,11},{10,... | collective-permute-start | bytes 1179656 | tf_op jit(solution)/shard_map/ppermute | solution.py:253
  12.1 18.4 %collective-permute-start.11 = (f32[3,4,64,128]{3,2,1,0:T(8,128)}, f32[3,4,64,128]{3,2,1,0:T(8,128)S(1)}, u32[]{:S(2)}, u32[]{:S(2)}) collective-permute-start(f32[3,4,64,128]{3,2,1,0:T(8,128)} %get-tuple-element.14), channel_id=1, source_target_pairs={{0,3},{1,0},{2,1},{3,2},{4,7},{5,4},{6,5},{7,6},{8,11},{9,8},{10,9... | collective-permute-start | bytes 1179656 | tf_op jit(solution)/shard_map/ppermute | solution.py:253
  13.4 17.2 %collective-permute-start.9 = (f32[3,4,64,128]{3,2,1,0:T(8,128)}, f32[3,4,64,128]{3,2,1,0:T(8,128)S(1)}, u32[]{:S(2)}, u32[]{:S(2)}) collective-permute-start(f32[3,4,64,128]{3,2,1,0:T(8,128)} %get-tuple-element.16), channel_id=1, source_target_pairs={{0,1},{1,2},{2,3},{3,0},{4,5},{5,6},{6,7},{7,4},{8,9},{9,10},{10,1... | collective-permute-start | bytes 1179656 | tf_op jit(solution)/shard_map/ppermute | solution.py:253
  18.1 29.1 %collective-permute-start = (f32[32,4096]{1,0:T(8,128)S(1)}, f32[32,4096]{1,0:T(8,128)S(1)}, u32[]{:S(2)}, u32[]{:S(2)}) collective-permute-start(f32[32,4096]{1,0:T(8,128)S(1)} %bitcast.21), channel_id=1, source_target_pairs={{0,16},{16,32},{32,48},{48,0},{1,17},{17,33},{33,49},{49,1},{2,18}... | collective-permute-start | bytes 1572872 | tf_op jit(solution)/shard_map/ppermute | solution.py:253
  21.4 25.8 %collective-permute-start.1 = (f32[32,4096]{1,0:T(8,128)S(1)}, f32[32,4096]{1,0:T(8,128)S(1)}, u32[]{:S(2)}, u32[]{:S(2)}) collective-permute-start(f32[32,4096]{1,0:T(8,128)S(1)} %bitcast.22), channel_id=1, source_target_pairs={{0,48},{16,0},{32,16},{48,32},{1,49},{17,1},{33,17},{49,33},{2,50}... | collective-permute-start | bytes 1572872 | tf_op jit(solution)/shard_map/ppermute | solution.py:253
  37.1 8.8 %copy-start.3 = (f32[256,256]{1,0:T(8,128)S(1)}, f32[256,256]{1,0:T(8,128)}, u32[]{:S(2)}) copy-start(f32[256,256]{1,0:T(8,128)} %refs_1_.1) | copy-start | bytes 786436
  37.1 31.8 %all-to-all-start.1 = ((f32[32,32,128]{2,1,0:T(8,128)}), f32[32,32,128]{2,1,0:T(8,128)}, u32[]{:S(2)}, u32[]{:S(2)}) async-start(f32[32,32,128]{2,1,0:T(8,128)} %darcy.1), calls=%async_computation.1 | async-start | bytes 1048576 | tf_op jit(solution)/shard_map/all_to_all | solution.py:292
  47.1 23.1 %collective-permute-start.4 = (f32[32,4096]{1,0:T(8,128)S(1)}, f32[32,4096]{1,0:T(8,128)S(1)}, u32[]{:S(2)}, u32[]{:S(2)}) collective-permute-start(f32[32,4096]{1,0:T(8,128)S(1)} %bitcast.23), channel_id=1, source_target_pairs={{0,4},{4,0},{1,5},{5,1},{2,6},{6,2},{3,7},{7,3},{8,12},{12,8},{9,1... | collective-permute-start | bytes 1572872 | tf_op jit(solution)/shard_map/ppermute | solution.py:253
  47.2 21.2 %collective-permute-start.2 = (f32[16,4096]{1,0:T(8,128)S(1)}, f32[16,4096]{1,0:T(8,128)S(1)}, u32[]{:S(2)}, u32[]{:S(2)}) collective-permute-start(f32[16,4096]{1,0:T(8,128)S(1)} %slice.6), channel_id=1, source_target_pairs={{0,16},{16,32},{32,48},{48,0},{1,17},{17,33},{33,49},{49,1},{2,18}... | collective-permute-start | bytes 786440 | tf_op jit(solution)/shard_map/ppermute | solution.py:253
  50.6 17.8 %collective-permute-start.3 = (f32[16,4096]{1,0:T(8,128)S(1)}, f32[16,4096]{1,0:T(8,128)}, u32[]{:S(2)}, u32[]{:S(2)}) collective-permute-start(f32[16,4096]{1,0:T(8,128)S(1)} %slice.7), channel_id=1, source_target_pairs={{0,48},{16,0},{32,16},{48,32},{1,49},{17,1},{33,17},{49,33},{2,50}... | collective-permute-start | bytes 786440 | tf_op jit(solution)/shard_map/ppermute | solution.py:253
  52.8 17.8 %collective-permute-start.5 = (f32[32,4096]{1,0:T(8,128)S(1)}, f32[32,4096]{1,0:T(8,128)S(1)}, u32[]{:S(2)}, u32[]{:S(2)}) collective-permute-start(f32[32,4096]{1,0:T(8,128)S(1)} %collective-permute-done.refs_1_), channel_id=1, source_target_pairs={{0,4},{4,0},{1,5},{5,1},{2,6},{6,2},{3,7},{7,3},{8,12},{12,8},{9,1... | collective-permute-start | bytes 1572872 | tf_op jit(solution)/shard_map/ppermute | solution.py:253
  53.0 17.6 %collective-permute-start.6 = (f32[32,4096]{1,0:T(8,128)S(1)}, f32[32,4096]{1,0:T(8,128)S(1)}, u32[]{:S(2)}, u32[]{:S(2)}) collective-permute-start(f32[32,4096]{1,0:T(8,128)S(1)} %collective-permute-done.1.refs_2_), channel_id=1, source_target_pairs={{0,4},{4,0},{1,5},{5,1},{2,6},{6,2},{3,7},{7,3},{8,12},{12,8},{9,1... | collective-permute-start | bytes 1572872 | tf_op jit(solution)/shard_map/ppermute | solution.py:253
  68.4 2.0 %collective-permute-start.7 = (f32[16,4096]{1,0:T(8,128)S(1)}, f32[16,4096]{1,0:T(8,128)}, u32[]{:S(2)}, u32[]{:S(2)}) collective-permute-start(f32[16,4096]{1,0:T(8,128)S(1)} %collective-permute-done.2.refs_3_), channel_id=1, source_target_pairs={{0,4},{4,0},{1,5},{5,1},{2,6},{6,2},{3,7},{7,3},{8,12},{12,8},{9,1... | collective-permute-start | bytes 786440 | tf_op jit(solution)/shard_map/ppermute | solution.py:253
  68.4 2.2 %collective-permute-start.8 = (f32[16,4096]{1,0:T(8,128)}, f32[16,4096]{1,0:T(8,128)}, u32[]{:S(2)}, u32[]{:S(2)}) collective-permute-start(f32[16,4096]{1,0:T(8,128)} %collective-permute-done.3.refs_4_), channel_id=1, source_target_pairs={{0,4},{4,0},{1,5},{5,1},{2,6},{6,2},{3,7},{7,3},{8,12},{12,8},{9,1... | collective-permute-start | bytes 786440 | tf_op jit(solution)/shard_map/ppermute | solution.py:253
  73.2 4.0 %collective-permute-start.12 = (f32[32,256]{1,0:T(8,128)S(1)}, f32[32,256]{1,0:T(8,128)S(1)}, u32[]{:S(2)}, u32[]{:S(2)}) collective-permute-start(f32[32,256]{1,0:T(8,128)S(1)} %gram.1), channel_id=1, source_target_pairs={{0,8},{8,0},{1,9},{9,1},{2,10},{10,2},{3,11},{11,3},{4,12},{12,4},... | collective-permute-start | bytes 98312 | tf_op jit(solution)/shard_map/ppermute | solution.py:253

commit v6 on v5

--- a/solution.py
+++ b/solution.py
@@ -12,7 +12,7 @@
 MISFIT_WEIGHT = 1000.0
 PAD = 8
 SPREAD_AXES = ("x", "zh")
-VMEM_LIMIT = 40 << 20
+VMEM_LIMIT = 16 << 20
 
 
 def offset(order):
@@ -146,32 +146,54 @@
     return jnp.concatenate([ref[:, start : start + size] for ref in refs], axis=0)
 
 
-def gram_kernel(*refs, tile):
-    *u_refs, g_ref, o_ref = refs
-    block, cells = g_ref.shape
-    members = o_ref.shape[1]
+def products(u_refs, own_ref, g_ref, tile):
+    block, groups, lanes = g_ref.shape
+    rows = sum(ref.shape[0] for ref in u_refs)
     dims = (((1,), (1,)), ((), ()))
-    total = jnp.zeros((2 * block, members), jnp.float32)
-    for start in range(0, cells, tile):
-        u = columns(u_refs, start, tile)
-        s_high, s_low = split(u - jnp.sum(u, axis=0, keepdims=True) * (1.0 / members))
-        pair = jnp.concatenate(split(g_ref[:, start : start + tile]), axis=0)
+    total = jnp.zeros((2 * block, rows), jnp.float32)
+    for start in range(0, groups * lanes, tile):
+        own = own_ref[:, start : start + tile]
+        shift = jnp.sum(own, axis=0, keepdims=True) * (1.0 / block)
+        s_high, s_low = split(columns(u_refs, start, tile) - shift)
+        g = [g_ref[:, r, :] for r in range(start // lanes, (start + tile) // lanes)]
+        pair = jnp.concatenate(split(jnp.concatenate(g, axis=1)), axis=0)
         total = total + lax.dot_general(pair, s_high, dims, preferred_element_type=jnp.float32)
         total = total + lax.dot_general(pair, s_low, dims, preferred_element_type=jnp.float32)
-    o_ref[...] = total[:block] + total[block:]
-
-
-def gram_product(blocks, g, tile):
-    members = sum(b.shape[0] for b in blocks)
+    return total[:block] + total[block:]
+
+
+def early_kernel(*refs, tile):
+    *u_refs, g_ref, o_ref = refs
+    o_ref[...] = products(u_refs, u_refs[0], g_ref, tile)
+
+
+def late_kernel(*refs, tile):
+    *u_refs, own_ref, g_ref, early_ref, o_ref = refs
+    early = early_ref[...]
+    late = products(u_refs, own_ref, g_ref, tile)
+    sums = jnp.sum(early, axis=1, keepdims=True) + jnp.sum(late, axis=1, keepdims=True)
+    mean = sums * (1.0 / o_ref.shape[1])
+    o_ref[:, : early.shape[1]] = early - mean
+    o_ref[:, early.shape[1] :] = late - mean
+
+
+def gram_product(early, late, g, tile):
     whole = pl.BlockSpec(memory_space=pltpu.VMEM)
-    return pl.pallas_call(
-        lambda *refs: gram_kernel(*refs, tile=tile),
-        in_specs=[whole] * (len(blocks) + 1),
-        out_specs=whole,
-        out_shape=jax.ShapeDtypeStruct((g.shape[0], members), jnp.float32),
-        compiler_params=pltpu.CompilerParams(vmem_limit_bytes=VMEM_LIMIT),
-        name="gram",
-    )(*blocks, g)
+
+    def call(name, kernel, inputs, members):
+        return pl.pallas_call(
+            lambda *refs: kernel(*refs, tile=tile),
+            in_specs=[whole] * len(inputs),
+            out_specs=whole,
+            out_shape=jax.ShapeDtypeStruct((g.shape[0], members), jnp.float32),
+            compiler_params=pltpu.CompilerParams(vmem_limit_bytes=VMEM_LIMIT),
+            name=name,
+        )(*inputs)
+
+    first = sum(b.shape[0] for b in early)
+    members = first + sum(b.shape[0] for b in late)
+    part = call("gram_early", early_kernel, (*early, g), first)
+    return call("gram_late", late_kernel, (*late, early[0], g, part), members)
 
 
 def move_kernel(*refs, scale, tile):
@@ -218,9 +240,11 @@
     chosen = jnp.where(j == column, scale, 0.0)
     k = lax.broadcasted_iota(jnp.int32, (members, members), 0)
     m = lax.broadcasted_iota(jnp.int32, (members, members), 1)
-    order = (m // block) % depth
+    near = depth - 1
+    place = m // block
+    order = jnp.where(place < 2 * near, place % near, near)
     m_zl = (zl + offset(order) + depth) % depth
-    m_core = (core + m // (block * depth)) % 2
+    m_core = (core + jnp.where(place < 2 * near, place // near, place - 2 * near)) % 2
     row = member(m_zl, m_core, (m // particles) % spots, m % particles)
     chosen_row = jnp.where(k == row, 1.0, 0.0)
     picked = lax.dot_general(
@@ -282,17 +306,17 @@
     ahead, back = own, own
     for _ in range(depth // 2 - 1):
         ahead, back = shifted(ahead, "zl", 1), shifted(back, "zl", depth - 1)
-        ahead, back, noise = lax.optimization_barrier((ahead, back, noise))
         blocks += [ahead, back]
     half = own.shape[0] // 2
-    blocks += [shifted(ahead[:half], "zl", 1), shifted(back[half:], "zl", depth - 1)]
+    last = [shifted(ahead[:half], "zl", 1), shifted(back[half:], "zl", depth - 1)]
     blocks += [shifted(block, "c", 1) for block in blocks]
-
+    blocks += last + [shifted(block, "c", 1) for block in last]
+
+    received, noise = lax.optimization_barrier((received, noise))
     gradient = darcy(y, logperm, source, observed, received, chunk)
     g = lax.all_to_all(gradient, SPREAD_AXES + ("y",), split_axis=0, concat_axis=0, tiled=True)
-    g = g.reshape(spots * particles, chunk * lanes)
-
-    part = gram_product(blocks, g, 1024)
+
+    part = gram_product(blocks[:depth], blocks[depth:], g, 1024)
     part = part + shifted(part, "zh", 1)
     copies = spots * slabs // 2
     parts = jnp.broadcast_to(part[None], (copies,) + part.shape)

time: 109 us -> 108 us (level)
    pallas_call x1 -> x2, Pallas kernels: 2.6 us -> 3.35 us  [call(): pl.pallas_call(lambda *refs: kernel(*refs, tile=tile), in_specs=[whole] *...]
    unnamed x10 -> x13, local copies, waits for them, and re-layouts: 2.58 us -> 1.86 us
  transfers between devices with their start and end apart: 15 -> 15, of which waited for: 7 -> 7; matrix products, arithmetic and copies ran while one was open for 3% -> 1% of each run, Pallas kernels for 7% -> 8%
where the time goes in v6:
time: 108 us
  starting transfers between devices  31 us (29%)
  waiting for transfers between devices  29.7 us (28%)
  blocking collectives  27.4 us (25%)
  Pallas kernels  13.8 us (13%)
  local copies, waits for them, and re-layouts  4.69 us (4%)
  other arithmetic  1.23 us (1%)
    ppermute x13, waiting for transfers between devices, shifted(): lax.ppermute(block, axis, [(i, (i + shift) % count) for i in range(count)])  26.1 us
    ppermute x13, starting transfers between devices, shifted(): lax.ppermute(block, axis, [(i, (i + shift) % count) for i in range(count)])  16.7 us
    all_to_all x1, blocking collectives, on_device(): lax.all_to_all(parts, ('x', 'y'), split_axis=0, concat_axis=0, tiled=True)  16.3 us
    all_to_all x1, blocking collectives, on_device(): lax.all_to_all(moved, SPREAD_AXES, split_axis=0, concat_axis=0, tiled=True)  11.1 us
    all_to_all x1, starting transfers between devices, on_device(): lax.all_to_all(gradient, SPREAD_AXES + ('y',), split_axis=0, concat_axis=...  8.49 us
    pallas_call x1, Pallas kernels, darcy(): pl.pallas_call(darcy_kernel, in_specs=[pl.BlockSpec(memory_space=pltpu.SM...  6.44 us
    all_to_all x1, starting transfers between devices, on_device(): lax.all_to_all(chunks, SPREAD_AXES, split_axis=0, concat_axis=0, tiled=True)  5.79 us
    all_to_all x1, waiting for transfers between devices, on_device(): lax.all_to_all(chunks, SPREAD_AXES, split_axis=0, concat_axis=0, tiled=True)  3.63 us
  transfers between devices with their start and end apart: 15, of which 7 were waited for; matrix products, arithmetic and copies ran while one was open for 1% of the time, Pallas kernels for 8%

profile of v6, /device:TPU:8, one launch (start us, length us, event | category | flops | bytes accessed | tf_op | source)
XLA Modules:
  0.0 107.9 jit_solution(13649224952561373472)
XLA Ops:
  0.0 1.9 %copy.11 = f32[4,8,32,128]{3,2,0,1:T(8,128)} copy(f32[4,8,32,128]{3,2,1,0:T(8,128)} %bitcast.23) | data formatting | bytes 1048576 | tf_op jit(solution)/shard_map/reshape | solution.py:290
  1.9 5.8 %all-to-all-start = ((f32[8,4,32,128]{3,2,1,0:T(8,128)}), f32[8,4,32,128]{3,2,1,0:T(8,128)S(1)}, u32[]{:S(2)}, u32[]{:S(2)}) async-start(f32[8,4,32,128]{3,2,1,0:T(8,128)} %bitcast.16), calls=%async_computation | async-start | bytes 1048576 | tf_op jit(solution)/shard_map/all_to_all | solution.py:291
  7.7 0.0 copy-done
  7.7 0.0 copy-start.1
  7.7 0.0 copy-start.2
  7.7 0.8 copy-done.1
  8.6 0.1 copy-done.2
  8.6 1.1 %pad_maximum_fusion = (f32[3,4,64,128]{3,2,1,0:T(8,128)}, f32[3,4,64,128]{3,2,1,0:T(8,128)}, f32[3,4,64,128]{3,2,1,0:T(8,128)}) fusion(f32[1,4,64,128]{3,2,1,0:T(8,128)S(1)} %bitcast.26, f32[1,4,64,128]{3,2,1,0:T(8,128)S(1)} %bitcast.25, f32[1,4,64,128]{3,2,1,0:T(8,128)S(1)} %get-tuple-element.13, f32[1,4,64,128]{3,2,1,0:T(8,128)S(1)} %get-tuple-element.14, ...), kind=kLoop, calls=%fused_computation | loop fusion | flops 589824 | bytes 1835008 | tf_op jit(solution)/shard_map/concatenate | solution.py:299
  9.8 2.3 %collective-permute-start.10 = (f32[3,4,64,128]{3,2,1,0:T(8,128)}, f32[3,4,64,128]{3,2,1,0:T(8,128)S(1)}, u32[]{:S(2)}, u32[]{:S(2)}) collective-permute-start(f32[3,4,64,128]{3,2,1,0:T(8,128)} %get-tuple-element.17), channel_id=1, source_target_pairs={{0,2},{1,3},{2,0},{3,1},{4,6},{5,7},{6,4},{7,5},{8,10},{9,11},{10,... | collective-permute-start | bytes 1179656 | tf_op jit(solution)/shard_map/ppermute | solution.py:277
  12.1 1.3 %collective-permute-start.11 = (f32[3,4,64,128]{3,2,1,0:T(8,128)}, f32[3,4,64,128]{3,2,1,0:T(8,128)S(1)}, u32[]{:S(2)}, u32[]{:S(2)}) collective-permute-start(f32[3,4,64,128]{3,2,1,0:T(8,128)} %get-tuple-element.16), channel_id=1, source_target_pairs={{0,3},{1,0},{2,1},{3,2},{4,7},{5,4},{6,5},{7,6},{8,11},{9,8},{10,9... | collective-permute-start | bytes 1179656 | tf_op jit(solution)/shard_map/ppermute | solution.py:277
  13.4 0.7 collective-permute-start.9
  14.1 3.6 %all-to-all-done = f32[8,4,32,128]{3,2,1,0:T(8,128)S(1)} async-done(((f32[8,4,32,128]{3,2,1,0:T(8,128)}), f32[8,4,32,128]{3,2,1,0:T(8,128)S(1)}, u32[]{:S(2)}, u32[]{:S(2)}) %all-to-all-start) | async-done | bytes 524320 | tf_op jit(solution)/shard_map/all_to_all | solution.py:291
  17.7 0.3 copy.10
  18.1 3.3 %collective-permute-start = (f32[32,4096]{1,0:T(8,128)S(1)}, f32[32,4096]{1,0:T(8,128)S(1)}, u32[]{:S(2)}, u32[]{:S(2)}) collective-permute-start(f32[32,4096]{1,0:T(8,128)S(1)} %bitcast.17), channel_id=1, source_target_pairs={{0,16},{16,32},{32,48},{48,0},{1,17},{17,33},{33,49},{49,1},{2,18}... | collective-permute-start | bytes 1572872 | tf_op jit(solution)/shard_map/ppermute | solution.py:277
  21.4 2.2 %collective-permute-start.1 = (f32[32,4096]{1,0:T(8,128)S(1)}, f32[32,4096]{1,0:T(8,128)S(1)}, u32[]{:S(2)}, u32[]{:S(2)}) collective-permute-start(f32[32,4096]{1,0:T(8,128)S(1)} %bitcast.18), channel_id=1, source_target_pairs={{0,48},{16,0},{32,16},{48,32},{1,49},{17,1},{33,17},{49,33},{2,50}... | collective-permute-start | bytes 1572872 | tf_op jit(solution)/shard_map/ppermute | solution.py:277
  23.6 0.1 pad_add_fusion.refs_0_
  23.7 1.3 %noise.1.refs_11_ = f32[32,256]{1,0:T(8,128)S(1)} custom-call(s32[2]{0:T(128)S(1)} %pad_add_fusion.refs_0_, f32[256,256]{1,0:T(8,128)S(1)} %copy-done.3), custom_call_target="tpu_custom_call" | custom-call | tf_op jit(solution)/shard_map/noise/pallas_call | solution.py:261
  25.0 0.6 copy-done.4
  25.6 0.0 collective-permute-done.10.r2_ref
  25.6 4.9 %collective-permute-done.11.r3_ref = f32[3,4,64,128]{3,2,1,0:T(8,128)S(1)} collective-permute-done((f32[3,4,64,128]{3,2,1,0:T(8,128)}, f32[3,4,64,128]{3,2,1,0:T(8,128)S(1)}, u32[]{:S(2)}, u32[]{:S(2)}) %collective-permute-start.11) | collective-permute-done | bytes 393248 | tf_op jit(solution)/shard_map/ppermute | solution.py:277
  30.5 0.2 collective-permute-done.9.r1_ref
  30.7 6.4 %darcy.1 = f32[32,32,128]{2,1,0:T(8,128)} custom-call(s32[1]{0:T(128)} %bitcast.2.y_ref, f32[4,4,64,128]{3,2,1,0:T(8,128)S(1)} %copy-done, f32[4,64,128]{2,1,0:T(8,128)S(1)} %copy-done.1, f32[4,64,128]{2,1,0:T(8,128)S(1)} %copy-done.2, f32[3,4,64,128]{3,2,1,0:T(8,128)S(1)} %collective-permute-done.9.r1_ref, ...), custom_call_target="tpu_custom_call" | custom-call | tf_op jit(solution)/shard_map/darcy/pallas_call | solution.py:128
  37.1 8.5 %all-to-all-start.1 = ((f32[32,32,128]{2,1,0:T(8,128)}), f32[32,32,128]{2,1,0:T(8,128)S(1)}, u32[]{:S(2)}, u32[]{:S(2)}) async-start(f32[32,32,128]{2,1,0:T(8,128)} %darcy.1), calls=%async_computation.1 | async-start | bytes 1048576 | tf_op jit(solution)/shard_map/all_to_all | solution.py:317
  45.6 0.1 collective-permute-start.2
  45.7 0.0 collective-permute-done.refs_1_
  45.7 3.3 %collective-permute-start.5 = (f32[16,4096]{1,0:T(8,128)S(1)}, f32[16,4096]{1,0:T(8,128)S(1)}, u32[]{:S(2)}, u32[]{:S(2)}) collective-permute-start(f32[16,4096]{1,0:T(8,128)S(1)} %slice.8), channel_id=1, source_target_pairs={{0,16},{16,32},{32,48},{48,0},{1,17},{17,33},{33,49},{49,1},{2,18}... | collective-permute-start | bytes 786440 | tf_op jit(solution)/shard_map/ppermute | solution.py:277
  49.1 0.0 collective-permute-done.1.refs_2_
  49.1 2.2 %collective-permute-start.6 = (f32[16,4096]{1,0:T(8,128)S(1)}, f32[16,4096]{1,0:T(8,128)}, u32[]{:S(2)}, u32[]{:S(2)}) collective-permute-start(f32[16,4096]{1,0:T(8,128)S(1)} %slice.9), channel_id=1, source_target_pairs={{0,48},{16,0},{32,16},{48,32},{1,49},{17,1},{33,17},{49,33},{2,50}... | collective-permute-start | bytes 786440 | tf_op jit(solution)/shard_map/ppermute | solution.py:277
  51.3 0.2 collective-permute-start.3
  51.6 0.3 collective-permute-start.4
  51.9 16.4 %collective-permute-done.5.refs_2_.refs_6_ = f32[16,4096]{1,0:T(8,128)S(1)} collective-permute-done((f32[16,4096]{1,0:T(8,128)S(1)}, f32[16,4096]{1,0:T(8,128)S(1)}, u32[]{:S(2)}, u32[]{:S(2)}) %collective-permute-start.5) | collective-permute-done | bytes 262176 | tf_op jit(solution)/shard_map/ppermute | solution.py:277
  68.3 0.0 collective-permute-start.7
  68.3 0.0 collective-permute-done.6.refs_3_.refs_7_
  68.3 0.5 collective-permute-start.8
  68.8 0.0 all-to-all-done.1.refs_4_.refs_7_
  68.8 0.0 collective-permute-done.2.refs_3_
  68.8 1.0 gram_early.1.refs_8_
  69.8 0.4 collective-permute-done.7.refs_4_.refs_8_
  70.2 0.3 collective-permute-done.8.refs_5_.refs_9_
  70.5 0.0 collective-permute-done.3.refs_0_.refs_4_
  70.5 0.0 collective-permute-done.4.refs_1_.refs_5_
  70.5 2.3 %gram_late.1 = f32[32,256]{1,0:T(8,128)S(1)} custom-call(f32[32,4096]{1,0:T(8,128)S(1)} %collective-permute-done.3.refs_0_.refs_4_, f32[32,4096]{1,0:T(8,128)} %collective-permute-done.4.refs_1_.refs_5_, f32[16,4096]{1,0:T(8,128)S(1)} %collective-permute-done.5.refs_2_.refs_6_, f32[16,4096]{1,0:T(8,128)} %collective-permute-done.6.refs_3_.refs_7_, ...), custom_call_target="tpu_custom_call" | custom-call | tf_op jit(solution)/shard_map/gram_late/pallas_call | solution.py:184
  72.8 0.1 collective-permute-start.12
  73.0 3.9 %collective-permute-done.12 = f32[32,256]{1,0:T(8,128)S(1)} collective-permute-done((f32[32,256]{1,0:T(8,128)S(1)}, f32[32,256]{1,0:T(8,128)S(1)}, u32[]{:S(2)}, u32[]{:S(2)}) %collective-permute-start.12) | collective-permute-done | bytes 32800 | tf_op jit(solution)/shard_map/ppermute | solution.py:277
  76.9 16.3 %all_to_all.20.refs_10_ = f32[16,32,256]{2,1,0:T(8,128)S(1)} all-to-all(f32[16,32,256]{2,1,0:T(8,128)S(1)} %broadcast_in_dim.2), channel_id=1, replica_groups=mesh['x'=4,'zl'=4,'zh'=2,'c'=2,'y'=4] {'x','y'}, dimensions={0} | all-to-all | bytes 1048576 | tf_op jit(solution)/shard_map/all_to_all | solution.py:323
  93.2 2.8 %move.1 = f32[32,32,128]{2,1,0:T(8,128)S(1)} custom-call(f32[32,4096]{1,0:T(8,128)S(1)} %bitcast.22, f32[32,4096]{1,0:T(8,128)S(1)} %collective-permute-done.refs_1_, f32[32,4096]{1,0:T(8,128)S(1)} %collective-permute-done.1.refs_2_, f32[32,4096]{1,0:T(8,128)S(1)} %collective-permute-done.2.refs_3_, f32[32,4096]{1,0:T(8,128)S(1)} %collective-permute-done.3.refs_0_.refs_4_, ...), custom_call_target="tpu_custom_call" | custom-call | tf_op jit(solution)/shard_map/move/pallas_call | solution.py:224
  96.0 11.1 %all_to_all.21 = f32[8,4,32,128]{3,2,1,0:T(8,128)S(1)} all-to-all(f32[8,4,32,128]{3,2,1,0:T(8,128)S(1)} %bitcast.24), channel_id=1, replica_groups=mesh['x'=4,'zl'=4,'zh'=2,'c'=2,'y'=4] {'x','zh'}, dimensions={0} | all-to-all | bytes 1048576 | tf_op jit(solution)/shard_map/all_to_all | solution.py:326
  107.1 0.8 copy.6
  (11 shorter events, 0.1 us)
Async XLA Ops:
  1.9 5.8 %copy-start = (f32[4,4,64,128]{3,2,1,0:T(8,128)S(1)}, f32[4,4,64,128]{3,2,1,0:T(8,128)}, u32[]{:S(2)}) copy-start(f32[4,4,64,128]{3,2,1,0:T(8,128)} %u_ref.1) | copy-start | bytes 1572868
  1.9 15.9 %all-to-all-start = ((f32[8,4,32,128]{3,2,1,0:T(8,128)}), f32[8,4,32,128]{3,2,1,0:T(8,128)S(1)}, u32[]{:S(2)}, u32[]{:S(2)}) async-start(f32[8,4,32,128]{3,2,1,0:T(8,128)} %bitcast.16), calls=%async_computation | async-start | bytes 1048576 | tf_op jit(solution)/shard_map/all_to_all | solution.py:291
  7.7 0.9 copy-start.1
  7.7 1.0 copy-start.2
  9.8 15.8 %collective-permute-start.10 = (f32[3,4,64,128]{3,2,1,0:T(8,128)}, f32[3,4,64,128]{3,2,1,0:T(8,128)S(1)}, u32[]{:S(2)}, u32[]{:S(2)}) collective-permute-start(f32[3,4,64,128]{3,2,1,0:T(8,128)} %get-tuple-element.17), channel_id=1, source_target_pairs={{0,2},{1,3},{2,0},{3,1},{4,6},{5,7},{6,4},{7,5},{8,10},{9,11},{10,... | collective-permute-start | bytes 1179656 | tf_op jit(solution)/shard_map/ppermute | solution.py:277
  12.1 18.4 %collective-permute-start.11 = (f32[3,4,64,128]{3,2,1,0:T(8,128)}, f32[3,4,64,128]{3,2,1,0:T(8,128)S(1)}, u32[]{:S(2)}, u32[]{:S(2)}) collective-permute-start(f32[3,4,64,128]{3,2,1,0:T(8,128)} %get-tuple-element.16), channel_id=1, source_target_pairs={{0,3},{1,0},{2,1},{3,2},{4,7},{5,4},{6,5},{7,6},{8,11},{9,8},{10,9... | collective-permute-start | bytes 1179656 | tf_op jit(solution)/shard_map/ppermute | solution.py:277
  13.4 17.2 %collective-permute-start.9 = (f32[3,4,64,128]{3,2,1,0:T(8,128)}, f32[3,4,64,128]{3,2,1,0:T(8,128)S(1)}, u32[]{:S(2)}, u32[]{:S(2)}) collective-permute-start(f32[3,4,64,128]{3,2,1,0:T(8,128)} %get-tuple-element.18), channel_id=1, source_target_pairs={{0,1},{1,2},{2,3},{3,0},{4,5},{5,6},{6,7},{7,4},{8,9},{9,10},{10,1... | collective-permute-start | bytes 1179656 | tf_op jit(solution)/shard_map/ppermute | solution.py:277
  17.7 6.0 %copy-start.3 = (f32[256,256]{1,0:T(8,128)S(1)}, f32[256,256]{1,0:T(8,128)}, u32[]{:S(2)}) copy-start(f32[256,256]{1,0:T(8,128)} %refs_1_.1) | copy-start | bytes 786436
  18.1 27.6 %collective-permute-start = (f32[32,4096]{1,0:T(8,128)S(1)}, f32[32,4096]{1,0:T(8,128)S(1)}, u32[]{:S(2)}, u32[]{:S(2)}) collective-permute-start(f32[32,4096]{1,0:T(8,128)S(1)} %bitcast.17), channel_id=1, source_target_pairs={{0,16},{16,32},{32,48},{48,0},{1,17},{17,33},{33,49},{49,1},{2,18}... | collective-permute-start | bytes 1572872 | tf_op jit(solution)/shard_map/ppermute | solution.py:277
  21.4 27.7 %collective-permute-start.1 = (f32[32,4096]{1,0:T(8,128)S(1)}, f32[32,4096]{1,0:T(8,128)S(1)}, u32[]{:S(2)}, u32[]{:S(2)}) collective-permute-start(f32[32,4096]{1,0:T(8,128)S(1)} %bitcast.18), channel_id=1, source_target_pairs={{0,48},{16,0},{32,16},{48,32},{1,49},{17,1},{33,17},{49,33},{2,50}... | collective-permute-start | bytes 1572872 | tf_op jit(solution)/shard_map/ppermute | solution.py:277
  25.0 0.6 copy-start.4
  37.1 31.7 %all-to-all-start.1 = ((f32[32,32,128]{2,1,0:T(8,128)}), f32[32,32,128]{2,1,0:T(8,128)S(1)}, u32[]{:S(2)}, u32[]{:S(2)}) async-start(f32[32,32,128]{2,1,0:T(8,128)} %darcy.1), calls=%async_computation.1 | async-start | bytes 1048576 | tf_op jit(solution)/shard_map/all_to_all | solution.py:317
  45.6 23.2 %collective-permute-start.2 = (f32[32,4096]{1,0:T(8,128)S(1)}, f32[32,4096]{1,0:T(8,128)S(1)}, u32[]{:S(2)}, u32[]{:S(2)}) collective-permute-start(f32[32,4096]{1,0:T(8,128)S(1)} %bitcast.19), channel_id=1, source_target_pairs={{0,4},{4,0},{1,5},{5,1},{2,6},{6,2},{3,7},{7,3},{8,12},{12,8},{9,1... | collective-permute-start | bytes 1572872 | tf_op jit(solution)/shard_map/ppermute | solution.py:277
  45.7 22.5 %collective-permute-start.5 = (f32[16,4096]{1,0:T(8,128)S(1)}, f32[16,4096]{1,0:T(8,128)S(1)}, u32[]{:S(2)}, u32[]{:S(2)}) collective-permute-start(f32[16,4096]{1,0:T(8,128)S(1)} %slice.8), channel_id=1, source_target_pairs={{0,16},{16,32},{32,48},{48,0},{1,17},{17,33},{33,49},{49,1},{2,18}... | collective-permute-start | bytes 786440 | tf_op jit(solution)/shard_map/ppermute | solution.py:277
  49.1 19.1 %collective-permute-start.6 = (f32[16,4096]{1,0:T(8,128)S(1)}, f32[16,4096]{1,0:T(8,128)}, u32[]{:S(2)}, u32[]{:S(2)}) collective-permute-start(f32[16,4096]{1,0:T(8,128)S(1)} %slice.9), channel_id=1, source_target_pairs={{0,48},{16,0},{32,16},{48,32},{1,49},{17,1},{33,17},{49,33},{2,50}... | collective-permute-start | bytes 786440 | tf_op jit(solution)/shard_map/ppermute | solution.py:277
  51.3 19.2 %collective-permute-start.3 = (f32[32,4096]{1,0:T(8,128)S(1)}, f32[32,4096]{1,0:T(8,128)S(1)}, u32[]{:S(2)}, u32[]{:S(2)}) collective-permute-start(f32[32,4096]{1,0:T(8,128)S(1)} %collective-permute-done.refs_1_), channel_id=1, source_target_pairs={{0,4},{4,0},{1,5},{5,1},{2,6},{6,2},{3,7},{7,3},{8,12},{12,8},{9,1... | collective-permute-start | bytes 1572872 | tf_op jit(solution)/shard_map/ppermute | solution.py:277
  51.6 19.0 %collective-permute-start.4 = (f32[32,4096]{1,0:T(8,128)S(1)}, f32[32,4096]{1,0:T(8,128)}, u32[]{:S(2)}, u32[]{:S(2)}) collective-permute-start(f32[32,4096]{1,0:T(8,128)S(1)} %collective-permute-done.1.refs_2_), channel_id=1, source_target_pairs={{0,4},{4,0},{1,5},{5,1},{2,6},{6,2},{3,7},{7,3},{8,12},{12,8},{9,1... | collective-permute-start | bytes 1572872 | tf_op jit(solution)/shard_map/ppermute | solution.py:277
  68.3 2.0 %collective-permute-start.7 = (f32[16,4096]{1,0:T(8,128)S(1)}, f32[16,4096]{1,0:T(8,128)}, u32[]{:S(2)}, u32[]{:S(2)}) collective-permute-start(f32[16,4096]{1,0:T(8,128)S(1)} %collective-permute-done.5.refs_2_.refs_6_), channel_id=1, source_target_pairs={{0,4},{4,0},{1,5},{5,1},{2,6},{6,2},{3,7},{7,3},{8,12},{12,8},{9,1... | collective-permute-start | bytes 786440 | tf_op jit(solution)/shard_map/ppermute | solution.py:277
  68.3 2.2 %collective-permute-start.8 = (f32[16,4096]{1,0:T(8,128)}, f32[16,4096]{1,0:T(8,128)}, u32[]{:S(2)}, u32[]{:S(2)}) collective-permute-start(f32[16,4096]{1,0:T(8,128)} %collective-permute-done.6.refs_3_.refs_7_), channel_id=1, source_target_pairs={{0,4},{4,0},{1,5},{5,1},{2,6},{6,2},{3,7},{7,3},{8,12},{12,8},{9,1... | collective-permute-start | bytes 786440 | tf_op jit(solution)/shard_map/ppermute | solution.py:277
  72.8 4.0 %collective-permute-start.12 = (f32[32,256]{1,0:T(8,128)S(1)}, f32[32,256]{1,0:T(8,128)S(1)}, u32[]{:S(2)}, u32[]{:S(2)}) collective-permute-start(f32[32,256]{1,0:T(8,128)S(1)} %gram_late.1), channel_id=1, source_target_pairs={{0,8},{8,0},{1,9},{9,1},{2,10},{10,2},{3,11},{11,3},{4,12},{12,4},... | collective-permute-start | bytes 98312 | tf_op jit(solution)/shard_map/ppermute | solution.py:277
  76.9 16.3 %copy-start.5 = (f32[32,256]{1,0:T(8,128)S(1)}, f32[32,256]{1,0:T(8,128)}, u32[]{:S(2)}) copy-start(f32[32,256]{1,0:T(8,128)} %copy-done.4) | copy-start | bytes 98308

commit v7 on v5

--- a/solution.py
+++ b/solution.py
@@ -12,7 +12,7 @@
 MISFIT_WEIGHT = 1000.0
 PAD = 8
 SPREAD_AXES = ("x", "zh")
-VMEM_LIMIT = 40 << 20
+VMEM_LIMIT = 16 << 20
 
 
 def offset(order):
@@ -148,14 +148,17 @@
 
 def gram_kernel(*refs, tile):
     *u_refs, g_ref, o_ref = refs
-    block, cells = g_ref.shape
+    block, groups, lanes = g_ref.shape
+    cells = groups * lanes
     members = o_ref.shape[1]
     dims = (((1,), (1,)), ((), ()))
     total = jnp.zeros((2 * block, members), jnp.float32)
     for start in range(0, cells, tile):
         u = columns(u_refs, start, tile)
         s_high, s_low = split(u - jnp.sum(u, axis=0, keepdims=True) * (1.0 / members))
-        pair = jnp.concatenate(split(g_ref[:, start : start + tile]), axis=0)
+        rows = range(start // lanes, (start + tile) // lanes)
+        g = jnp.concatenate([g_ref[:, r, :] for r in rows], axis=1)
+        pair = jnp.concatenate(split(g), axis=0)
         total = total + lax.dot_general(pair, s_high, dims, preferred_element_type=jnp.float32)
         total = total + lax.dot_general(pair, s_low, dims, preferred_element_type=jnp.float32)
     o_ref[...] = total[:block] + total[block:]
@@ -282,15 +285,14 @@
     ahead, back = own, own
     for _ in range(depth // 2 - 1):
         ahead, back = shifted(ahead, "zl", 1), shifted(back, "zl", depth - 1)
-        ahead, back, noise = lax.optimization_barrier((ahead, back, noise))
         blocks += [ahead, back]
     half = own.shape[0] // 2
     blocks += [shifted(ahead[:half], "zl", 1), shifted(back[half:], "zl", depth - 1)]
     blocks += [shifted(block, "c", 1) for block in blocks]
 
+    received, noise = lax.optimization_barrier((received, noise))
     gradient = darcy(y, logperm, source, observed, received, chunk)
     g = lax.all_to_all(gradient, SPREAD_AXES + ("y",), split_axis=0, concat_axis=0, tiled=True)
-    g = g.reshape(spots * particles, chunk * lanes)
 
     part = gram_product(blocks, g, 1024)
     part = part + shifted(part, "zh", 1)

time: 109 us -> 109 us (level)
    unnamed x10 -> x13, local copies, waits for them, and re-layouts: 2.58 us -> 1.86 us
  transfers between devices with their start and end apart: 15 -> 15, of which waited for: 7 -> 7; matrix products, arithmetic and copies ran while one was open for 3% -> 1% of each run, Pallas kernels for 7% -> 7%
where the time goes in v7:
time: 109 us; the launch traced here: 108 us
  starting transfers between devices  31 us (28%)
  waiting for transfers between devices  30.7 us (28%)
  blocking collectives  27.4 us (25%)
  Pallas kernels  13.3 us (12%)
  local copies, waits for them, and re-layouts  4.69 us (4%)
  other arithmetic  1.23 us (1%)
    ppermute x13, waiting for transfers between devices, shifted(): lax.ppermute(block, axis, [(i, (i + shift) % count) for i in range(count)])  27 us
    ppermute x13, starting transfers between devices, shifted(): lax.ppermute(block, axis, [(i, (i + shift) % count) for i in range(count)])  16.7 us
    all_to_all x1, blocking collectives, on_device(): lax.all_to_all(parts, ('x', 'y'), split_axis=0, concat_axis=0, tiled=True)  16.3 us
    all_to_all x1, blocking collectives, on_device(): lax.all_to_all(moved, SPREAD_AXES, split_axis=0, concat_axis=0, tiled=True)  11.1 us
    all_to_all x1, starting transfers between devices, on_device(): lax.all_to_all(gradient, SPREAD_AXES + ('y',), split_axis=0, concat_axis=...  8.55 us
    pallas_call x1, Pallas kernels, darcy(): pl.pallas_call(darcy_kernel, in_specs=[pl.BlockSpec(memory_space=pltpu.SM...  6.44 us
    all_to_all x1, starting transfers between devices, on_device(): lax.all_to_all(chunks, SPREAD_AXES, split_axis=0, concat_axis=0, tiled=True)  5.79 us
    all_to_all x1, waiting for transfers between devices, on_device(): lax.all_to_all(chunks, SPREAD_AXES, split_axis=0, concat_axis=0, tiled=True)  3.63 us
  transfers between devices with their start and end apart: 15, of which 7 were waited for; matrix products, arithmetic and copies ran while one was open for 1% of the time, Pallas kernels for 7%

profile of v7, /device:TPU:8, one launch (start us, length us, event | category | flops | bytes accessed | tf_op | source)
XLA Modules:
  0.0 108.4 jit_solution(17402499043026841564)
XLA Ops:
  0.0 1.9 %copy.11 = f32[4,8,32,128]{3,2,0,1:T(8,128)} copy(f32[4,8,32,128]{3,2,1,0:T(8,128)} %bitcast.22) | data formatting | bytes 1048576 | tf_op jit(solution)/shard_map/reshape | solution.py:269
  1.9 5.8 %all-to-all-start = ((f32[8,4,32,128]{3,2,1,0:T(8,128)}), f32[8,4,32,128]{3,2,1,0:T(8,128)S(1)}, u32[]{:S(2)}, u32[]{:S(2)}) async-start(f32[8,4,32,128]{3,2,1,0:T(8,128)} %bitcast.16), calls=%async_computation | async-start | bytes 1048576 | tf_op jit(solution)/shard_map/all_to_all | solution.py:270
  7.7 0.0 copy-done
  7.7 0.0 copy-start.1
  7.7 0.0 copy-start.2
  7.7 0.8 copy-done.1
  8.6 0.1 copy-done.2
  8.6 1.1 %pad_maximum_fusion = (f32[3,4,64,128]{3,2,1,0:T(8,128)}, f32[3,4,64,128]{3,2,1,0:T(8,128)}, f32[3,4,64,128]{3,2,1,0:T(8,128)}) fusion(f32[1,4,64,128]{3,2,1,0:T(8,128)S(1)} %bitcast.25, f32[1,4,64,128]{3,2,1,0:T(8,128)S(1)} %bitcast.24, f32[1,4,64,128]{3,2,1,0:T(8,128)S(1)} %get-tuple-element.13, f32[1,4,64,128]{3,2,1,0:T(8,128)S(1)} %get-tuple-element.14, ...), kind=kLoop, calls=%fused_computation | loop fusion | flops 589824 | bytes 1835008 | tf_op jit(solution)/shard_map/concatenate | solution.py:278
  9.8 2.3 %collective-permute-start.10 = (f32[3,4,64,128]{3,2,1,0:T(8,128)}, f32[3,4,64,128]{3,2,1,0:T(8,128)S(1)}, u32[]{:S(2)}, u32[]{:S(2)}) collective-permute-start(f32[3,4,64,128]{3,2,1,0:T(8,128)} %get-tuple-element.17), channel_id=1, source_target_pairs={{0,2},{1,3},{2,0},{3,1},{4,6},{5,7},{6,4},{7,5},{8,10},{9,11},{10,... | collective-permute-start | bytes 1179656 | tf_op jit(solution)/shard_map/ppermute | solution.py:256
  12.1 1.3 %collective-permute-start.11 = (f32[3,4,64,128]{3,2,1,0:T(8,128)}, f32[3,4,64,128]{3,2,1,0:T(8,128)S(1)}, u32[]{:S(2)}, u32[]{:S(2)}) collective-permute-start(f32[3,4,64,128]{3,2,1,0:T(8,128)} %get-tuple-element.16), channel_id=1, source_target_pairs={{0,3},{1,0},{2,1},{3,2},{4,7},{5,4},{6,5},{7,6},{8,11},{9,8},{10,9... | collective-permute-start | bytes 1179656 | tf_op jit(solution)/shard_map/ppermute | solution.py:256
  13.4 0.7 collective-permute-start.9
  14.1 3.6 %all-to-all-done = f32[8,4,32,128]{3,2,1,0:T(8,128)S(1)} async-done(((f32[8,4,32,128]{3,2,1,0:T(8,128)}), f32[8,4,32,128]{3,2,1,0:T(8,128)S(1)}, u32[]{:S(2)}, u32[]{:S(2)}) %all-to-all-start) | async-done | bytes 524320 | tf_op jit(solution)/shard_map/all_to_all | solution.py:270
  17.7 0.3 copy.10
  18.1 3.3 %collective-permute-start = (f32[32,4096]{1,0:T(8,128)S(1)}, f32[32,4096]{1,0:T(8,128)S(1)}, u32[]{:S(2)}, u32[]{:S(2)}) collective-permute-start(f32[32,4096]{1,0:T(8,128)S(1)} %bitcast.17), channel_id=1, source_target_pairs={{0,16},{16,32},{32,48},{48,0},{1,17},{17,33},{33,49},{49,1},{2,18}... | collective-permute-start | bytes 1572872 | tf_op jit(solution)/shard_map/ppermute | solution.py:256
  21.4 2.2 %collective-permute-start.1 = (f32[32,4096]{1,0:T(8,128)S(1)}, f32[32,4096]{1,0:T(8,128)S(1)}, u32[]{:S(2)}, u32[]{:S(2)}) collective-permute-start(f32[32,4096]{1,0:T(8,128)S(1)} %bitcast.18), channel_id=1, source_target_pairs={{0,48},{16,0},{32,16},{48,32},{1,49},{17,1},{33,17},{49,33},{2,50}... | collective-permute-start | bytes 1572872 | tf_op jit(solution)/shard_map/ppermute | solution.py:256
  23.6 0.1 pad_add_fusion.refs_0_
  23.7 0.0 copy-done.3
  23.7 1.3 %noise.1.refs_11_ = f32[32,256]{1,0:T(8,128)S(1)} custom-call(s32[2]{0:T(128)S(1)} %pad_add_fusion.refs_0_, f32[256,256]{1,0:T(8,128)S(1)} %copy-done.3), custom_call_target="tpu_custom_call" | custom-call | tf_op jit(solution)/shard_map/noise/pallas_call | solution.py:240
  25.0 0.6 copy-done.4
  25.6 0.0 collective-permute-done.10.r2_ref
  25.6 4.9 %collective-permute-done.11.r3_ref = f32[3,4,64,128]{3,2,1,0:T(8,128)S(1)} collective-permute-done((f32[3,4,64,128]{3,2,1,0:T(8,128)}, f32[3,4,64,128]{3,2,1,0:T(8,128)S(1)}, u32[]{:S(2)}, u32[]{:S(2)}) %collective-permute-start.11) | collective-permute-done | bytes 393248 | tf_op jit(solution)/shard_map/ppermute | solution.py:256
  30.5 0.2 collective-permute-done.9.r1_ref
  30.7 6.4 %darcy.1 = f32[32,32,128]{2,1,0:T(8,128)} custom-call(s32[1]{0:T(128)} %bitcast.2.y_ref, f32[4,4,64,128]{3,2,1,0:T(8,128)S(1)} %copy-done, f32[4,64,128]{2,1,0:T(8,128)S(1)} %copy-done.1, f32[4,64,128]{2,1,0:T(8,128)S(1)} %copy-done.2, f32[3,4,64,128]{3,2,1,0:T(8,128)S(1)} %collective-permute-done.9.r1_ref, ...), custom_call_target="tpu_custom_call" | custom-call | tf_op jit(solution)/shard_map/darcy/pallas_call | solution.py:128
  37.1 8.5 %all-to-all-start.1 = ((f32[32,32,128]{2,1,0:T(8,128)}), f32[32,32,128]{2,1,0:T(8,128)}, u32[]{:S(2)}, u32[]{:S(2)}) async-start(f32[32,32,128]{2,1,0:T(8,128)} %darcy.1), calls=%async_computation.1 | async-start | bytes 1048576 | tf_op jit(solution)/shard_map/all_to_all | solution.py:295
  45.7 0.1 collective-permute-start.4
  45.8 0.0 collective-permute-done.refs_1_
  45.8 3.3 %collective-permute-start.2 = (f32[16,4096]{1,0:T(8,128)S(1)}, f32[16,4096]{1,0:T(8,128)S(1)}, u32[]{:S(2)}, u32[]{:S(2)}) collective-permute-start(f32[16,4096]{1,0:T(8,128)S(1)} %slice.8), channel_id=1, source_target_pairs={{0,16},{16,32},{32,48},{48,0},{1,17},{17,33},{33,49},{49,1},{2,18}... | collective-permute-start | bytes 786440 | tf_op jit(solution)/shard_map/ppermute | solution.py:256
  49.1 0.0 collective-permute-done.1.refs_2_
  49.2 2.2 %collective-permute-start.3 = (f32[16,4096]{1,0:T(8,128)S(1)}, f32[16,4096]{1,0:T(8,128)}, u32[]{:S(2)}, u32[]{:S(2)}) collective-permute-start(f32[16,4096]{1,0:T(8,128)S(1)} %slice.9), channel_id=1, source_target_pairs={{0,48},{16,0},{32,16},{48,32},{1,49},{17,1},{33,17},{49,33},{2,50}... | collective-permute-start | bytes 786440 | tf_op jit(solution)/shard_map/ppermute | solution.py:256
  51.4 0.2 collective-permute-start.5
  51.6 0.3 collective-permute-start.6
  51.9 16.3 %collective-permute-done.2.refs_3_ = f32[16,4096]{1,0:T(8,128)S(1)} collective-permute-done((f32[16,4096]{1,0:T(8,128)S(1)}, f32[16,4096]{1,0:T(8,128)S(1)}, u32[]{:S(2)}, u32[]{:S(2)}) %collective-permute-start.2) | collective-permute-done | bytes 262176 | tf_op jit(solution)/shard_map/ppermute | solution.py:256
  68.3 0.0 collective-permute-start.7
  68.3 0.0 collective-permute-done.3.refs_4_
  68.3 0.5 collective-permute-start.8
  68.8 0.0 all-to-all-done.1.refs_10_
  68.8 0.0 collective-permute-done.4.refs_5_
  68.8 1.4 %collective-permute-done.7.refs_8_ = f32[16,4096]{1,0:T(8,128)} collective-permute-done((f32[16,4096]{1,0:T(8,128)S(1)}, f32[16,4096]{1,0:T(8,128)}, u32[]{:S(2)}, u32[]{:S(2)}) %collective-permute-start.7) | collective-permute-done | bytes 262176 | tf_op jit(solution)/shard_map/ppermute | solution.py:256
  70.2 0.3 collective-permute-done.8.refs_9_
  70.5 0.0 collective-permute-done.5.refs_6_
  70.5 0.0 collective-permute-done.6.refs_7_
  70.5 2.9 %gram.1 = f32[32,256]{1,0:T(8,128)S(1)} custom-call(f32[32,4096]{1,0:T(8,128)S(1)} %bitcast.20, f32[32,4096]{1,0:T(8,128)S(1)} %collective-permute-done.refs_1_, f32[32,4096]{1,0:T(8,128)S(1)} %collective-permute-done.1.refs_2_, f32[16,4096]{1,0:T(8,128)S(1)} %collective-permute-done.2.refs_3_, f32[16,4096]{1,0:T(8,128)} %collective-permute-done.3.refs_4_, ...), custom_call_target="tpu_custom_call" | custom-call | tf_op jit(solution)/shard_map/gram/pallas_call | solution.py:170
  73.4 0.1 collective-permute-start.12
  73.5 3.9 %collective-permute-done.12 = f32[32,256]{1,0:T(8,128)S(1)} collective-permute-done((f32[32,256]{1,0:T(8,128)S(1)}, f32[32,256]{1,0:T(8,128)S(1)}, u32[]{:S(2)}, u32[]{:S(2)}) %collective-permute-start.12) | collective-permute-done | bytes 32800 | tf_op jit(solution)/shard_map/ppermute | solution.py:256
  77.5 16.3 %all_to_all.20.refs_10_ = f32[16,32,256]{2,1,0:T(8,128)S(1)} all-to-all(f32[16,32,256]{2,1,0:T(8,128)S(1)} %broadcast_in_dim.2), channel_id=1, replica_groups=mesh['x'=4,'zl'=4,'zh'=2,'c'=2,'y'=4] {'x','y'}, dimensions={0} | all-to-all | bytes 1048576 | tf_op jit(solution)/shard_map/all_to_all | solution.py:301
  93.8 2.6 %move.1 = f32[32,32,128]{2,1,0:T(8,128)S(1)} custom-call(f32[32,4096]{1,0:T(8,128)S(1)} %bitcast.21, f32[32,4096]{1,0:T(8,128)S(1)} %collective-permute-done.refs_1_, f32[32,4096]{1,0:T(8,128)S(1)} %collective-permute-done.1.refs_2_, f32[16,4096]{1,0:T(8,128)S(1)} %collective-permute-done.2.refs_3_, f32[16,4096]{1,0:T(8,128)} %collective-permute-done.3.refs_4_, ...), custom_call_target="tpu_custom_call" | custom-call | tf_op jit(solution)/shard_map/move/pallas_call | solution.py:205
  96.5 11.1 %all_to_all.21 = f32[8,4,32,128]{3,2,1,0:T(8,128)S(1)} all-to-all(f32[8,4,32,128]{3,2,1,0:T(8,128)S(1)} %bitcast.23), channel_id=1, replica_groups=mesh['x'=4,'zl'=4,'zh'=2,'c'=2,'y'=4] {'x','zh'}, dimensions={0} | all-to-all | bytes 1048576 | tf_op jit(solution)/shard_map/all_to_all | solution.py:304
  107.6 0.8 copy.6
  (10 shorter events, 0.1 us)
Async XLA Ops:
  1.9 5.8 %copy-start = (f32[4,4,64,128]{3,2,1,0:T(8,128)S(1)}, f32[4,4,64,128]{3,2,1,0:T(8,128)}, u32[]{:S(2)}) copy-start(f32[4,4,64,128]{3,2,1,0:T(8,128)} %u_ref.1) | copy-start | bytes 1572868
  1.9 15.9 %all-to-all-start = ((f32[8,4,32,128]{3,2,1,0:T(8,128)}), f32[8,4,32,128]{3,2,1,0:T(8,128)S(1)}, u32[]{:S(2)}, u32[]{:S(2)}) async-start(f32[8,4,32,128]{3,2,1,0:T(8,128)} %bitcast.16), calls=%async_computation | async-start | bytes 1048576 | tf_op jit(solution)/shard_map/all_to_all | solution.py:270
  7.7 0.9 copy-start.1
  7.7 1.0 copy-start.2
  9.8 15.8 %collective-permute-start.10 = (f32[3,4,64,128]{3,2,1,0:T(8,128)}, f32[3,4,64,128]{3,2,1,0:T(8,128)S(1)}, u32[]{:S(2)}, u32[]{:S(2)}) collective-permute-start(f32[3,4,64,128]{3,2,1,0:T(8,128)} %get-tuple-element.17), channel_id=1, source_target_pairs={{0,2},{1,3},{2,0},{3,1},{4,6},{5,7},{6,4},{7,5},{8,10},{9,11},{10,... | collective-permute-start | bytes 1179656 | tf_op jit(solution)/shard_map/ppermute | solution.py:256
  12.1 18.4 %collective-permute-start.11 = (f32[3,4,64,128]{3,2,1,0:T(8,128)}, f32[3,4,64,128]{3,2,1,0:T(8,128)S(1)}, u32[]{:S(2)}, u32[]{:S(2)}) collective-permute-start(f32[3,4,64,128]{3,2,1,0:T(8,128)} %get-tuple-element.16), channel_id=1, source_target_pairs={{0,3},{1,0},{2,1},{3,2},{4,7},{5,4},{6,5},{7,6},{8,11},{9,8},{10,9... | collective-permute-start | bytes 1179656 | tf_op jit(solution)/shard_map/ppermute | solution.py:256
  13.4 17.2 %collective-permute-start.9 = (f32[3,4,64,128]{3,2,1,0:T(8,128)}, f32[3,4,64,128]{3,2,1,0:T(8,128)S(1)}, u32[]{:S(2)}, u32[]{:S(2)}) collective-permute-start(f32[3,4,64,128]{3,2,1,0:T(8,128)} %get-tuple-element.18), channel_id=1, source_target_pairs={{0,1},{1,2},{2,3},{3,0},{4,5},{5,6},{6,7},{7,4},{8,9},{9,10},{10,1... | collective-permute-start | bytes 1179656 | tf_op jit(solution)/shard_map/ppermute | solution.py:256
  17.7 6.0 %copy-start.3 = (f32[256,256]{1,0:T(8,128)S(1)}, f32[256,256]{1,0:T(8,128)}, u32[]{:S(2)}) copy-start(f32[256,256]{1,0:T(8,128)} %refs_1_.1) | copy-start | bytes 786436
  18.1 27.7 %collective-permute-start = (f32[32,4096]{1,0:T(8,128)S(1)}, f32[32,4096]{1,0:T(8,128)S(1)}, u32[]{:S(2)}, u32[]{:S(2)}) collective-permute-start(f32[32,4096]{1,0:T(8,128)S(1)} %bitcast.17), channel_id=1, source_target_pairs={{0,16},{16,32},{32,48},{48,0},{1,17},{17,33},{33,49},{49,1},{2,18}... | collective-permute-start | bytes 1572872 | tf_op jit(solution)/shard_map/ppermute | solution.py:256
  21.4 27.7 %collective-permute-start.1 = (f32[32,4096]{1,0:T(8,128)S(1)}, f32[32,4096]{1,0:T(8,128)S(1)}, u32[]{:S(2)}, u32[]{:S(2)}) collective-permute-start(f32[32,4096]{1,0:T(8,128)S(1)} %bitcast.18), channel_id=1, source_target_pairs={{0,48},{16,0},{32,16},{48,32},{1,49},{17,1},{33,17},{49,33},{2,50}... | collective-permute-start | bytes 1572872 | tf_op jit(solution)/shard_map/ppermute | solution.py:256
  25.0 0.6 copy-start.4
  37.1 31.7 %all-to-all-start.1 = ((f32[32,32,128]{2,1,0:T(8,128)}), f32[32,32,128]{2,1,0:T(8,128)}, u32[]{:S(2)}, u32[]{:S(2)}) async-start(f32[32,32,128]{2,1,0:T(8,128)} %darcy.1), calls=%async_computation.1 | async-start | bytes 1048576 | tf_op jit(solution)/shard_map/all_to_all | solution.py:295
  45.7 23.1 %collective-permute-start.4 = (f32[32,4096]{1,0:T(8,128)S(1)}, f32[32,4096]{1,0:T(8,128)S(1)}, u32[]{:S(2)}, u32[]{:S(2)}) collective-permute-start(f32[32,4096]{1,0:T(8,128)S(1)} %bitcast.19), channel_id=1, source_target_pairs={{0,4},{4,0},{1,5},{5,1},{2,6},{6,2},{3,7},{7,3},{8,12},{12,8},{9,1... | collective-permute-start | bytes 1572872 | tf_op jit(solution)/shard_map/ppermute | solution.py:256
  45.8 22.5 %collective-permute-start.2 = (f32[16,4096]{1,0:T(8,128)S(1)}, f32[16,4096]{1,0:T(8,128)S(1)}, u32[]{:S(2)}, u32[]{:S(2)}) collective-permute-start(f32[16,4096]{1,0:T(8,128)S(1)} %slice.8), channel_id=1, source_target_pairs={{0,16},{16,32},{32,48},{48,0},{1,17},{17,33},{33,49},{49,1},{2,18}... | collective-permute-start | bytes 786440 | tf_op jit(solution)/shard_map/ppermute | solution.py:256
  49.2 19.1 %collective-permute-start.3 = (f32[16,4096]{1,0:T(8,128)S(1)}, f32[16,4096]{1,0:T(8,128)}, u32[]{:S(2)}, u32[]{:S(2)}) collective-permute-start(f32[16,4096]{1,0:T(8,128)S(1)} %slice.9), channel_id=1, source_target_pairs={{0,48},{16,0},{32,16},{48,32},{1,49},{17,1},{33,17},{49,33},{2,50}... | collective-permute-start | bytes 786440 | tf_op jit(solution)/shard_map/ppermute | solution.py:256
  51.4 19.1 %collective-permute-start.5 = (f32[32,4096]{1,0:T(8,128)S(1)}, f32[32,4096]{1,0:T(8,128)S(1)}, u32[]{:S(2)}, u32[]{:S(2)}) collective-permute-start(f32[32,4096]{1,0:T(8,128)S(1)} %collective-permute-done.refs_1_), channel_id=1, source_target_pairs={{0,4},{4,0},{1,5},{5,1},{2,6},{6,2},{3,7},{7,3},{8,12},{12,8},{9,1... | collective-permute-start | bytes 1572872 | tf_op jit(solution)/shard_map/ppermute | solution.py:256
  51.6 18.9 %collective-permute-start.6 = (f32[32,4096]{1,0:T(8,128)S(1)}, f32[32,4096]{1,0:T(8,128)S(1)}, u32[]{:S(2)}, u32[]{:S(2)}) collective-permute-start(f32[32,4096]{1,0:T(8,128)S(1)} %collective-permute-done.1.refs_2_), channel_id=1, source_target_pairs={{0,4},{4,0},{1,5},{5,1},{2,6},{6,2},{3,7},{7,3},{8,12},{12,8},{9,1... | collective-permute-start | bytes 1572872 | tf_op jit(solution)/shard_map/ppermute | solution.py:256
  68.3 2.0 %collective-permute-start.7 = (f32[16,4096]{1,0:T(8,128)S(1)}, f32[16,4096]{1,0:T(8,128)}, u32[]{:S(2)}, u32[]{:S(2)}) collective-permute-start(f32[16,4096]{1,0:T(8,128)S(1)} %collective-permute-done.2.refs_3_), channel_id=1, source_target_pairs={{0,4},{4,0},{1,5},{5,1},{2,6},{6,2},{3,7},{7,3},{8,12},{12,8},{9,1... | collective-permute-start | bytes 786440 | tf_op jit(solution)/shard_map/ppermute | solution.py:256
  68.3 2.2 %collective-permute-start.8 = (f32[16,4096]{1,0:T(8,128)}, f32[16,4096]{1,0:T(8,128)}, u32[]{:S(2)}, u32[]{:S(2)}) collective-permute-start(f32[16,4096]{1,0:T(8,128)} %collective-permute-done.3.refs_4_), channel_id=1, source_target_pairs={{0,4},{4,0},{1,5},{5,1},{2,6},{6,2},{3,7},{7,3},{8,12},{12,8},{9,1... | collective-permute-start | bytes 786440 | tf_op jit(solution)/shard_map/ppermute | solution.py:256
  73.4 4.0 %collective-permute-start.12 = (f32[32,256]{1,0:T(8,128)S(1)}, f32[32,256]{1,0:T(8,128)S(1)}, u32[]{:S(2)}, u32[]{:S(2)}) collective-permute-start(f32[32,256]{1,0:T(8,128)S(1)} %gram.1), channel_id=1, source_target_pairs={{0,8},{8,0},{1,9},{9,1},{2,10},{10,2},{3,11},{11,3},{4,12},{12,4},... | collective-permute-start | bytes 98312 | tf_op jit(solution)/shard_map/ppermute | solution.py:256
  77.5 16.3 %copy-start.5 = (f32[32,256]{1,0:T(8,128)S(1)}, f32[32,256]{1,0:T(8,128)}, u32[]{:S(2)}) copy-start(f32[32,256]{1,0:T(8,128)} %copy-done.4) | copy-start | bytes 98308
